TPU v7x, 32 devices: a whole 2x2x4 slice. The times are simulated.
32 devices in a mesh: group: 2 (over y), role: 2 (over core), dev: 8 (over z, x).
Axes of the slice: x: 2, y: 2, z: 4, core: 2. Of those that a mesh axis runs over, the one named last changes fastest.
Arguments:
- hidden: bfloat16 [64, 7168], P(('group', 'role', 'dev')), parts along dimension 0, may hold values from -6 to 6
- norm_gain: bfloat16 [7168], replicated, may hold values from 0.099609375 to 1.8984375
- routes: int32 [64, 8], P(('group', 'role', 'dev')), parts along dimension 0, may hold values from 0 to 15, all different within a row; in each aligned block of 2 rows (0 to 1, 2 to 3, ...) at most 2 rows name the same one
- gate_weights: float32 [64, 8], P(('group', 'role', 'dev')), parts along dimension 0, may hold values from 0.1 to 0.5
- w_gate: bfloat16 [7168, 32768], P(None, ('role', 'dev')), may hold values from -0.0625 to 0.0625
- w_up: bfloat16 [7168, 32768], P(None, ('role', 'dev')), may hold values from -0.0625 to 0.0625
- w_down: bfloat16 [32768, 7168], P(('role', 'dev')), may hold values from -0.125 to 0.125
- queries: bfloat16 [64, 64, 576], P(('group', 'role', 'dev')), parts along dimension 0, may hold values from -48 to 48
- local_cache: bfloat16 [64, 64, 576], P(('group', 'role', 'dev')), parts along dimension 0, may hold values from -6 to 6
- cache_lengths: int32 [64], P(('group', 'role', 'dev')), parts along dimension 0, may hold values from 2 to 64
- swap_pool: bfloat16 [512, 16, 576], P(('group', 'role', 'dev')), parts along dimension 0, may hold values from -6 to 6
- page_ids: int32 [32, 16], P(('group', 'role', 'dev')), parts along dimension 0, may hold values from 0 to 15
- page_owner: int32 [32, 16], P(('group', 'role', 'dev')), parts along dimension 0, may hold values from 0 to 1
Outputs:
- attn_out: bfloat16 [64, 64, 512], P(('group', 'role', 'dev')), parts along dimension 0
- moe_out: bfloat16 [64, 7168], P(('group', 'role', 'dev')), parts along dimension 0
There are 2 independent parts, one for each index of `group`. A program takes and returns all parts, laid end to end along the dimension named above; an argument that names none is the same for every part. Nothing has to cross between parts.
Inputs may be any that keep to these rules, and one draw needn't show every extreme that they name: `routes`: each row names 8 different experts; in the rows of one device no expert is named more than 2 times. `page_ids`: every device receives exactly one page from every holder.
All inputs are finite; a program needn't handle non-finite values.
Results may differ from a plain program's by a relative error of at most 0.0046.
Values may be sent and summed in bfloat16 or wider, within the bound.
No kernel may reach another device: no remote copies, remote signals or barrier semaphores. Data moves between devices by JAX's collectives and lax.ppermute only.
A program may use at most 128 MiB of HBM per device.

v0:
```python
import jax
import jax.numpy as jnp
from jax import lax
from jax.sharding import PartitionSpec as P

ROPE = 64
EXPERTS = 16


score_scale = 192.0 ** (-0.5)
norm_eps = 1e-06


def device_attention(queries, local_cache, cache_lengths, fetched, owners):
    local_scores = (
        jnp.einsum("rhc,rtc->rht", queries, local_cache, preferred_element_type=jnp.float32)
        * score_scale
    )
    positions = jnp.arange(local_cache.shape[1], dtype=jnp.int32)
    local_valid = positions[None, None, :] < cache_lengths[:, None, None]
    local_scores = jnp.where(local_valid, local_scores, -jnp.inf)
    page_query = queries[owners]
    page_scores = (
        jnp.einsum("phc,ptc->pht", page_query, fetched, preferred_element_type=jnp.float32)
        * score_scale
    )
    request_ids = jnp.arange(queries.shape[0], dtype=jnp.int32)
    belongs = owners[None, :] == request_ids[:, None]
    page_peak = jnp.max(page_scores, axis=2)
    owned_peak = jnp.max(jnp.where(belongs[:, :, None], page_peak[None], -jnp.inf), axis=1)
    row_peak = jnp.maximum(jnp.max(local_scores, axis=2), owned_peak)
    local_exp = jnp.exp(local_scores - row_peak[:, :, None])
    page_exp = jnp.exp(page_scores - row_peak[owners][:, :, None])
    page_total = jnp.sum(page_exp, axis=2)
    owned_total = jnp.sum(jnp.where(belongs[:, :, None], page_total[None], 0.0), axis=1)
    normalizer = jnp.sum(local_exp, axis=2) + owned_total
    local_probs = (local_exp / normalizer[:, :, None]).astype(jnp.bfloat16)
    page_probs = (page_exp / normalizer[owners][:, :, None]).astype(jnp.bfloat16)
    value_width = queries.shape[2] - ROPE
    local_part = jnp.einsum(
        "rht,rtc->rhc",
        local_probs,
        local_cache[:, :, :value_width],
        preferred_element_type=jnp.float32,
    )
    page_part = jnp.einsum(
        "pht,ptc->phc", page_probs, fetched[:, :, :value_width], preferred_element_type=jnp.float32
    )
    owned_part = jnp.einsum(
        "rp,phc->rhc", belongs.astype(jnp.float32), page_part, precision=lax.Precision.HIGHEST
    )
    return (local_part + owned_part).astype(jnp.bfloat16)


def expert_block(slot_rows, w_gate, w_up, w_down):
    flat_rows = slot_rows.reshape(-1, slot_rows.shape[-1])
    gate_proj = jnp.dot(flat_rows, w_gate, preferred_element_type=jnp.float32)
    up_proj = jnp.dot(flat_rows, w_up, preferred_element_type=jnp.float32)
    act_units = (jax.nn.silu(gate_proj) * up_proj).astype(jnp.bfloat16)
    output = jnp.dot(act_units, w_down, preferred_element_type=jnp.float32)
    return output.reshape(slot_rows.shape[:-1] + (w_down.shape[1],))


def slot_table(route_codes, expert_ids, capacity):
    is_routed = jnp.any(route_codes[:, :, None, :] == expert_ids[None, None, :, None], axis=3)
    routed_int = is_routed.astype(jnp.int32)
    before = jnp.cumsum(routed_int, axis=1) - routed_int
    slot_ids = jnp.arange(capacity, dtype=jnp.int32)
    chosen = is_routed[:, :, :, None] & (before[:, :, :, None] == slot_ids[None, None, None, :])
    return jnp.transpose(chosen, (0, 2, 3, 1)).astype(jnp.bfloat16)


def per_device(
    hidden,
    norm_gain,
    routes,
    gate_weights,
    w_gate,
    w_up,
    w_down,
    queries,
    local_cache,
    cache_lengths,
    swap_pool,
    page_ids,
    page_owner,
):
    devices = lax.axis_size(("role", "dev"))
    slices = devices // EXPERTS
    row_count = hidden.shape[0]
    width = hidden.shape[1]
    capacity = row_count // 2 + 1
    wanted = lax.all_to_all(
        page_ids.reshape(-1), ("role", "dev"), split_axis=0, concat_axis=0, tiled=True
    )
    outgoing = swap_pool[wanted]
    arrived = lax.all_to_all(outgoing, ("role", "dev"), split_axis=0, concat_axis=0, tiled=True)
    attn_out = device_attention(
        queries, local_cache, cache_lengths, arrived, page_owner.reshape(-1)
    )
    hidden_wide = hidden.astype(jnp.float32)
    inv_rms = lax.rsqrt(jnp.mean(hidden_wide * hidden_wide, axis=1, keepdims=True) + norm_eps)
    normed = (hidden_wide * inv_rms * norm_gain.astype(jnp.float32)[None, :]).astype(jnp.bfloat16)
    expert_ids = jnp.arange(EXPERTS, dtype=jnp.int32)
    own_table = slot_table(routes[None], expert_ids, capacity)[0]
    per_expert = jnp.einsum(
        "ecr,rd->ecd", own_table, normed, preferred_element_type=jnp.float32
    ).astype(jnp.bfloat16)
    spread = jnp.broadcast_to(per_expert[:, None], (EXPERTS, slices, capacity, width)).reshape(
        devices, capacity, width
    )
    partial_out = expert_block(
        lax.all_to_all(spread, ("role", "dev"), split_axis=0, concat_axis=0, tiled=True),
        w_gate,
        w_up,
        w_down,
    )
    returned = lax.all_to_all(partial_out, ("role", "dev"), split_axis=0, concat_axis=0, tiled=True)
    summed = jnp.sum(returned.reshape(EXPERTS, slices, capacity, width), axis=1)
    route_weight = jnp.sum(
        jnp.where(routes[:, :, None] == expert_ids[None, None, :], gate_weights[:, :, None], 0.0),
        axis=1,
    )
    mixing = own_table.astype(jnp.float32) * jnp.transpose(route_weight)[:, None, :]
    combined = jnp.einsum("ecr,ecd->rd", mixing, summed, precision=lax.Precision.HIGHEST)
    moe_out = (hidden_wide + combined).astype(jnp.bfloat16)
    return (attn_out, moe_out)


def solution(mesh):
    in_specs = (
        P(("group", "role", "dev"), None),
        P(),
        P(("group", "role", "dev"), None),
        P(("group", "role", "dev"), None),
        P(None, ("role", "dev")),
        P(None, ("role", "dev")),
        P(("role", "dev"), None),
        P(("group", "role", "dev"), None, None),
        P(("group", "role", "dev"), None, None),
        P(("group", "role", "dev")),
        P(("group", "role", "dev"), None, None),
        P(("group", "role", "dev"), None),
        P(("group", "role", "dev"), None),
    )
    out_specs = (P(("group", "role", "dev"), None, None), P(("group", "role", "dev"), None))
    return jax.shard_map(
        per_device, mesh=mesh, in_specs=in_specs, out_specs=out_specs, check_vma=False
    )
```

profile of v0, /device:TPU:0, one launch (start us, length us, event | category | flops | bytes accessed | tf_op | source)
XLA Modules:
  0.0 107.1 jit_solution(9635600186236785544)
XLA Ops:
  0.6 1.4 %copy.34 = s32[16,1,1]{2,1,0:T(1,128)} copy(s32[16,1,1]{0,2,1:T(1,128)} %bitcast.44) | data formatting | bytes 128 | tf_op jit(solution)/shard_map/all_to_all | solution.py:93
  2.0 7.4 %all-to-all-start = ((s32[16,1,1]{2,1,0:T(1,128)}), s32[16,1,1]{2,1,0:T(1,128)S(1)}, u32[]{:S(2)}, u32[]{:S(2)}) async-start(s32[16,1,1]{2,1,0:T(1,128)} %copy.34), calls=%async_computation | async-start | bytes 16384 | tf_op jit(solution)/shard_map/all_to_all | solution.py:93
  9.4 0.7 fusion.38
  10.1 0.8 fusion.29
  10.9 0.7 convert_element_type.61
  11.6 0.9 fusion.22
  12.5 1.1 %convolution_convert_fusion = bf16[16,2,7168]{2,0,1:T(8,128)(2,1)S(1)} fusion(bf16[2,7168]{1,0:T(2,128)(2,1)} %param.13, f32[2]{0:T(128)S(1)} %add_rsqrt_fusion, f32[7168]{0:T(1024)S(1)} %convert_element_type.61, pred[2,16]{1,0:T(4,128)(4,1)S(1)} %fusion.29, s32[2,16]{1,0:T(2,128)S(1)} %convert_subtract_fusion), kind=kOutput, calls=%fused_computation.4 | convolution fusion | flops 1204352 | bytes 516264 | tf_op jit(solution)/shard_map/ecr,rd->ecd/dot_general | solution.py:106
  13.7 1.2 %copy.38 = bf16[16,2,7168]{2,1,0:T(2,128)(2,1)} copy(bf16[16,2,7168]{2,0,1:T(8,128)(2,1)S(1)} %convolution_convert_fusion) | data formatting | bytes 917504 | tf_op jit(solution)/shard_map/convert_element_type | solution.py:108
  14.9 1.7 %gather_fusion = bf16[16,64,576]{2,1,0:T(8,128)(2,1)S(1)} fusion(bf16[2,64,576]{2,1,0:T(8,128)(2,1)} %param.20, s32[1024]{0:T(1024)S(1)} %pad_clamp_fusion.1), kind=kCustom, calls=%fused_computation | custom fusion | bytes 2359360 | tf_op jit(solution)/shard_map/gather | solution.py:22
  16.6 6.0 %all-to-all-start.2 = ((bf16[16,2,7168]{2,1,0:T(2,128)(2,1)}), bf16[16,2,7168]{2,1,0:T(2,128)(2,1)S(1)}, u32[]{:S(2)}, u32[]{:S(2)}) async-start(bf16[16,2,7168]{2,1,0:T(2,128)(2,1)} %copy.38), calls=%async_computation.2 | async-start | bytes 917504 | tf_op jit(solution)/shard_map/all_to_all | solution.py:113
  22.7 0.8 select_reduce_fusion.2
  23.4 0.7 iota_compare_fusion.3
  24.2 1.2 %fusion.41 = (f32[2,64]{1,0:T(2,128)S(1)}, f32[2,64,64]{1,2,0:T(8,128)S(1)}) fusion(bf16[2,64,576]{2,1,0:T(8,128)(2,1)} %param.20, bf16[2,64,576]{2,1,0:T(8,128)(2,1)} %param.21, pred[2,64]{1,0:T(4,128)(4,1)S(1)} %iota_compare_fusion.3), kind=kOutput, calls=%fused_computation.71 | convolution fusion | flops 9461632 | bytes 328320 | tf_op jit(solution)/shard_map/rhc,rtc->rht/dot_general | solution.py:16
  25.4 0.4 reduce.1
  25.8 1.3 %gather_fusion.1 = bf16[16,16,576]{2,1,0:T(8,128)(2,1)} fusion(bf16[16,16,576]{2,1,0:T(8,128)(2,1)S(1)} %copy-done, s32[1024]{0:T(1024)S(1)} %pad_clamp_fusion), kind=kCustom, calls=%fused_computation.1 | custom fusion | bytes 589888 | tf_op jit(solution)/shard_map/gather | solution.py:96
  27.1 10.0 %all-to-all-done.2 = bf16[16,2,7168]{2,1,0:T(2,128)(2,1)S(1)} async-done(((bf16[16,2,7168]{2,1,0:T(2,128)(2,1)}), bf16[16,2,7168]{2,1,0:T(2,128)(2,1)S(1)}, u32[]{:S(2)}, u32[]{:S(2)}) %all-to-all-start.2) | async-done | bytes 458784 | tf_op jit(solution)/shard_map/all_to_all | solution.py:113
  37.1 3.5 %all-to-all-start.1 = ((bf16[16,16,576]{2,1,0:T(8,128)(2,1)}), bf16[16,16,576]{2,1,0:T(8,128)(2,1)S(1)}, u32[]{:S(2)}, u32[]{:S(2)}) async-start(bf16[16,16,576]{2,1,0:T(8,128)(2,1)} %gather_fusion.1), calls=%async_computation.1 | async-start | bytes 655360 | tf_op jit(solution)/shard_map/all_to_all | solution.py:97
  40.6 0.2 reshape.196
  40.8 12.7 %fusion.43 = f32[32,2048]{1,0:T(8,128)} fusion(bf16[32,7168]{1,0:T(8,128)(2,1)S(1)} %reshape.196, bf16[7168,2048]{1,0:T(8,128)(2,1)} %param.17), kind=kOutput, calls=%fused_computation.73 | convolution fusion | flops 939524096 | bytes 30081024 | tf_op jit(solution)/shard_map/dot_general | solution.py:57
  53.5 20.8 %fusion.3 = f32[32,7168]{1,0:T(8,128)S(1)} fusion(bf16[2048,7168]{1,0:T(8,128)(2,1)} %param.19, bf16[32,7168]{1,0:T(8,128)(2,1)S(1)} %reshape.196, bf16[7168,2048]{1,0:T(8,128)(2,1)} %param.18, f32[32,2048]{1,0:T(8,128)} %fusion.43), kind=kOutput, calls=%fused_computation.10 | convolution fusion | flops 1879441408 | bytes 60358656 | tf_op jit(solution)/shard_map/dot_general | solution.py:60
  74.3 1.5 %reshape.197 = f32[16,2,7168]{2,1,0:T(2,128)} reshape(f32[32,7168]{1,0:T(8,128)S(1)} %fusion.3) | data formatting | bytes 1835008 | tf_op jit(solution)/shard_map/reshape | solution.py:61
  75.8 5.9 %all-to-all-start.3 = ((f32[16,2,7168]{2,1,0:T(2,128)}), f32[16,2,7168]{2,1,0:T(2,128)S(1)}, u32[]{:S(2)}, u32[]{:S(2)}) async-start(f32[16,2,7168]{2,1,0:T(2,128)} %reshape.197), calls=%async_computation.3 | async-start | bytes 1835008 | tf_op jit(solution)/shard_map/all_to_all | solution.py:118
  81.8 0.5 fusion.42
  82.3 0.1 select_reduce_fusion.1
  82.4 0.6 gather_fusion.2
  83.0 0.1 select_reduce_fusion
  83.1 0.6 gather_fusion.3
  83.7 0.5 fusion.9
  84.2 2.0 %fusion.4 = f32[2,64,512]{2,0,1:T(2,128)S(1)} fusion(f32[16,64,512]{2,1,0:T(8,128)S(1)} %fusion.9, s32[16]{0:T(128)S(1)} %bitcast.43), kind=kOutput, calls=%fused_computation.11 | convolution fusion | flops 12582944 | bytes 2359360 | tf_op jit(solution)/shard_map/rp,phc->rhc/dot_general | solution.py:49
  86.2 1.8 %fusion.6 = bf16[2,64,512]{2,1,0:T(8,128)(2,1)} fusion(f32[2,64,512]{2,0,1:T(2,128)S(1)} %fusion.4, bf16[2,64,576]{2,1,0:T(8,128)(2,1)} %param.21, f32[2,64,64]{1,2,0:T(8,128)S(1)} %get-tuple-element.3, f32[2,64]{1,0:T(2,128)S(1)} %add.49, f32[2,64]{1,0:T(2,128)S(1)} %max.7), kind=kOutput, calls=%fused_computation.14 | convolution fusion | flops 8544256 | bytes 558080 | tf_op jit(solution)/shard_map/rht,rtc->rhc/dot_general | solution.py:40
  88.0 17.6 %all-to-all-done.3 = f32[16,2,7168]{2,1,0:T(2,128)S(1)} async-done(((f32[16,2,7168]{2,1,0:T(2,128)}), f32[16,2,7168]{2,1,0:T(2,128)S(1)}, u32[]{:S(2)}, u32[]{:S(2)}) %all-to-all-start.3) | async-done | bytes 917536 | tf_op jit(solution)/shard_map/all_to_all | solution.py:118
  105.6 1.4 %fusion.1 = bf16[2,7168]{1,0:T(2,128)(2,1)} fusion(f32[16,2,7168]{2,1,0:T(2,128)S(1)} %all-to-all-done.3, bf16[2,7168]{1,0:T(2,128)(2,1)S(1)} %copy-done.1, pred[2,16]{1,0:T(4,128)(4,1)S(1)} %fusion.29, f32[16,2]{0,1:T(2,128)S(1)} %bitcast.41, s32[2,16]{1,0:T(2,128)S(1)} %convert_subtract_fusion), kind=kOutput, calls=%fused_computation.7 | convolution fusion | flops 5548352 | bytes 975136 | tf_op jit(solution)/shard_map/ecr,ecd->rd/dot_general | solution.py:125
  (20 shorter events, 0.2 us)
Async XLA Ops:
  0.6 25.1 %copy-start = (bf16[16,16,576]{2,1,0:T(8,128)(2,1)S(1)}, bf16[16,16,576]{2,1,0:T(8,128)(2,1)}, u32[]{:S(2)}) copy-start(bf16[16,16,576]{2,1,0:T(8,128)(2,1)} %param.23) | copy-start | bytes 884740
  2.0 14.6 %all-to-all-start = ((s32[16,1,1]{2,1,0:T(1,128)}), s32[16,1,1]{2,1,0:T(1,128)S(1)}, u32[]{:S(2)}, u32[]{:S(2)}) async-start(s32[16,1,1]{2,1,0:T(1,128)} %copy.34), calls=%async_computation | async-start | bytes 16384 | tf_op jit(solution)/shard_map/all_to_all | solution.py:93
  16.6 20.4 %all-to-all-start.2 = ((bf16[16,2,7168]{2,1,0:T(2,128)(2,1)}), bf16[16,2,7168]{2,1,0:T(2,128)(2,1)S(1)}, u32[]{:S(2)}, u32[]{:S(2)}) async-start(bf16[16,2,7168]{2,1,0:T(2,128)(2,1)} %copy.38), calls=%async_computation.2 | async-start | bytes 917504 | tf_op jit(solution)/shard_map/all_to_all | solution.py:113
  37.1 38.7 %all-to-all-start.1 = ((bf16[16,16,576]{2,1,0:T(8,128)(2,1)}), bf16[16,16,576]{2,1,0:T(8,128)(2,1)S(1)}, u32[]{:S(2)}, u32[]{:S(2)}) async-start(bf16[16,16,576]{2,1,0:T(8,128)(2,1)} %gather_fusion.1), calls=%async_computation.1 | async-start | bytes 655360 | tf_op jit(solution)/shard_map/all_to_all | solution.py:97
  53.5 28.2 %copy-start.2 = (s32[1,16]{1,0:T(1,128)S(1)}, s32[1,16]{1,0:T(1,128)}, u32[]{:S(2)}) copy-start(s32[1,16]{1,0:T(1,128)} %param.25) | copy-start | bytes 196
  53.5 52.1 %copy-start.1 = (bf16[2,7168]{1,0:T(2,128)(2,1)S(1)}, bf16[2,7168]{1,0:T(2,128)(2,1)}, u32[]{:S(2)}) copy-start(bf16[2,7168]{1,0:T(2,128)(2,1)} %param.13) | copy-start | bytes 86020
  75.8 29.8 %all-to-all-start.3 = ((f32[16,2,7168]{2,1,0:T(2,128)}), f32[16,2,7168]{2,1,0:T(2,128)S(1)}, u32[]{:S(2)}, u32[]{:S(2)}) async-start(f32[16,2,7168]{2,1,0:T(2,128)} %reshape.197), calls=%async_computation.3 | async-start | bytes 1835008 | tf_op jit(solution)/shard_map/all_to_all | solution.py:118
where the time goes:
time: 108 us; the launch traced here: 107 us
  matrix products  42 us (39%)
  waiting for transfers between devices  27.6 us (26%)
  starting transfers between devices  22.9 us (21%)
  local copies, waits for them, and re-layouts  8.41 us (8%)
  other arithmetic  5.31 us (5%)
    dot_general x1, matrix products, expert_block(): output = jnp.dot(act_units, w_down, preferred_element_type=jnp.float32)  20.8 us
    all_to_all x1, waiting for transfers between devices, per_device(): lax.all_to_all(partial_out, ('role', 'dev'), split_axis=0, concat_axis=0,...  17.6 us
    dot_general x1, matrix products, expert_block(): gate_proj = jnp.dot(flat_rows, w_gate, preferred_element_type=jnp.float32)  12.7 us
    all_to_all x1, waiting for transfers between devices, per_device(): lax.all_to_all(spread, ('role', 'dev'), split_axis=0, concat_axis=0, tile...  9.98 us
    all_to_all x1, starting transfers between devices, per_device(): lax.all_to_all(page_ids.reshape(-1), ('role', 'dev'), split_axis=0, conca...  7.39 us
    all_to_all x1, starting transfers between devices, per_device(): lax.all_to_all(spread, ('role', 'dev'), split_axis=0, concat_axis=0, tile...  6.02 us
    all_to_all x1, starting transfers between devices, per_device(): lax.all_to_all(partial_out, ('role', 'dev'), split_axis=0, concat_axis=0,...  5.92 us
    all_to_all x1, starting transfers between devices, per_device(): lax.all_to_all(outgoing, ('role', 'dev'), split_axis=0, concat_axis=0, ti...  3.54 us
  transfers between devices with their start and end apart: 4, of which 2 were waited for; matrix products, arithmetic and copies ran while one was open for 49% of the time, Pallas kernels for 0%

commit v1 on v0

v1 whole, which is shorter than its diff:
```python
import functools

import jax
import jax.numpy as jnp
from jax import lax
from jax.experimental import pallas as pl
from jax.experimental.pallas import tpu as pltpu
from jax.sharding import PartitionSpec as P

ROPE = 64
EXPERTS = 16
LANES = 128

score_scale = 192.0 ** (-0.5)
norm_eps = 1e-06


VM = pl.BlockSpec(memory_space=pltpu.VMEM)
SM = pl.BlockSpec(memory_space=pltpu.SMEM)
ANY = pl.BlockSpec(memory_space=pl.ANY)


def exchange_rounds(role_size, dev_size):
    rounds = []
    bit = dev_size // 2
    while bit:
        rounds.append(("dev", bit, dev_size))
        bit //= 2
    bit = role_size // 2
    while bit:
        rounds.append(("role", bit, role_size))
        bit //= 2
    return rounds


def swap(x, rnd):
    axis, bit, size = rnd
    return lax.ppermute(x, axis, [(i, i ^ bit) for i in range(size)])


def pack_kernel(hid_ref, gain_ref, routes_ref, weights_ref, ids_ref, out_ref):
    width = hid_ref.shape[1]
    rows = hid_ref.shape[0]
    extra = out_ref.shape[1] - width
    x = hid_ref[...].astype(jnp.float32)
    inv = lax.rsqrt(jnp.mean(x * x, axis=1, keepdims=True) + norm_eps)
    out_ref[:, :width] = (x * inv * gain_ref[...].astype(jnp.float32)).astype(jnp.bfloat16)
    lane = lax.broadcasted_iota(jnp.int32, (rows, LANES), 1)
    expert = lax.rem(lane, EXPERTS)
    routes = routes_ref[...]
    weights = weights_ref[...]
    weight = jnp.zeros((rows, LANES), jnp.float32)
    for k in range(routes.shape[1]):
        weight = weight + jnp.where(routes[:, k : k + 1] == expert, weights[:, k : k + 1], 0.0)
    high = weight.astype(jnp.bfloat16).astype(jnp.float32)
    tail = jnp.where(lane < EXPERTS, high, jnp.where(lane < 2 * EXPERTS, weight - high, 0.0))
    out_ref[:, width : width + LANES] = tail.astype(jnp.bfloat16)
    ids = ids_ref[...].astype(jnp.float32)
    out_ref[:, width + LANES :] = jnp.broadcast_to(ids, (rows, extra - LANES)).astype(jnp.bfloat16)


def pick_kernel(me_ref, ids_ref, pool_ref, out_ref, sems, *, rounds, role_size, dev_size):
    me = me_ref[0]
    count = out_ref.shape[0]

    def copy(d):
        away = d ^ me
        slot = jnp.int32(0)
        for i, (axis, bit, _) in enumerate(rounds):
            flat = bit if axis == "dev" else bit * dev_size
            slot = slot + jnp.where((away & flat) != 0, jnp.int32(1 << i), jnp.int32(0))
        page = ids_ref[slot, me]
        return pltpu.make_async_copy(pool_ref.at[page], out_ref.at[d], sems.at[d])

    def start(d, c):
        copy(d).start()
        return c

    def wait(d, c):
        pltpu.make_async_copy(pool_ref.at[0], out_ref.at[d], sems.at[d]).wait()
        return c

    lax.fori_loop(0, count, start, 0)
    lax.fori_loop(0, count, wait, 0)


def expert_kernel(
    expert_ref, xa_ref, xb_ref, g_ref, u_ref, d_ref, keep_ref, send_ref,
    gb, ub, db, ga, ua, h, wsel, sem, semd, *, tk, tn, nb, nd,
):
    k_size, f_size = g_ref.shape
    n1, n2 = k_size // tk, k_size // tn
    half = xa_ref.shape[0]

    def cg(i):
        s = lax.rem(i, nb)
        return pltpu.make_async_copy(g_ref.at[pl.ds(i * tk, tk)], gb.at[s], sem.at[0, s])

    def cu(i):
        s = lax.rem(i, nb)
        return pltpu.make_async_copy(u_ref.at[pl.ds(i * tk, tk)], ub.at[s], sem.at[1, s])

    def cd(j):
        s = lax.rem(j, nd)
        cols = pl.ds(pl.multiple_of(j * tn, tn), tn)
        return pltpu.make_async_copy(d_ref.at[:, cols], db.at[s], semd.at[s])

    for i in range(nb):
        cg(i).start()
        cu(i).start()
    ga[...] = jnp.zeros_like(ga)
    ua[...] = jnp.zeros_like(ua)
    lane = lax.broadcasted_iota(jnp.int32, (half, LANES), 1)
    chosen = (lane == expert_ref[0]) | (lane == expert_ref[0] + EXPERTS)
    for i, ref in enumerate((xa_ref, xb_ref)):
        tail = ref[:, k_size : k_size + LANES].astype(jnp.float32)
        wsel[i * half : (i + 1) * half] = jnp.sum(jnp.where(chosen, tail, 0.0), axis=1, keepdims=True)

    def first(i, c):
        s = lax.rem(i, nb)
        cg(i).wait()
        cu(i).wait()
        cols = pl.ds(pl.multiple_of(i * tk, tk), tk)
        xs = jnp.concatenate([xa_ref[:, cols], xb_ref[:, cols]], axis=0)
        ga[...] += jnp.dot(xs, gb[s], preferred_element_type=jnp.float32)
        ua[...] += jnp.dot(xs, ub[s], preferred_element_type=jnp.float32)

        @pl.when(i + nb < n1)
        def _():
            cg(i + nb).start()
            cu(i + nb).start()

        @pl.when(i + nd >= n1)
        def _():
            cd(i + nd - n1).start()

        return c

    lax.fori_loop(0, n1, first, 0)
    g = ga[...]
    h[...] = ((g / (1.0 + jnp.exp(-g))) * ua[...]).astype(jnp.bfloat16)

    def second(j, c):
        s = lax.rem(j, nd)
        cd(j).wait()
        cols = pl.ds(pl.multiple_of(j * tn, tn), tn)
        out = jnp.dot(h[...], db[s], preferred_element_type=jnp.float32)
        out = out * wsel[...]
        keep_ref[:, cols] = out[:half]
        send_ref[:, cols] = out[half:].astype(jnp.bfloat16)

        @pl.when(j + nd < n2)
        def _():
            cd(j + nd).start()

        return c

    lax.fori_loop(0, n2, second, 0)


def attention_kernel(len_ref, owner_ref, q_ref, local_ref, page_ref, out_ref):
    requests, heads, width = q_ref.shape
    value = out_ref.shape[2]
    local_len = local_ref.shape[1]
    pages, page_len, _ = page_ref.shape
    paged = page_ref[...].reshape(pages * page_len, width)
    row = lax.broadcasted_iota(jnp.int32, (pages, pages * page_len), 0)
    col = lax.broadcasted_iota(jnp.int32, (pages, pages * page_len), 1)
    inside = (col >= row * page_len) & (col < (row + 1) * page_len)
    owner = jnp.broadcast_to(jnp.transpose(owner_ref[...].astype(jnp.float32)), inside.shape)
    key_owner = jnp.sum(jnp.where(inside, owner, 0.0), axis=0, keepdims=True)
    nt = (((1,), (1,)), ((), ()))
    for r in range(requests):
        q = q_ref[r]
        local = local_ref[r]
        s_local = lax.dot_general(q, local, nt, preferred_element_type=jnp.float32) * score_scale
        pos = lax.broadcasted_iota(jnp.int32, (heads, local_len), 1)
        s_local = jnp.where(pos < len_ref[r], s_local, -jnp.inf)
        s_page = lax.dot_general(q, paged, nt, preferred_element_type=jnp.float32) * score_scale
        s_page = jnp.where(key_owner == float(r), s_page, -jnp.inf)
        peak = jnp.maximum(jnp.max(s_local, axis=1, keepdims=True), jnp.max(s_page, axis=1, keepdims=True))
        e_local = jnp.exp(s_local - peak)
        e_page = jnp.exp(s_page - peak)
        total = jnp.sum(e_local, axis=1, keepdims=True) + jnp.sum(e_page, axis=1, keepdims=True)
        p_local = (e_local / total).astype(jnp.bfloat16)
        p_page = (e_page / total).astype(jnp.bfloat16)
        out = jnp.dot(p_local, local[:, :value], preferred_element_type=jnp.float32)
        out = out + jnp.dot(p_page, paged[:, :value], preferred_element_type=jnp.float32)
        out_ref[r] = out.astype(jnp.bfloat16)


def tile_of(size, want):
    tile = min(size, want)
    while size % tile:
        tile -= LANES
    return tile


def per_device(
    hidden, norm_gain, routes, gate_weights, w_gate, w_up, w_down,
    queries, local_cache, cache_lengths, swap_pool, page_ids, page_owner,
):
    role_size, dev_size = lax.axis_size("role"), lax.axis_size("dev")
    devices = role_size * dev_size
    slices = devices // EXPERTS
    rounds = exchange_rounds(role_size, dev_size)
    me = lax.axis_index("role") * dev_size + lax.axis_index("dev")
    me_arr = jnp.reshape(me, (1,)).astype(jnp.int32)
    expert_arr = jnp.reshape(me // slices, (1,)).astype(jnp.int32)
    rows, width = hidden.shape
    units = w_gate.shape[1]
    id_cols = pl.cdiv(devices, LANES) * LANES
    packed_width = width + LANES + id_cols
    ids_padded = jnp.pad(page_ids, ((0, 0), (0, id_cols - devices)))
    packed = pl.pallas_call(
        pack_kernel,
        out_shape=jax.ShapeDtypeStruct((rows, packed_width), jnp.bfloat16),
        in_specs=[VM] * 5,
        out_specs=VM,
        compiler_params=pltpu.CompilerParams(vmem_limit_bytes=4 << 20),
    )(hidden, norm_gain.reshape(1, width), routes, gate_weights, ids_padded)

    held = packed[None]
    for rnd in rounds[:-1]:
        held = jnp.concatenate([held, swap(held, rnd)], axis=0)
    held = held.reshape(-1, packed_width)
    other = swap(held, rounds[-1])
    half = held.shape[0]

    ids = jnp.concatenate(
        [held[::rows, width + LANES : width + LANES + devices], other[::rows, width + LANES : width + LANES + devices]],
        axis=0,
    ).astype(jnp.int32)
    outgoing = pl.pallas_call(
        functools.partial(pick_kernel, rounds=rounds, role_size=role_size, dev_size=dev_size),
        out_shape=jax.ShapeDtypeStruct((devices,) + swap_pool.shape[1:], jnp.bfloat16),
        in_specs=[SM, SM, ANY],
        out_specs=VM,
        scratch_shapes=[pltpu.SemaphoreType.DMA((devices,))],
        compiler_params=pltpu.CompilerParams(vmem_limit_bytes=12 << 20),
    )(me_arr, ids, swap_pool)
    arrived = lax.all_to_all(outgoing, ("role", "dev"), split_axis=0, concat_axis=0, tiled=True)

    tk, tn = tile_of(width, 512), tile_of(width, 512)
    nb = nd = 4
    keep, send = pl.pallas_call(
        functools.partial(expert_kernel, tk=tk, tn=tn, nb=nb, nd=nd),
        out_shape=(
            jax.ShapeDtypeStruct((half, width), jnp.float32),
            jax.ShapeDtypeStruct((half, width), jnp.bfloat16),
        ),
        in_specs=[SM, VM, VM, ANY, ANY, ANY],
        out_specs=(VM, VM),
        scratch_shapes=[
            pltpu.VMEM((nb, tk, units), jnp.bfloat16),
            pltpu.VMEM((nb, tk, units), jnp.bfloat16),
            pltpu.VMEM((nd, units, tn), jnp.bfloat16),
            pltpu.VMEM((2 * half, units), jnp.float32),
            pltpu.VMEM((2 * half, units), jnp.float32),
            pltpu.VMEM((2 * half, units), jnp.bfloat16),
            pltpu.VMEM((2 * half, 1), jnp.float32),
            pltpu.SemaphoreType.DMA((2, nb)),
            pltpu.SemaphoreType.DMA((nd,)),
        ],
        compiler_params=pltpu.CompilerParams(vmem_limit_bytes=56 << 20),
        cost_estimate=pl.CostEstimate(
            flops=6 * 2 * half * width * units, bytes_accessed=6 * width * units, transcendentals=0
        ),
    )(expert_arr, held, other, w_gate, w_up, w_down)

    attn_out = pl.pallas_call(
        attention_kernel,
        out_shape=jax.ShapeDtypeStruct(queries.shape[:2] + (queries.shape[2] - ROPE,), jnp.bfloat16),
        in_specs=[SM, VM, VM, VM, VM],
        out_specs=VM,
        compiler_params=pltpu.CompilerParams(vmem_limit_bytes=24 << 20),
        cost_estimate=pl.CostEstimate(flops=1 << 27, bytes_accessed=1 << 20, transcendentals=1 << 16),
    )(cache_lengths, page_owner, queries, local_cache, arrived)

    total = keep + swap(send, rounds[-1]).astype(jnp.float32)
    for rnd in rounds[-2::-1]:
        total = total.reshape(2, -1, rows, width)
        got = swap(total[1].astype(jnp.bfloat16), rnd)
        total = total[0] + got.astype(jnp.float32)
    moe_out = (hidden.astype(jnp.float32) + total.reshape(rows, width)).astype(jnp.bfloat16)
    return (attn_out, moe_out)


def solution(mesh):
    in_specs = (
        P(("group", "role", "dev"), None),
        P(),
        P(("group", "role", "dev"), None),
        P(("group", "role", "dev"), None),
        P(None, ("role", "dev")),
        P(None, ("role", "dev")),
        P(("role", "dev"), None),
        P(("group", "role", "dev"), None, None),
        P(("group", "role", "dev"), None, None),
        P(("group", "role", "dev")),
        P(("group", "role", "dev"), None, None),
        P(("group", "role", "dev"), None),
        P(("group", "role", "dev"), None),
    )
    out_specs = (P(("group", "role", "dev"), None, None), P(("group", "role", "dev"), None))
    return jax.shard_map(
        per_device, mesh=mesh, in_specs=in_specs, out_specs=out_specs, check_vma=False
    )
```

time: 108 us -> 88.3 us (0.82)
  matrix products: 42 us -> 0 us
  Pallas kernels: 0 us -> 34.1 us
  starting transfers between devices: 22.9 us -> 18 us
  other arithmetic: 5.31 us -> 2.4 us
  local copies, waits for them, and re-layouts: 8.41 us -> 6 us
  waiting for transfers between devices: 27.6 us -> 26.5 us
    dot_general x9 -> x0, matrix products: 42 us -> none  [the longest x1 20.8 us: expert_block(): output = jnp.dot(act_units, w_down, preferred_element_type=jnp.float32)]
    pallas_call x0 -> x4, Pallas kernels: none -> 34.1 us  [the longest x1 29.2 us: per_device(): pl.pallas_call(functools.partial(expert_kernel, tk=tk, tn=tn, nb=nb, nd=n...]
    all_to_all x3 -> x0, waiting for transfers between devices: 27.6 us -> none  [the longest x1 17.6 us: per_device(): lax.all_to_all(partial_out, ('role', 'dev'), split_axis=0, concat_axis=0,...]
    all_to_all x3 -> x0, starting transfers between devices: 19.3 us -> none  [the longest x1 7.39 us: per_device(): lax.all_to_all(page_ids.reshape(-1), ('role', 'dev'), split_axis=0, conca...]
    ppermute x0 -> x8, waiting for transfers between devices: none -> 15.5 us  [swap(): return lax.ppermute(x, axis, [(i, i ^ bit) for i in range(size)])]
    ppermute x0 -> x8, starting transfers between devices: none -> 13.9 us  [swap(): return lax.ppermute(x, axis, [(i, i ^ bit) for i in range(size)])]
    all_to_all x1, waiting for transfers between devices: 0.01 us -> 11 us  [per_device(): lax.all_to_all(outgoing, ('role', 'dev'), split_axis=0, concat_axis=0, ti...]
    gather x4 -> x0, local copies, waits for them, and re-layouts: 4.13 us -> none  [the longest x1 1.7 us: device_attention(): page_query = queries[owners]]
  transfers between devices with their start and end apart: 4 -> 9, of which waited for: 2 -> 8; matrix products, arithmetic and copies ran while one was open for 49% -> 3% of each run, Pallas kernels for 0% -> 3%
where the time goes in v1:
time: 88.3 us; the launch traced here: 87.8 us
  Pallas kernels  34.1 us (39%)
  waiting for transfers between devices  26.5 us (30%)
  starting transfers between devices  18 us (20%)
  local copies, waits for them, and re-layouts  6 us (7%)
  other arithmetic  2.4 us (3%)
    pallas_call x1, Pallas kernels, per_device(): pl.pallas_call(functools.partial(expert_kernel, tk=tk, tn=tn, nb=nb, nd=n...  29.2 us
    ppermute x8, waiting for transfers between devices, swap(): return lax.ppermute(x, axis, [(i, i ^ bit) for i in range(size)])  15.5 us
    ppermute x8, starting transfers between devices, swap(): return lax.ppermute(x, axis, [(i, i ^ bit) for i in range(size)])  13.9 us
    all_to_all x1, waiting for transfers between devices, per_device(): lax.all_to_all(outgoing, ('role', 'dev'), split_axis=0, concat_axis=0, ti...  11 us
    all_to_all x1, starting transfers between devices, per_device(): lax.all_to_all(outgoing, ('role', 'dev'), split_axis=0, concat_axis=0, ti...  4.08 us
    unnamed x22, local copies, waits for them, and re-layouts  2.83 us
    pallas_call x1, Pallas kernels, per_device(): pl.pallas_call(attention_kernel, out_shape=jax.ShapeDtypeStruct(queries.s...  2.45 us
    pallas_call x1, Pallas kernels, per_device(): pl.pallas_call(functools.partial(pick_kernel, rounds=rounds, role_size=ro...  2.32 us
  transfers between devices with their start and end apart: 9, of which 8 were waited for; matrix products, arithmetic and copies ran while one was open for 3% of the time, Pallas kernels for 3%

profile of v1, /device:TPU:0, one launch (start us, length us, event | category | flops | bytes accessed | tf_op | source)
XLA Modules:
  0.0 87.8 jit_solution(2392677707284468731)
XLA Ops:
  0.6 0.7 reshape.36.gain_ref
  1.4 0.7 pad.4.ids_ref
  2.0 0.7 copy-done.3
  2.8 0.7 copy-done.5
  3.5 0.7 copy-done.6
  4.1 0.2 shard_map.140
  4.3 4.1 %collective-permute-start = (bf16[1,2,7424]{2,1,0:T(2,128)(2,1)S(1)}, bf16[1,2,7424]{2,1,0:T(2,128)(2,1)S(1)}, u32[]{:S(2)}, u32[]{:S(2)}) collective-permute-start(bf16[1,2,7424]{2,1,0:T(2,128)(2,1)S(1)} %bitcast.11), channel_id=1, source_target_pairs={{0,4},{1,5},{2,6},{3,7},{4,0},{5,1},{6,2},{7,3},{8,12},{9,13},{10,... | collective-permute-start | bytes 89096 | tf_op jit(solution)/shard_map/ppermute | solution.py:38
  8.4 2.2 %collective-permute-done = bf16[1,2,7424]{2,1,0:T(2,128)(2,1)S(1)} collective-permute-done((bf16[1,2,7424]{2,1,0:T(2,128)(2,1)S(1)}, bf16[1,2,7424]{2,1,0:T(2,128)(2,1)S(1)}, u32[]{:S(2)}, u32[]{:S(2)}) %collective-permute-start) | collective-permute-done | bytes 29728 | tf_op jit(solution)/shard_map/ppermute | solution.py:38
  10.7 1.7 %collective-permute-start.1 = (bf16[2,2,7424]{2,1,0:T(2,128)(2,1)S(1)}, bf16[2,2,7424]{2,1,0:T(2,128)(2,1)S(1)}, u32[]{:S(2)}, u32[]{:S(2)}) collective-permute-start(bf16[2,2,7424]{2,1,0:T(2,128)(2,1)S(1)} %pad_maximum_fusion.2), channel_id=1, source_target_pairs={{0,2},{1,3},{2,0},{3,1},{4,6},{5,7},{6,4},{7,5},{8,10},{9,11},{10,... | collective-permute-start | bytes 178184 | tf_op jit(solution)/shard_map/ppermute | solution.py:38
  12.4 2.6 %collective-permute-done.1 = bf16[2,2,7424]{2,1,0:T(2,128)(2,1)S(1)} collective-permute-done((bf16[2,2,7424]{2,1,0:T(2,128)(2,1)S(1)}, bf16[2,2,7424]{2,1,0:T(2,128)(2,1)S(1)}, u32[]{:S(2)}, u32[]{:S(2)}) %collective-permute-start.1) | collective-permute-done | bytes 59424 | tf_op jit(solution)/shard_map/ppermute | solution.py:38
  15.0 0.2 pad_maximum_fusion.1
  15.2 1.8 %collective-permute-start.2 = (bf16[4,2,7424]{2,1,0:T(2,128)(2,1)S(1)}, bf16[4,2,7424]{2,1,0:T(2,128)(2,1)S(1)}, u32[]{:S(2)}, u32[]{:S(2)}) collective-permute-start(bf16[4,2,7424]{2,1,0:T(2,128)(2,1)S(1)} %pad_maximum_fusion.1), channel_id=1, source_target_pairs={{0,1},{1,0},{2,3},{3,2},{4,5},{5,4},{6,7},{7,6},{8,9},{9,8},{10,11... | collective-permute-start | bytes 356360 | tf_op jit(solution)/shard_map/ppermute | solution.py:38
  16.9 3.1 %collective-permute-done.2 = bf16[4,2,7424]{2,1,0:T(2,128)(2,1)S(1)} collective-permute-done((bf16[4,2,7424]{2,1,0:T(2,128)(2,1)S(1)}, bf16[4,2,7424]{2,1,0:T(2,128)(2,1)S(1)}, u32[]{:S(2)}, u32[]{:S(2)}) %collective-permute-start.2) | collective-permute-done | bytes 118816 | tf_op jit(solution)/shard_map/ppermute | solution.py:38
  20.1 0.3 pad_maximum_fusion
  20.6 1.5 %collective-permute-done.3.xb_ref = bf16[16,7424]{1,0:T(8,128)(2,1)S(1)} collective-permute-done((bf16[16,7424]{1,0:T(8,128)(2,1)S(1)}, bf16[16,7424]{1,0:T(8,128)(2,1)S(1)}, u32[]{:S(2)}, u32[]{:S(2)}) %collective-permute-start.3) | collective-permute-done | bytes 237600 | tf_op jit(solution)/shard_map/ppermute | solution.py:38
  22.1 0.7 copy-done.10
  22.8 29.2 %shard_map.143 = (f32[16,7168]{1,0:T(8,128)}, bf16[16,7168]{1,0:T(8,128)(2,1)}) custom-call(s32[1]{0:T(128)} %bitcast.me_ref.expert_ref, bf16[16,7424]{1,0:T(8,128)(2,1)} %copy-done.9, bf16[16,7424]{1,0:T(8,128)(2,1)} %copy-done.10, bf16[7168,2048]{1,0:T(8,128)(2,1)} %g_ref.1, bf16[7168,2048]{1,0:T(8,128)(2,1)} %u_ref.1, bf16[2048,7168]{1,0:T(8,128)(2,1)} %d_ref.1), custom_call_target="tpu_custom_call" | custom-call | flops 2818572288 | bytes 88080384 | tf_op jit(solution)/shard_map/pallas_call | solution.py:246
  52.0 0.2 collective-permute-start.4
  52.2 1.6 %collective-permute-done.4 = bf16[16,7168]{1,0:T(8,128)(2,1)S(1)} collective-permute-done((bf16[16,7168]{1,0:T(8,128)(2,1)}, bf16[16,7168]{1,0:T(8,128)(2,1)S(1)}, u32[]{:S(2)}, u32[]{:S(2)}) %collective-permute-start.4) | collective-permute-done | bytes 229408 | tf_op jit(solution)/shard_map/ppermute | solution.py:38
  53.7 1.1 %convert_add_fusion = f32[16,7168]{1,0:T(8,128)S(1)} fusion(f32[16,7168]{1,0:T(8,128)} %get-tuple-element.4, bf16[16,7168]{1,0:T(8,128)(2,1)S(1)} %collective-permute-done.4), kind=kLoop, calls=%fused_computation | loop fusion | flops 229376 | bytes 1146880 | tf_op jit(solution)/shard_map/add | solution.py:280
  54.9 1.8 %collective-permute-start.5 = (bf16[4,2,7168]{2,1,0:T(2,128)(2,1)S(1)}, bf16[4,2,7168]{2,1,0:T(2,128)(2,1)S(1)}, u32[]{:S(2)}, u32[]{:S(2)}) collective-permute-start(bf16[4,2,7168]{2,1,0:T(2,128)(2,1)S(1)} %convert_element_type.32), channel_id=1, source_target_pairs={{0,1},{1,0},{2,3},{3,2},{4,5},{5,4},{6,7},{7,6},{8,9},{9,8},{10,11... | collective-permute-start | bytes 344072 | tf_op jit(solution)/shard_map/ppermute | solution.py:38
  56.8 3.3 %collective-permute-done.5 = bf16[4,2,7168]{2,1,0:T(2,128)(2,1)S(1)} collective-permute-done((bf16[4,2,7168]{2,1,0:T(2,128)(2,1)S(1)}, bf16[4,2,7168]{2,1,0:T(2,128)(2,1)S(1)}, u32[]{:S(2)}, u32[]{:S(2)}) %collective-permute-start.5) | collective-permute-done | bytes 114720 | tf_op jit(solution)/shard_map/ppermute | solution.py:38
  60.2 1.7 %collective-permute-start.6 = (bf16[2,2,7168]{2,1,0:T(2,128)(2,1)S(1)}, bf16[2,2,7168]{2,1,0:T(2,128)(2,1)S(1)}, u32[]{:S(2)}, u32[]{:S(2)}) collective-permute-start(bf16[2,2,7168]{2,1,0:T(2,128)(2,1)S(1)} %slice.59), channel_id=1, source_target_pairs={{0,2},{1,3},{2,0},{3,1},{4,6},{5,7},{6,4},{7,5},{8,10},{9,11},{10,... | collective-permute-start | bytes 172040 | tf_op jit(solution)/shard_map/ppermute | solution.py:38
  61.9 0.7 slice.33
  62.6 0.7 slice.34
  63.3 1.2 %collective-permute-done.6 = bf16[2,2,7168]{2,1,0:T(2,128)(2,1)S(1)} collective-permute-done((bf16[2,2,7168]{2,1,0:T(2,128)(2,1)S(1)}, bf16[2,2,7168]{2,1,0:T(2,128)(2,1)S(1)}, u32[]{:S(2)}, u32[]{:S(2)}) %collective-permute-start.6) | collective-permute-done | bytes 57376 | tf_op jit(solution)/shard_map/ppermute | solution.py:38
  64.5 2.7 %collective-permute-start.7 = (bf16[1,2,7168]{2,1,0:T(2,128)(2,1)S(1)}, bf16[1,2,7168]{2,1,0:T(2,128)(2,1)S(1)}, u32[]{:S(2)}, u32[]{:S(2)}) collective-permute-start(bf16[1,2,7168]{2,1,0:T(2,128)(2,1)S(1)} %slice.60), channel_id=1, source_target_pairs={{0,4},{1,5},{2,6},{3,7},{4,0},{5,1},{6,2},{7,3},{8,12},{9,13},{10,... | collective-permute-start | bytes 86024 | tf_op jit(solution)/shard_map/ppermute | solution.py:38
  67.2 2.3 %shard_map.141 = bf16[16,16,576]{2,1,0:T(8,128)(2,1)} custom-call(s32[1]{0:T(128)} %bitcast.me_ref.expert_ref, s32[16,16]{1,0:T(8,128)S(1)} %maximum_convert_fusion.ids_ref, bf16[16,16,576]{2,1,0:T(8,128)(2,1)S(1)} %copy-done), custom_call_target="tpu_custom_call" | custom-call | tf_op jit(solution)/shard_map/pallas_call | solution.py:234
  69.6 4.1 %all-to-all-start = ((bf16[16,16,576]{2,1,0:T(8,128)(2,1)}), bf16[16,16,576]{2,1,0:T(8,128)(2,1)S(1)}, u32[]{:S(2)}, u32[]{:S(2)}) async-start(bf16[16,16,576]{2,1,0:T(8,128)(2,1)} %shard_map.141), calls=%async_computation | async-start | bytes 655360 | tf_op jit(solution)/shard_map/all_to_all | solution.py:242
  73.7 0.7 fusion.2
  74.3 11.0 %all-to-all-done.page_ref = bf16[16,16,576]{2,1,0:T(8,128)(2,1)S(1)} async-done(((bf16[16,16,576]{2,1,0:T(8,128)(2,1)}), bf16[16,16,576]{2,1,0:T(8,128)(2,1)S(1)}, u32[]{:S(2)}, u32[]{:S(2)}) %all-to-all-start) | async-done | bytes 294944 | tf_op jit(solution)/shard_map/all_to_all | solution.py:242
  85.4 2.4 %shard_map.142 = bf16[2,64,512]{2,1,0:T(8,128)(2,1)} custom-call(s32[2]{0:T(128)S(1)} %copy-done.7, s32[1,16]{1,0:T(1,128)S(1)} %copy-done.8, bf16[2,64,576]{2,1,0:T(8,128)(2,1)S(1)} %copy-done.1, bf16[2,64,576]{2,1,0:T(8,128)(2,1)S(1)} %copy-done.2, bf16[16,16,576]{2,1,0:T(8,128)(2,1)S(1)} %all-to-all-done.page_ref), custom_call_target="tpu_custom_call" | custom-call | flops 134217728 | bytes 1048576 | tf_op jit(solution)/shard_map/pallas_call | solution.py:271
  (31 shorter events, 0.7 us)
Async XLA Ops:
  2.0 0.7 copy-start.3
  2.8 0.7 copy-start.5
  3.5 0.7 copy-start.6
  4.3 6.3 %collective-permute-start = (bf16[1,2,7424]{2,1,0:T(2,128)(2,1)S(1)}, bf16[1,2,7424]{2,1,0:T(2,128)(2,1)S(1)}, u32[]{:S(2)}, u32[]{:S(2)}) collective-permute-start(bf16[1,2,7424]{2,1,0:T(2,128)(2,1)S(1)} %bitcast.11), channel_id=1, source_target_pairs={{0,4},{1,5},{2,6},{3,7},{4,0},{5,1},{6,2},{7,3},{8,12},{9,13},{10,... | collective-permute-start | bytes 89096 | tf_op jit(solution)/shard_map/ppermute | solution.py:38
  10.7 4.3 %collective-permute-start.1 = (bf16[2,2,7424]{2,1,0:T(2,128)(2,1)S(1)}, bf16[2,2,7424]{2,1,0:T(2,128)(2,1)S(1)}, u32[]{:S(2)}, u32[]{:S(2)}) collective-permute-start(bf16[2,2,7424]{2,1,0:T(2,128)(2,1)S(1)} %pad_maximum_fusion.2), channel_id=1, source_target_pairs={{0,2},{1,3},{2,0},{3,1},{4,6},{5,7},{6,4},{7,5},{8,10},{9,11},{10,... | collective-permute-start | bytes 178184 | tf_op jit(solution)/shard_map/ppermute | solution.py:38
  15.2 4.9 %collective-permute-start.2 = (bf16[4,2,7424]{2,1,0:T(2,128)(2,1)S(1)}, bf16[4,2,7424]{2,1,0:T(2,128)(2,1)S(1)}, u32[]{:S(2)}, u32[]{:S(2)}) collective-permute-start(bf16[4,2,7424]{2,1,0:T(2,128)(2,1)S(1)} %pad_maximum_fusion.1), channel_id=1, source_target_pairs={{0,1},{1,0},{2,3},{3,2},{4,5},{5,4},{6,7},{7,6},{8,9},{9,8},{10,11... | collective-permute-start | bytes 356360 | tf_op jit(solution)/shard_map/ppermute | solution.py:38
  20.5 1.6 %copy-start.9 = (bf16[16,7424]{1,0:T(8,128)(2,1)}, bf16[16,7424]{1,0:T(8,128)(2,1)S(1)}, u32[]{:S(2)}) copy-start(bf16[16,7424]{1,0:T(8,128)(2,1)S(1)} %reshape.37.xa_ref) | copy-start | bytes 712708
  20.5 1.6 %collective-permute-start.3 = (bf16[16,7424]{1,0:T(8,128)(2,1)S(1)}, bf16[16,7424]{1,0:T(8,128)(2,1)S(1)}, u32[]{:S(2)}, u32[]{:S(2)}) collective-permute-start(bf16[16,7424]{1,0:T(8,128)(2,1)S(1)} %reshape.37.xa_ref), channel_id=1, source_target_pairs={{0,8},{8,0},{1,9},{9,1},{2,10},{10,2},{3,11},{11,3},{4,12},{12,4},... | collective-permute-start | bytes 712712 | tf_op jit(solution)/shard_map/ppermute | solution.py:38
  22.1 0.7 copy-start.10
  22.8 44.5 %copy-start = (bf16[16,16,576]{2,1,0:T(8,128)(2,1)S(1)}, bf16[16,16,576]{2,1,0:T(8,128)(2,1)}, u32[]{:S(2)}) copy-start(bf16[16,16,576]{2,1,0:T(8,128)(2,1)} %pool_ref.1) | copy-start | bytes 884740
  22.8 50.9 %copy-start.4 = (bf16[2,7168]{1,0:T(2,128)(2,1)S(1)}, bf16[2,7168]{1,0:T(2,128)(2,1)}, u32[]{:S(2)}) copy-start(bf16[2,7168]{1,0:T(2,128)(2,1)} %hid_ref.1) | copy-start | bytes 86020
  22.8 62.6 %copy-start.1 = (bf16[2,64,576]{2,1,0:T(8,128)(2,1)S(1)}, bf16[2,64,576]{2,1,0:T(8,128)(2,1)}, u32[]{:S(2)}) copy-start(bf16[2,64,576]{2,1,0:T(8,128)(2,1)} %q_ref.1) | copy-start | bytes 442372
  22.8 62.6 %copy-start.2 = (bf16[2,64,576]{2,1,0:T(8,128)(2,1)S(1)}, bf16[2,64,576]{2,1,0:T(8,128)(2,1)}, u32[]{:S(2)}) copy-start(bf16[2,64,576]{2,1,0:T(8,128)(2,1)} %local_ref.1) | copy-start | bytes 442372
  22.8 62.6 %copy-start.7 = (s32[2]{0:T(128)S(1)}, s32[2]{0:T(128)}, u32[]{:S(2)}) copy-start(s32[2]{0:T(128)} %len_ref.1) | copy-start | bytes 28
  22.8 62.6 %copy-start.8 = (s32[1,16]{1,0:T(1,128)S(1)}, s32[1,16]{1,0:T(1,128)}, u32[]{:S(2)}) copy-start(s32[1,16]{1,0:T(1,128)} %owner_ref.1) | copy-start | bytes 196
  52.0 1.8 %collective-permute-start.4 = (bf16[16,7168]{1,0:T(8,128)(2,1)}, bf16[16,7168]{1,0:T(8,128)(2,1)S(1)}, u32[]{:S(2)}, u32[]{:S(2)}) collective-permute-start(bf16[16,7168]{1,0:T(8,128)(2,1)} %get-tuple-element.5), channel_id=1, source_target_pairs={{0,8},{8,0},{1,9},{9,1},{2,10},{10,2},{3,11},{11,3},{4,12},{12,4},... | collective-permute-start | bytes 688136 | tf_op jit(solution)/shard_map/ppermute | solution.py:38
  54.9 5.3 %collective-permute-start.5 = (bf16[4,2,7168]{2,1,0:T(2,128)(2,1)S(1)}, bf16[4,2,7168]{2,1,0:T(2,128)(2,1)S(1)}, u32[]{:S(2)}, u32[]{:S(2)}) collective-permute-start(bf16[4,2,7168]{2,1,0:T(2,128)(2,1)S(1)} %convert_element_type.32), channel_id=1, source_target_pairs={{0,1},{1,0},{2,3},{3,2},{4,5},{5,4},{6,7},{7,6},{8,9},{9,8},{10,11... | collective-permute-start | bytes 344072 | tf_op jit(solution)/shard_map/ppermute | solution.py:38
  60.2 4.2 %collective-permute-start.6 = (bf16[2,2,7168]{2,1,0:T(2,128)(2,1)S(1)}, bf16[2,2,7168]{2,1,0:T(2,128)(2,1)S(1)}, u32[]{:S(2)}, u32[]{:S(2)}) collective-permute-start(bf16[2,2,7168]{2,1,0:T(2,128)(2,1)S(1)} %slice.59), channel_id=1, source_target_pairs={{0,2},{1,3},{2,0},{3,1},{4,6},{5,7},{6,4},{7,5},{8,10},{9,11},{10,... | collective-permute-start | bytes 172040 | tf_op jit(solution)/shard_map/ppermute | solution.py:38
  64.5 9.1 %collective-permute-start.7 = (bf16[1,2,7168]{2,1,0:T(2,128)(2,1)S(1)}, bf16[1,2,7168]{2,1,0:T(2,128)(2,1)S(1)}, u32[]{:S(2)}, u32[]{:S(2)}) collective-permute-start(bf16[1,2,7168]{2,1,0:T(2,128)(2,1)S(1)} %slice.60), channel_id=1, source_target_pairs={{0,4},{1,5},{2,6},{3,7},{4,0},{5,1},{6,2},{7,3},{8,12},{9,13},{10,... | collective-permute-start | bytes 86024 | tf_op jit(solution)/shard_map/ppermute | solution.py:38
  69.6 15.8 %all-to-all-start = ((bf16[16,16,576]{2,1,0:T(8,128)(2,1)}), bf16[16,16,576]{2,1,0:T(8,128)(2,1)S(1)}, u32[]{:S(2)}, u32[]{:S(2)}) async-start(bf16[16,16,576]{2,1,0:T(8,128)(2,1)} %shard_map.141), calls=%async_computation | async-start | bytes 655360 | tf_op jit(solution)/shard_map/all_to_all | solution.py:242

commit v2 on v1

v2 whole, which is shorter than its diff:
```python
import functools

import jax
import jax.numpy as jnp
from jax import lax
from jax.experimental import pallas as pl
from jax.experimental.pallas import tpu as pltpu
from jax.sharding import PartitionSpec as P


ROPE = 64
EXPERTS = 16
LANES = 128

LOADS = (3,3,3,1)
GATE_SLOTS = 3
UP_SLOTS = 6
DOWN_SLOTS = 6

score_scale = 192.0 ** (-0.5)
norm_eps = 1e-06


VM = pl.BlockSpec(memory_space=pltpu.VMEM)
SM = pl.BlockSpec(memory_space=pltpu.SMEM)
HBM = pl.BlockSpec(memory_space=pltpu.HBM)


def role_swap(x):
    size = lax.axis_size("role")
    return lax.ppermute(x, "role", [(i, size - 1 - i) for i in range(size)])


def pack_kernel(me_ref, hid_ref, gain_ref, routes_ref, weights_ref, ids_ref, out_ref, hid, gain, routes_v, weights_v, ids_v, sems):
    rows, width = hid.shape
    copies = [
        pltpu.make_async_copy(src, dst, sems.at[i])
        for i, (src, dst) in enumerate(
            ((hid_ref, hid), (gain_ref, gain), (routes_ref, routes_v), (weights_ref, weights_v), (ids_ref, ids_v))
        )
    ]
    for c in copies:
        c.start()
    for c in copies:
        c.wait()
    x = hid[...].astype(jnp.float32)
    inv = lax.rsqrt(jnp.mean(x * x, axis=1, keepdims=True) + norm_eps)
    gains = gain[...].astype(jnp.float32).reshape(1, width)
    normed = (x * inv * gains).astype(jnp.bfloat16)
    lane = lax.broadcasted_iota(jnp.int32, (rows, LANES), 1)
    expert = lax.rem(lane, EXPERTS)
    routes = routes_v[...]
    weights = weights_v[...]
    weight = jnp.zeros((rows, LANES), jnp.float32)
    for k in range(routes.shape[1]):
        weight = weight + jnp.where(routes[:, k : k + 1] == expert, weights[:, k : k + 1], 0.0)
    high = weight.astype(jnp.bfloat16).astype(jnp.float32)
    tail = jnp.where(lane < EXPERTS, high, jnp.where(lane < 2 * EXPERTS, weight - high, 0.0))
    tail = tail.astype(jnp.bfloat16)
    count = ids_v.shape[1]
    ids = jnp.broadcast_to(ids_v[...].astype(jnp.float32), (rows, count)).astype(jnp.bfloat16)
    out_ref[:, :width] = normed
    out_ref[:, width : width + LANES] = tail
    out_ref[:, width + LANES : width + LANES + count] = ids


def merge_kernel(me_ref, own_ref, got_ref, out_ref, *, bit):
    rows = own_ref.shape[0]
    upper = (me_ref[0] & bit) != 0

    @pl.when(upper)
    def _():
        out_ref[:rows] = got_ref[...]
        out_ref[rows:] = own_ref[...]

    @pl.when(jnp.logical_not(upper))
    def _():
        out_ref[:rows] = own_ref[...]
        out_ref[rows:] = got_ref[...]


def load_kernel(src_ref, out_ref, sems, *, start):
    parts = sems.shape[0]
    step = out_ref.shape[0] // parts
    copies = [
        pltpu.make_async_copy(src_ref.at[pl.ds(start + i * step, step)], out_ref.at[pl.ds(i * step, step)], sems.at[i])
        for i in range(parts)
    ]
    for c in copies:
        c.start()
    for c in copies:
        c.wait()


def expert_kernel(*refs, tk, tn, base, rows, slices, role_size, loads):
    me_ref, xa_ref, xb_ref = refs[:3]
    pre_refs = refs[3 : 3 + loads]
    g_ref, u_ref, d_ref, pool_ref, keep_ref, send_ref, page_ref = refs[3 + loads : 10 + loads]
    gb, ub, db, ga, ua, h, wsel, vec, ids, semg, semu, semd, semi, semp = refs[10 + loads :]
    width = d_ref.shape[1]
    n1, n2 = width // tk, width // tn
    ready = sum(r.shape[0] for r in pre_refs) // tk
    nb, nd, ng = ub.shape[0], db.shape[0], gb.shape[0]
    half = xa_ref.shape[0]
    me = me_ref[0]

    def cg(i):
        s = lax.rem(i - ready, ng)
        return pltpu.make_async_copy(g_ref.at[pl.ds(i * tk, tk)], gb.at[s], semg.at[s])

    def cu(i):
        s = lax.rem(i, nb)
        return pltpu.make_async_copy(u_ref.at[pl.ds(i * tk, tk)], ub.at[s], semu.at[s])

    def cd(j):
        s = lax.rem(j, nd)
        cols = pl.ds(pl.multiple_of(j * tn, tn), tn)
        return pltpu.make_async_copy(d_ref.at[:, cols], db.at[s], semd.at[s])

    for i in range(ready, min(ready + ng, n1)):
        cg(i).start()
    for i in range(min(nb, n1)):
        cu(i).start()
    cols = vec.shape[1]
    vec[:half] = xa_ref[:, base : base + cols].astype(jnp.float32).astype(jnp.int32)
    vec[half:] = xb_ref[:, base : base + cols].astype(jnp.float32).astype(jnp.int32)
    move = pltpu.make_async_copy(vec, ids, semi)
    move.start()

    ga[...] = jnp.zeros_like(ga)
    ua[...] = jnp.zeros_like(ua)
    expert = me // slices
    lane = lax.broadcasted_iota(jnp.int32, (half, LANES), 1)
    chosen = (lane == expert) | (lane == expert + EXPERTS)
    for i, ref in enumerate((xa_ref, xb_ref)):
        tail = ref[:, width : width + LANES].astype(jnp.float32)
        wsel[i * half : (i + 1) * half] = jnp.sum(jnp.where(chosen, tail, 0.0), axis=1, keepdims=True)

    def rows_of(i):
        at = pl.ds(pl.multiple_of(i * tk, tk), tk)
        return jnp.concatenate([xa_ref[:, at], xb_ref[:, at]], axis=0)

    first = 0
    for ref in pre_refs:
        count = ref.shape[0] // tk

        def early(i, c, ref=ref, first=first):
            at = pl.ds(pl.multiple_of((i - first) * tk, tk), tk)
            ga[...] += jnp.dot(rows_of(i), ref[at, :], preferred_element_type=jnp.float32)
            return c

        lax.fori_loop(first, first + count, early, 0)
        first += count

    move.wait()
    count = page_ref.shape[0]
    peers = count // role_size
    bits = peers.bit_length() - 1
    mine = me // peers

    def page_start(d, c):
        other = d // peers != mine
        within = lax.rem(d, peers)
        block = jnp.int32(0)
        for b in range(bits):
            block = block * 2 + (lax.shift_right_logical(within, jnp.int32(b)) & 1)
        row = block * rows + jnp.where(other, half, 0)
        pltpu.make_async_copy(pool_ref.at[ids[row, me]], page_ref.at[d], semp.at[d]).start()
        return c

    def page_wait(d, c):
        pltpu.make_async_copy(pool_ref.at[0], page_ref.at[d], semp.at[d]).wait()
        return c

    lax.fori_loop(0, count, page_start, 0)

    def late(i, c):
        cg(i).wait()
        ga[...] += jnp.dot(rows_of(i), gb[lax.rem(i - ready, ng)], preferred_element_type=jnp.float32)

        @pl.when(i + ng < n1)
        def _():
            cg(i + ng).start()

        return c

    def up(i, c):
        cu(i).wait()
        ua[...] += jnp.dot(rows_of(i), ub[lax.rem(i, nb)], preferred_element_type=jnp.float32)

        @pl.when(i + nb < n1)
        def _():
            cu(i + nb).start()

        @pl.when((i + nd >= n1) & (i + nd - n1 < n2))
        def _():
            cd(i + nd - n1).start()

        return c

    lax.fori_loop(ready, n1, late, 0)
    lax.fori_loop(0, n1, up, 0)
    g = ga[...]
    h[...] = ((g / (1.0 + jnp.exp(-g))) * ua[...]).astype(jnp.bfloat16)

    def down(j, c):
        cd(j).wait()
        at = pl.ds(pl.multiple_of(j * tn, tn), tn)
        out = jnp.dot(h[...], db[lax.rem(j, nd)], preferred_element_type=jnp.float32)
        out = out * wsel[...]
        keep_ref[:, at] = out[:half]
        send_ref[:, at] = out[half:].astype(jnp.bfloat16)

        @pl.when(j + nd < n2)
        def _():
            cd(j + nd).start()

        return c

    lax.fori_loop(0, n2, down, 0)
    lax.fori_loop(0, count, page_wait, 0)


def attention_kernel(len_ref, owner_ref, q_ref, local_ref, page_ref, out_ref):
    requests, heads, width = q_ref.shape
    value = out_ref.shape[2]
    local_len = local_ref.shape[1]
    pages, page_len, _ = page_ref.shape
    paged = page_ref[...].reshape(pages * page_len, width)
    row = lax.broadcasted_iota(jnp.int32, (pages, pages * page_len), 0)
    col = lax.broadcasted_iota(jnp.int32, (pages, pages * page_len), 1)
    inside = (col >= row * page_len) & (col < (row + 1) * page_len)
    owner = jnp.broadcast_to(jnp.transpose(owner_ref[...].astype(jnp.float32)), inside.shape)
    key_owner = jnp.sum(jnp.where(inside, owner, 0.0), axis=0, keepdims=True)
    nt = (((1,), (1,)), ((), ()))
    for r in range(requests):
        q = q_ref[r]
        local = local_ref[r]
        s_local = lax.dot_general(q, local, nt, preferred_element_type=jnp.float32) * score_scale
        pos = lax.broadcasted_iota(jnp.int32, (heads, local_len), 1)
        s_local = jnp.where(pos < len_ref[r], s_local, -jnp.inf)
        s_page = lax.dot_general(q, paged, nt, preferred_element_type=jnp.float32) * score_scale
        s_page = jnp.where(key_owner == float(r), s_page, -jnp.inf)
        peak = jnp.maximum(jnp.max(s_local, axis=1, keepdims=True), jnp.max(s_page, axis=1, keepdims=True))
        e_local = jnp.exp(s_local - peak)
        e_page = jnp.exp(s_page - peak)
        total = jnp.sum(e_local, axis=1, keepdims=True) + jnp.sum(e_page, axis=1, keepdims=True)
        p_local = (e_local / total).astype(jnp.bfloat16)
        p_page = (e_page / total).astype(jnp.bfloat16)
        out = jnp.dot(p_local, local[:, :value], preferred_element_type=jnp.float32)
        out = out + jnp.dot(p_page, paged[:, :value], preferred_element_type=jnp.float32)
        out_ref[r] = out.astype(jnp.bfloat16)


def tile_of(size, want):
    tile = min(size, want)
    while size % tile:
        tile -= LANES
    return tile


def per_device(
    hidden, norm_gain, routes, gate_weights, w_gate, w_up, w_down,
    queries, local_cache, cache_lengths, swap_pool, page_ids, page_owner,
):
    role_size, dev_size = lax.axis_size("role"), lax.axis_size("dev")
    devices = role_size * dev_size
    slices = devices // EXPERTS
    me = lax.axis_index("role") * dev_size + lax.axis_index("dev")
    me_arr = jnp.reshape(me, (1,)).astype(jnp.int32)
    rows, width = hidden.shape
    units = w_gate.shape[1]
    id_cols = pl.cdiv(devices, LANES) * LANES
    packed_width = width + LANES + id_cols
    half = dev_size * rows
    total_rows = role_size * half
    tk = tn = tile_of(width, 512)
    weight_bytes = 2 * width * units
    bits = [dev_size >> (k + 1) for k in range(dev_size.bit_length() - 1)]
    weights_in = [pltpu.with_memory_space_constraint(w, pltpu.HBM) for w in (w_gate, w_up, w_down)]
    pool_in = pltpu.with_memory_space_constraint(swap_pool, pltpu.HBM)
    small_in = [
        pltpu.with_memory_space_constraint(a, pltpu.HBM)
        for a in (hidden, norm_gain, routes, gate_weights, page_ids)
    ]

    held = pl.pallas_call(
        pack_kernel,
        out_shape=jax.ShapeDtypeStruct((rows, packed_width), jnp.bfloat16),
        in_specs=[SM] + [HBM] * 5,
        out_specs=VM,
        scratch_shapes=[
            pltpu.VMEM(hidden.shape, hidden.dtype),
            pltpu.VMEM(norm_gain.shape, norm_gain.dtype),
            pltpu.VMEM(routes.shape, routes.dtype),
            pltpu.VMEM(gate_weights.shape, gate_weights.dtype),
            pltpu.VMEM(page_ids.shape, page_ids.dtype),
            pltpu.SemaphoreType.DMA((5,)),
        ],
        compiler_params=pltpu.CompilerParams(vmem_limit_bytes=6 << 20),
    )(me_arr, *small_in)

    def load(index, start):
        size = LOADS[index] * tk
        return pl.pallas_call(
            functools.partial(load_kernel, start=start),
            out_shape=pltpu.VMEM((size, units), jnp.bfloat16),
            in_specs=[HBM],
            out_specs=VM,
            scratch_shapes=[pltpu.SemaphoreType.DMA((LOADS[index],))],
            compiler_params=pltpu.CompilerParams(vmem_limit_bytes=1 << 20),
            cost_estimate=pl.CostEstimate(flops=0, bytes_accessed=2 * size * units, transcendentals=0),
        )(weights_in[0])

    loaded = []
    taken = 0
    for k, bit in enumerate(bits):
        got = lax.ppermute(held, "dev", [(i, i ^ bit) for i in range(dev_size)])
        if k < len(LOADS) - 1:
            loaded.append(load(k, taken))
            taken += LOADS[k] * tk
        held = pl.pallas_call(
            functools.partial(merge_kernel, bit=bit),
            out_shape=jax.ShapeDtypeStruct((2 * held.shape[0], packed_width), jnp.bfloat16),
            in_specs=[SM, VM, VM],
            out_specs=VM,
            compiler_params=pltpu.CompilerParams(vmem_limit_bytes=6 << 20),
        )(me_arr, held, got)
    other = role_swap(held)
    loaded.append(load(len(LOADS) - 1, taken))

    keep, send, outgoing = pl.pallas_call(
        functools.partial(
            expert_kernel, tk=tk, tn=tn, base=width + LANES, rows=rows, slices=slices,
            role_size=role_size, loads=len(loaded),
        ),
        out_shape=(
            jax.ShapeDtypeStruct((half, width), jnp.float32),
            jax.ShapeDtypeStruct((half, width), jnp.bfloat16),
            jax.ShapeDtypeStruct((devices,) + swap_pool.shape[1:], jnp.bfloat16),
        ),
        in_specs=[SM, VM, VM] + [VM] * len(loaded) + [HBM] * 4,
        out_specs=(VM, VM, VM),
        scratch_shapes=[
            pltpu.VMEM((GATE_SLOTS, tk, units), jnp.bfloat16),
            pltpu.VMEM((UP_SLOTS, tk, units), jnp.bfloat16),
            pltpu.VMEM((DOWN_SLOTS, units, tn), jnp.bfloat16),
            pltpu.VMEM((total_rows, units), jnp.float32),
            pltpu.VMEM((total_rows, units), jnp.float32),
            pltpu.VMEM((total_rows, units), jnp.bfloat16),
            pltpu.VMEM((total_rows, 1), jnp.float32),
            pltpu.VMEM((total_rows, id_cols), jnp.int32),
            pltpu.SMEM((total_rows, id_cols), jnp.int32),
            pltpu.SemaphoreType.DMA((GATE_SLOTS,)),
            pltpu.SemaphoreType.DMA((UP_SLOTS,)),
            pltpu.SemaphoreType.DMA((DOWN_SLOTS,)),
            pltpu.SemaphoreType.DMA,
            pltpu.SemaphoreType.DMA((devices,)),
        ],
        compiler_params=pltpu.CompilerParams(vmem_limit_bytes=32 << 20),
        cost_estimate=pl.CostEstimate(
            flops=6 * total_rows * width * units, bytes_accessed=3 * weight_bytes, transcendentals=0
        ),
    )(me_arr, held, other, *loaded, *weights_in, pool_in)

    crossed = role_swap(send)
    arrived = lax.all_to_all(outgoing, ("role", "dev"), split_axis=0, concat_axis=0, tiled=True)

    attn_out = pl.pallas_call(
        attention_kernel,
        out_shape=jax.ShapeDtypeStruct(queries.shape[:2] + (queries.shape[2] - ROPE,), jnp.bfloat16),
        in_specs=[SM, VM, VM, VM, VM],
        out_specs=VM,
        compiler_params=pltpu.CompilerParams(vmem_limit_bytes=20 << 20),
        cost_estimate=pl.CostEstimate(flops=1 << 27, bytes_accessed=1 << 20, transcendentals=1 << 16),
    )(cache_lengths, page_owner, queries, local_cache, arrived)

    total = (keep + crossed.astype(jnp.float32)).astype(jnp.bfloat16)
    count = len(bits)
    total = total.reshape((2,) * count + (rows, width))
    total = total.transpose(tuple(range(count - 1, -1, -1)) + (count, count + 1)).reshape(dev_size, rows, width)
    parts = lax.all_to_all(total, "dev", split_axis=0, concat_axis=0, tiled=True)
    total = jnp.sum(parts.astype(jnp.float32), axis=0)
    moe_out = (hidden.astype(jnp.float32) + total).astype(jnp.bfloat16)
    return (attn_out, moe_out)


def solution(mesh):
    in_specs = (
        P(("group", "role", "dev"), None),
        P(),
        P(("group", "role", "dev"), None),
        P(("group", "role", "dev"), None),
        P(None, ("role", "dev")),
        P(None, ("role", "dev")),
        P(("role", "dev"), None),
        P(("group", "role", "dev"), None, None),
        P(("group", "role", "dev"), None, None),
        P(("group", "role", "dev")),
        P(("group", "role", "dev"), None, None),
        P(("group", "role", "dev"), None),
        P(("group", "role", "dev"), None),
    )
    out_specs = (P(("group", "role", "dev"), None, None), P(("group", "role", "dev"), None))
    return jax.shard_map(per_device, mesh=mesh, in_specs=in_specs, out_specs=out_specs, check_vma=False)
```

time: 88.3 us -> 83.4 us (0.945)
  local copies, waits for them, and re-layouts: 6 us -> 0.97 us
  Pallas kernels: 34.1 us -> 38.3 us
  waiting for transfers between devices: 26.5 us -> 24.2 us
  other arithmetic: 2.4 us -> 0.89 us
    ppermute x8 -> x5, waiting for transfers between devices: 15.5 us -> 7.93 us  [the longest x3 7.93 us: per_device(): got = lax.ppermute(held, 'dev', [(i, i ^ bit) for i in range(dev_size)])]
    ppermute x8 -> x5, starting transfers between devices: 13.9 us -> 8.17 us  [the longest x3 7.55 us: per_device(): got = lax.ppermute(held, 'dev', [(i, i ^ bit) for i in range(dev_size)])]
    all_to_all x0 -> x1, waiting for transfers between devices: none -> 5.62 us  [per_device(): lax.all_to_all(total, 'dev', split_axis=0, concat_axis=0, tiled=True)]
    pallas_call x2 -> x8, Pallas kernels: 31.5 us -> 34.9 us  [the longest x1 24.6 us: per_device(): pl.pallas_call(functools.partial(expert_kernel, tk=tk, tn=tn, base=width...]
    all_to_all x0 -> x1, starting transfers between devices: none -> 3.4 us  [per_device(): lax.all_to_all(total, 'dev', split_axis=0, concat_axis=0, tiled=True)]
    unnamed x22 -> x10, local copies, waits for them, and re-layouts: 2.83 us -> 0.03 us
    all_to_all x1, starting transfers between devices: 4.08 us -> 6.14 us  [per_device(): lax.all_to_all(outgoing, ('role', 'dev'), split_axis=0, concat_axis=0, ti...]
    slice x6 -> x0, local copies, waits for them, and re-layouts: 1.49 us -> none  [the longest x1 0.7 us: per_device(): other[::rows, width + LANES:width + LANES + devices]]
  transfers between devices with their start and end apart: 9 -> 7, of which waited for: 8 -> 5; matrix products, arithmetic and copies ran while one was open for 3% -> 1% of each run, Pallas kernels for 3% -> 15%
where the time goes in v2:
time: 83.4 us; the launch traced here: 83 us
  Pallas kernels  38.3 us (46%)
  waiting for transfers between devices  24.2 us (29%)
  starting transfers between devices  17.7 us (21%)
  local copies, waits for them, and re-layouts  0.97 us (1%)
  other arithmetic  0.89 us (1%)
    pallas_call x1, Pallas kernels, per_device(): pl.pallas_call(functools.partial(expert_kernel, tk=tk, tn=tn, base=width...  24.6 us
    all_to_all x1, waiting for transfers between devices, per_device(): lax.all_to_all(outgoing, ('role', 'dev'), split_axis=0, concat_axis=0, ti...  10.7 us
    pallas_call x4, Pallas kernels, load(): pl.pallas_call(functools.partial(load_kernel, start=start), out_shape=plt...  10.3 us
    ppermute x3, waiting for transfers between devices, per_device(): got = lax.ppermute(held, 'dev', [(i, i ^ bit) for i in range(dev_size)])  7.93 us
    ppermute x3, starting transfers between devices, per_device(): got = lax.ppermute(held, 'dev', [(i, i ^ bit) for i in range(dev_size)])  7.55 us
    all_to_all x1, starting transfers between devices, per_device(): lax.all_to_all(outgoing, ('role', 'dev'), split_axis=0, concat_axis=0, ti...  6.14 us
    all_to_all x1, waiting for transfers between devices, per_device(): lax.all_to_all(total, 'dev', split_axis=0, concat_axis=0, tiled=True)  5.62 us
    all_to_all x1, starting transfers between devices, per_device(): lax.all_to_all(total, 'dev', split_axis=0, concat_axis=0, tiled=True)  3.4 us
  transfers between devices with their start and end apart: 7, of which 5 were waited for; matrix products, arithmetic and copies ran while one was open for 1% of the time, Pallas kernels for 15%

profile of v2, /device:TPU:0, one launch (start us, length us, event | category | flops | bytes accessed | tf_op | source)
XLA Modules:
  0.0 83.0 jit_solution(3779727289421384055)
XLA Ops:
  0.6 1.0 %shard_map.140.own_ref = bf16[2,7424]{1,0:T(2,128)(2,1)S(1)} custom-call(s32[1]{0:T(128)} %bitcast.me_ref.refs_0_, bf16[2,7168]{1,0:T(2,128)(2,1)} %hid_ref.1, bf16[7168]{0:T(1024)(128)(2,1)} %gain_ref.1, s32[2,8]{1,0:T(2,128)} %routes_ref.1, f32[2,8]{1,0:T(2,128)} %weights_ref.1, s32[1,16]{1,0:T(1,128)} %ids_ref.1), custom_call_target="tpu_custom_call" | custom-call | tf_op jit(solution)/shard_map/pallas_call | solution.py:287
  1.6 4.1 %collective-permute-start = (bf16[2,7424]{1,0:T(2,128)(2,1)S(1)}, bf16[2,7424]{1,0:T(2,128)(2,1)S(1)}, u32[]{:S(2)}, u32[]{:S(2)}) collective-permute-start(bf16[2,7424]{1,0:T(2,128)(2,1)S(1)} %shard_map.140.own_ref), channel_id=1, source_target_pairs={{0,4},{1,5},{2,6},{3,7},{4,0},{5,1},{6,2},{7,3},{8,12},{9,13},{10,... | collective-permute-start | bytes 89096 | tf_op jit(solution)/shard_map/ppermute | solution.py:318
  5.8 2.2 %collective-permute-done.got_ref = bf16[2,7424]{1,0:T(2,128)(2,1)S(1)} collective-permute-done((bf16[2,7424]{1,0:T(2,128)(2,1)S(1)}, bf16[2,7424]{1,0:T(2,128)(2,1)S(1)}, u32[]{:S(2)}, u32[]{:S(2)}) %collective-permute-start) | collective-permute-done | bytes 29728 | tf_op jit(solution)/shard_map/ppermute | solution.py:318
  8.0 1.7 %collective-permute-start.1 = (bf16[4,7424]{1,0:T(4,128)(2,1)S(1)}, bf16[4,7424]{1,0:T(4,128)(2,1)S(1)}, u32[]{:S(2)}, u32[]{:S(2)}) collective-permute-start(bf16[4,7424]{1,0:T(4,128)(2,1)S(1)} %shard_map.141.own_ref), channel_id=1, source_target_pairs={{0,2},{1,3},{2,0},{3,1},{4,6},{5,7},{6,4},{7,5},{8,10},{9,11},{10,... | collective-permute-start | bytes 178184 | tf_op jit(solution)/shard_map/ppermute | solution.py:318
  9.6 2.6 %collective-permute-done.1.got_ref = bf16[4,7424]{1,0:T(4,128)(2,1)S(1)} collective-permute-done((bf16[4,7424]{1,0:T(4,128)(2,1)S(1)}, bf16[4,7424]{1,0:T(4,128)(2,1)S(1)}, u32[]{:S(2)}, u32[]{:S(2)}) %collective-permute-start.1) | collective-permute-done | bytes 59424 | tf_op jit(solution)/shard_map/ppermute | solution.py:318
  12.3 1.8 %collective-permute-start.2 = (bf16[8,7424]{1,0:T(8,128)(2,1)S(1)}, bf16[8,7424]{1,0:T(8,128)(2,1)S(1)}, u32[]{:S(2)}, u32[]{:S(2)}) collective-permute-start(bf16[8,7424]{1,0:T(8,128)(2,1)S(1)} %shard_map.142.own_ref), channel_id=1, source_target_pairs={{0,1},{1,0},{2,3},{3,2},{4,5},{5,4},{6,7},{7,6},{8,9},{9,8},{10,11... | collective-permute-start | bytes 356360 | tf_op jit(solution)/shard_map/ppermute | solution.py:318
  14.0 3.1 %collective-permute-done.2.got_ref = bf16[8,7424]{1,0:T(8,128)(2,1)S(1)} collective-permute-done((bf16[8,7424]{1,0:T(8,128)(2,1)S(1)}, bf16[8,7424]{1,0:T(8,128)(2,1)S(1)}, u32[]{:S(2)}, u32[]{:S(2)}) %collective-permute-start.2) | collective-permute-done | bytes 118816 | tf_op jit(solution)/shard_map/ppermute | solution.py:318
  17.2 0.1 collective-permute-start.3
  17.3 1.6 %shard_map.147.refs_6_ = bf16[512,2048]{1,0:T(8,128)(2,1)S(1)} custom-call(bf16[7168,2048]{1,0:T(8,128)(2,1)} %refs_7_.1), custom_call_target="tpu_custom_call" | custom-call | bytes 2097152 | tf_op jit(solution)/shard_map/pallas_call | solution.py:305
  18.9 2.9 %shard_map.146.refs_5_ = bf16[1536,2048]{1,0:T(8,128)(2,1)S(1)} custom-call(bf16[7168,2048]{1,0:T(8,128)(2,1)} %refs_7_.1), custom_call_target="tpu_custom_call" | custom-call | bytes 6291456 | tf_op jit(solution)/shard_map/pallas_call | solution.py:305
  21.8 2.9 %shard_map.145.refs_4_ = bf16[1536,2048]{1,0:T(8,128)(2,1)S(1)} custom-call(bf16[7168,2048]{1,0:T(8,128)(2,1)} %refs_7_.1), custom_call_target="tpu_custom_call" | custom-call | bytes 6291456 | tf_op jit(solution)/shard_map/pallas_call | solution.py:305
  24.7 2.9 %shard_map.144.refs_3_ = bf16[1536,2048]{1,0:T(8,128)(2,1)S(1)} custom-call(bf16[7168,2048]{1,0:T(8,128)(2,1)} %refs_7_.1), custom_call_target="tpu_custom_call" | custom-call | bytes 6291456 | tf_op jit(solution)/shard_map/pallas_call | solution.py:305
  27.6 0.0 copy-start
  27.6 0.0 copy-start.1
  27.6 0.0 copy-start.2
  27.6 0.0 copy-start.3
  27.6 0.0 copy-start.4
  27.6 0.0 collective-permute-done.3.refs_2_
  27.6 24.6 %shard_map.148 = (f32[16,7168]{1,0:T(8,128)S(1)}, bf16[16,7168]{1,0:T(8,128)(2,1)S(1)}, bf16[16,16,576]{2,1,0:T(8,128)(2,1)}) custom-call(s32[1]{0:T(128)} %bitcast.me_ref.refs_0_, bf16[16,7424]{1,0:T(8,128)(2,1)S(1)} %shard_map.143.refs_1_, bf16[16,7424]{1,0:T(8,128)(2,1)S(1)} %collective-permute-done.3.refs_2_, bf16[1536,2048]{1,0:T(8,128)(2,1)S(1)} %shard_map.144.refs_3_, ...), custom_call_target="tpu_custom_call" | custom-call | flops 2818572288 | bytes 88080384 | tf_op jit(solution)/shard_map/pallas_call | solution.py:332
  52.2 0.6 collective-permute-start.4
  52.8 6.1 %all-to-all-start = ((bf16[16,16,576]{2,1,0:T(8,128)(2,1)}), bf16[16,16,576]{2,1,0:T(8,128)(2,1)S(1)}, u32[]{:S(2)}, u32[]{:S(2)}) async-start(bf16[16,16,576]{2,1,0:T(8,128)(2,1)} %get-tuple-element.5), calls=%async_computation | async-start | bytes 655360 | tf_op jit(solution)/shard_map/all_to_all | solution.py:367
  58.9 0.0 collective-permute-done.4
  58.9 0.1 add_convert_fusion
  59.0 0.1 reshape.14
  59.1 0.8 %copy.15 = bf16[2,2,2,2,7168]{4,3,0,1,2:T(2,128)(2,1)} copy(bf16[2,2,2,2,7168]{4,3,2,1,0:T(2,128)(2,1)S(1)} %reshape.14) | data formatting | bytes 458752 | tf_op jit(solution)/shard_map/reshape | solution.py:380
  59.9 10.7 %all-to-all-done.page_ref = bf16[16,16,576]{2,1,0:T(8,128)(2,1)S(1)} async-done(((bf16[16,16,576]{2,1,0:T(8,128)(2,1)}), bf16[16,16,576]{2,1,0:T(8,128)(2,1)S(1)}, u32[]{:S(2)}, u32[]{:S(2)}) %all-to-all-start) | async-done | bytes 294944 | tf_op jit(solution)/shard_map/all_to_all | solution.py:367
  70.6 3.4 %all-to-all-start.1 = ((bf16[8,2,7168]{2,1,0:T(2,128)(2,1)}), bf16[8,2,7168]{2,1,0:T(2,128)(2,1)S(1)}, u32[]{:S(2)}, u32[]{:S(2)}) async-start(bf16[8,2,7168]{2,1,0:T(2,128)(2,1)} %bitcast.2), calls=%async_computation.1 | async-start | bytes 458752 | tf_op jit(solution)/shard_map/all_to_all | solution.py:382
  74.1 2.4 %shard_map.149 = bf16[2,64,512]{2,1,0:T(8,128)(2,1)} custom-call(s32[2]{0:T(128)S(1)} %copy-done.2, s32[1,16]{1,0:T(1,128)S(1)} %copy-done.3, bf16[2,64,576]{2,1,0:T(8,128)(2,1)S(1)} %copy-done, bf16[2,64,576]{2,1,0:T(8,128)(2,1)S(1)} %copy-done.1, bf16[16,16,576]{2,1,0:T(8,128)(2,1)S(1)} %all-to-all-done.page_ref), custom_call_target="tpu_custom_call" | custom-call | flops 134217728 | bytes 1048576 | tf_op jit(solution)/shard_map/pallas_call | solution.py:369
  76.5 5.6 %all-to-all-done.1 = bf16[8,2,7168]{2,1,0:T(2,128)(2,1)S(1)} async-done(((bf16[8,2,7168]{2,1,0:T(2,128)(2,1)}), bf16[8,2,7168]{2,1,0:T(2,128)(2,1)S(1)}, u32[]{:S(2)}, u32[]{:S(2)}) %all-to-all-start.1) | async-done | bytes 229408 | tf_op jit(solution)/shard_map/all_to_all | solution.py:382
  82.1 0.2 convert_reduce_fusion
  82.3 0.0 copy-done.4
  82.3 0.6 add_convert_fusion.1
  (7 shorter events, 0.1 us)
Async XLA Ops:
  1.6 6.3 %collective-permute-start = (bf16[2,7424]{1,0:T(2,128)(2,1)S(1)}, bf16[2,7424]{1,0:T(2,128)(2,1)S(1)}, u32[]{:S(2)}, u32[]{:S(2)}) collective-permute-start(bf16[2,7424]{1,0:T(2,128)(2,1)S(1)} %shard_map.140.own_ref), channel_id=1, source_target_pairs={{0,4},{1,5},{2,6},{3,7},{4,0},{5,1},{6,2},{7,3},{8,12},{9,13},{10,... | collective-permute-start | bytes 89096 | tf_op jit(solution)/shard_map/ppermute | solution.py:318
  8.0 4.3 %collective-permute-start.1 = (bf16[4,7424]{1,0:T(4,128)(2,1)S(1)}, bf16[4,7424]{1,0:T(4,128)(2,1)S(1)}, u32[]{:S(2)}, u32[]{:S(2)}) collective-permute-start(bf16[4,7424]{1,0:T(4,128)(2,1)S(1)} %shard_map.141.own_ref), channel_id=1, source_target_pairs={{0,2},{1,3},{2,0},{3,1},{4,6},{5,7},{6,4},{7,5},{8,10},{9,11},{10,... | collective-permute-start | bytes 178184 | tf_op jit(solution)/shard_map/ppermute | solution.py:318
  12.3 4.9 %collective-permute-start.2 = (bf16[8,7424]{1,0:T(8,128)(2,1)S(1)}, bf16[8,7424]{1,0:T(8,128)(2,1)S(1)}, u32[]{:S(2)}, u32[]{:S(2)}) collective-permute-start(bf16[8,7424]{1,0:T(8,128)(2,1)S(1)} %shard_map.142.own_ref), channel_id=1, source_target_pairs={{0,1},{1,0},{2,3},{3,2},{4,5},{5,4},{6,7},{7,6},{8,9},{9,8},{10,11... | collective-permute-start | bytes 356360 | tf_op jit(solution)/shard_map/ppermute | solution.py:318
  17.2 10.4 %collective-permute-start.3 = (bf16[16,7424]{1,0:T(8,128)(2,1)S(1)}, bf16[16,7424]{1,0:T(8,128)(2,1)S(1)}, u32[]{:S(2)}, u32[]{:S(2)}) collective-permute-start(bf16[16,7424]{1,0:T(8,128)(2,1)S(1)} %shard_map.143.refs_1_), channel_id=1, source_target_pairs={{0,8},{8,0},{1,9},{9,1},{2,10},{10,2},{3,11},{11,3},{4,12},{12,4},... | collective-permute-start | bytes 712712 | tf_op jit(solution)/shard_map/ppermute | solution.py:31
  27.6 46.5 %copy-start = (bf16[2,64,576]{2,1,0:T(8,128)(2,1)S(1)}, bf16[2,64,576]{2,1,0:T(8,128)(2,1)}, u32[]{:S(2)}) copy-start(bf16[2,64,576]{2,1,0:T(8,128)(2,1)} %q_ref.1) | copy-start | bytes 442372
  27.6 46.5 %copy-start.1 = (bf16[2,64,576]{2,1,0:T(8,128)(2,1)S(1)}, bf16[2,64,576]{2,1,0:T(8,128)(2,1)}, u32[]{:S(2)}) copy-start(bf16[2,64,576]{2,1,0:T(8,128)(2,1)} %local_ref.1) | copy-start | bytes 442372
  27.6 46.5 %copy-start.2 = (s32[2]{0:T(128)S(1)}, s32[2]{0:T(128)}, u32[]{:S(2)}) copy-start(s32[2]{0:T(128)} %len_ref.1) | copy-start | bytes 28
  27.6 46.5 %copy-start.3 = (s32[1,16]{1,0:T(1,128)S(1)}, s32[1,16]{1,0:T(1,128)}, u32[]{:S(2)}) copy-start(s32[1,16]{1,0:T(1,128)} %owner_ref.1) | copy-start | bytes 196
  27.6 54.7 %copy-start.4 = (bf16[2,7168]{1,0:T(2,128)(2,1)S(1)}, bf16[2,7168]{1,0:T(2,128)(2,1)}, u32[]{:S(2)}) copy-start(bf16[2,7168]{1,0:T(2,128)(2,1)} %hid_ref.1) | copy-start | bytes 86020
  52.2 6.7 %collective-permute-start.4 = (bf16[16,7168]{1,0:T(8,128)(2,1)S(1)}, bf16[16,7168]{1,0:T(8,128)(2,1)S(1)}, u32[]{:S(2)}, u32[]{:S(2)}) collective-permute-start(bf16[16,7168]{1,0:T(8,128)(2,1)S(1)} %get-tuple-element.7), channel_id=1, source_target_pairs={{0,8},{8,0},{1,9},{9,1},{2,10},{10,2},{3,11},{11,3},{4,12},{12,4},... | collective-permute-start | bytes 688136 | tf_op jit(solution)/shard_map/ppermute | solution.py:31
  52.8 17.8 %all-to-all-start = ((bf16[16,16,576]{2,1,0:T(8,128)(2,1)}), bf16[16,16,576]{2,1,0:T(8,128)(2,1)S(1)}, u32[]{:S(2)}, u32[]{:S(2)}) async-start(bf16[16,16,576]{2,1,0:T(8,128)(2,1)} %get-tuple-element.5), calls=%async_computation | async-start | bytes 655360 | tf_op jit(solution)/shard_map/all_to_all | solution.py:367
  70.6 11.5 %all-to-all-start.1 = ((bf16[8,2,7168]{2,1,0:T(2,128)(2,1)}), bf16[8,2,7168]{2,1,0:T(2,128)(2,1)S(1)}, u32[]{:S(2)}, u32[]{:S(2)}) async-start(bf16[8,2,7168]{2,1,0:T(2,128)(2,1)} %bitcast.2), calls=%async_computation.1 | async-start | bytes 458752 | tf_op jit(solution)/shard_map/all_to_all | solution.py:382

commit v3 on v2

--- a/solution.py
+++ b/solution.py
@@ -12,10 +12,10 @@
 EXPERTS = 16
 LANES = 128
 
-LOADS = (3,3,3,1)
-GATE_SLOTS = 3
-UP_SLOTS = 6
-DOWN_SLOTS = 6
+LOADS = (3, 3, 2)
+GATE_SLOTS = 4
+UP_SLOTS = 5
+DOWN_SLOTS = 5
 
 score_scale = 192.0 ** (-0.5)
 norm_eps = 1e-06
@@ -64,19 +64,35 @@
     out_ref[:, width + LANES : width + LANES + count] = ids
 
 
-def merge_kernel(me_ref, own_ref, got_ref, out_ref, *, bit):
-    rows = own_ref.shape[0]
-    upper = (me_ref[0] & bit) != 0
-
-    @pl.when(upper)
-    def _():
-        out_ref[:rows] = got_ref[...]
-        out_ref[rows:] = own_ref[...]
-
-    @pl.when(jnp.logical_not(upper))
-    def _():
-        out_ref[:rows] = own_ref[...]
-        out_ref[rows:] = got_ref[...]
+def bit_groups(size):
+    groups = []
+    top = size.bit_length() - 1
+    while top > 0:
+        length = min(2, top)
+        top -= length
+        groups.append((top, 1 << length))
+    return groups
+
+
+def block_of(index, groups):
+    block = 0
+    for low, members in reversed(groups):
+        block = block * members + ((index >> low) & (members - 1))
+    return block
+
+
+def merge_kernel(me_ref, *refs, low):
+    members = len(refs) - 1
+    out_ref = refs[-1]
+    rows = refs[0].shape[0]
+    mine = (me_ref[0] >> low) & (members - 1)
+    for place in range(members):
+
+        @pl.when(mine == place)
+        def _(place=place):
+            for offset in range(members):
+                at = (place ^ offset) * rows
+                out_ref[at : at + rows] = refs[offset][...]
 
 
 def load_kernel(src_ref, out_ref, sems, *, start):
@@ -92,11 +108,11 @@
         c.wait()
 
 
-def expert_kernel(*refs, tk, tn, base, rows, slices, role_size, loads):
+def expert_kernel(*refs, tk, tn, base, rows, slices, groups, loads):
     me_ref, xa_ref, xb_ref = refs[:3]
     pre_refs = refs[3 : 3 + loads]
-    g_ref, u_ref, d_ref, pool_ref, keep_ref, send_ref, page_ref = refs[3 + loads : 10 + loads]
-    gb, ub, db, ga, ua, h, wsel, vec, ids, semg, semu, semd, semi, semp = refs[10 + loads :]
+    g_ref, u_ref, d_ref, pool_ref, keep_ref, send_ref, near_ref, far_ref = refs[3 + loads : 11 + loads]
+    gb, ub, db, ga, ua, h, wsel, vec, ids, semg, semu, semd, semi, semp = refs[11 + loads :]
     width = d_ref.shape[1]
     n1, n2 = width // tk, width // tn
     ready = sum(r.shape[0] for r in pre_refs) // tk
@@ -117,10 +133,10 @@
         cols = pl.ds(pl.multiple_of(j * tn, tn), tn)
         return pltpu.make_async_copy(d_ref.at[:, cols], db.at[s], semd.at[s])
 
+    for i in range(min(nb, n1)):
+        cu(i).start()
     for i in range(ready, min(ready + ng, n1)):
         cg(i).start()
-    for i in range(min(nb, n1)):
-        cu(i).start()
     cols = vec.shape[1]
     vec[:half] = xa_ref[:, base : base + cols].astype(jnp.float32).astype(jnp.int32)
     vec[half:] = xb_ref[:, base : base + cols].astype(jnp.float32).astype(jnp.int32)
@@ -140,66 +156,57 @@
         at = pl.ds(pl.multiple_of(i * tk, tk), tk)
         return jnp.concatenate([xa_ref[:, at], xb_ref[:, at]], axis=0)
 
+    def up(i, xs):
+        cu(i).wait()
+        ua[...] += jnp.dot(xs, ub[lax.rem(i, nb)], preferred_element_type=jnp.float32)
+
+        @pl.when(i + nb < n1)
+        def _():
+            cu(i + nb).start()
+
+        @pl.when((i + nd >= n1) & (i + nd - n1 < n2))
+        def _():
+            cd(i + nd - n1).start()
+
+    peers = near_ref.shape[0]
+
+    def page_start(d):
+        row = block_of(d, groups) * rows
+        for n, ref in enumerate((near_ref, far_ref)):
+            page = pool_ref.at[ids[row + n * half, me]]
+            pltpu.make_async_copy(page, ref.at[d], semp.at[n]).start()
+
     first = 0
-    for ref in pre_refs:
-        count = ref.shape[0] // tk
+    for n, ref in enumerate(pre_refs):
+        size = ref.shape[0] // tk
 
         def early(i, c, ref=ref, first=first):
             at = pl.ds(pl.multiple_of((i - first) * tk, tk), tk)
-            ga[...] += jnp.dot(rows_of(i), ref[at, :], preferred_element_type=jnp.float32)
+            xs = rows_of(i)
+            ga[...] += jnp.dot(xs, ref[at, :], preferred_element_type=jnp.float32)
+            up(i, xs)
             return c
 
-        lax.fori_loop(first, first + count, early, 0)
-        first += count
-
-    move.wait()
-    count = page_ref.shape[0]
-    peers = count // role_size
-    bits = peers.bit_length() - 1
-    mine = me // peers
-
-    def page_start(d, c):
-        other = d // peers != mine
-        within = lax.rem(d, peers)
-        block = jnp.int32(0)
-        for b in range(bits):
-            block = block * 2 + (lax.shift_right_logical(within, jnp.int32(b)) & 1)
-        row = block * rows + jnp.where(other, half, 0)
-        pltpu.make_async_copy(pool_ref.at[ids[row, me]], page_ref.at[d], semp.at[d]).start()
-        return c
-
-    def page_wait(d, c):
-        pltpu.make_async_copy(pool_ref.at[0], page_ref.at[d], semp.at[d]).wait()
-        return c
-
-    lax.fori_loop(0, count, page_start, 0)
+        lax.fori_loop(first, first + size, early, 0)
+        first += size
+        if n == 0:
+            move.wait()
+            for d in range(peers):
+                page_start(d)
 
     def late(i, c):
         cg(i).wait()
-        ga[...] += jnp.dot(rows_of(i), gb[lax.rem(i - ready, ng)], preferred_element_type=jnp.float32)
+        xs = rows_of(i)
+        ga[...] += jnp.dot(xs, gb[lax.rem(i - ready, ng)], preferred_element_type=jnp.float32)
 
         @pl.when(i + ng < n1)
         def _():
             cg(i + ng).start()
 
+        up(i, xs)
         return c
 
-    def up(i, c):
-        cu(i).wait()
-        ua[...] += jnp.dot(rows_of(i), ub[lax.rem(i, nb)], preferred_element_type=jnp.float32)
-
-        @pl.when(i + nb < n1)
-        def _():
-            cu(i + nb).start()
-
-        @pl.when((i + nd >= n1) & (i + nd - n1 < n2))
-        def _():
-            cd(i + nd - n1).start()
-
-        return c
-
     lax.fori_loop(ready, n1, late, 0)
-    lax.fori_loop(0, n1, up, 0)
     g = ga[...]
     h[...] = ((g / (1.0 + jnp.exp(-g))) * ua[...]).astype(jnp.bfloat16)
 
@@ -218,38 +225,82 @@
         return c
 
     lax.fori_loop(0, n2, down, 0)
-    lax.fori_loop(0, count, page_wait, 0)
-
-
-def attention_kernel(len_ref, owner_ref, q_ref, local_ref, page_ref, out_ref):
+    for n, ref in enumerate((near_ref, far_ref)):
+        pltpu.make_async_copy(ref, ref, semp.at[n]).wait()
+
+
+def fold_kernel(me_ref, *refs, low, members, arrived):
+    own_ref, got_refs = refs[0], refs[1 : 1 + arrived]
+    keep_ref, send_refs = refs[1 + arrived], refs[2 + arrived :]
+    rows = keep_ref.shape[0]
+    mine = (me_ref[0] >> low) & (members - 1)
+
+    def block(place):
+        at = slice(place * rows, (place + 1) * rows)
+        total = own_ref[at]
+        for ref in got_refs:
+            total = total + ref[at].astype(jnp.float32)
+        return total
+
+    for place in range(members):
+
+        @pl.when(mine == place)
+        def _(place=place):
+            for offset in range(1, members):
+                send_refs[offset - 1][...] = block(place ^ offset).astype(jnp.bfloat16)
+            keep_ref[...] = block(place)
+
+
+def stack_kernel(near_ref, far_ref, out_ref):
+    page = near_ref.shape[1]
+    out_ref[:, :page] = near_ref[...]
+    out_ref[:, page:] = far_ref[...]
+
+
+def finish_kernel(me_ref, len_ref, owner_ref, q_ref, local_ref, page_ref, hid_ref, own_ref, *refs):
+    got_refs, out_ref, moe_ref = refs[:-2], refs[-2], refs[-1]
+    total = own_ref[...]
+    for ref in got_refs:
+        total = total + ref[...].astype(jnp.float32)
+    moe_ref[...] = (hid_ref[...].astype(jnp.float32) + total).astype(jnp.bfloat16)
+
     requests, heads, width = q_ref.shape
     value = out_ref.shape[2]
     local_len = local_ref.shape[1]
-    pages, page_len, _ = page_ref.shape
-    paged = page_ref[...].reshape(pages * page_len, width)
-    row = lax.broadcasted_iota(jnp.int32, (pages, pages * page_len), 0)
-    col = lax.broadcasted_iota(jnp.int32, (pages, pages * page_len), 1)
-    inside = (col >= row * page_len) & (col < (row + 1) * page_len)
-    owner = jnp.broadcast_to(jnp.transpose(owner_ref[...].astype(jnp.float32)), inside.shape)
-    key_owner = jnp.sum(jnp.where(inside, owner, 0.0), axis=0, keepdims=True)
+    peers, both, _ = page_ref.shape
+    page_len = both // 2
+    devices = owner_ref.shape[1]
+    role = me_ref[0] // peers
+    keys = page_ref[...].reshape(peers * both, width)
+    holder = lax.broadcasted_iota(jnp.int32, (devices, peers * both), 0)
+    col = lax.broadcasted_iota(jnp.int32, (devices, peers * both), 1)
+    source = col // both
+    far = (col - source * both) // page_len
+    sender = jnp.where(far == 0, role, devices // peers - 1 - role) * peers + source
+    owner = jnp.broadcast_to(jnp.transpose(owner_ref[...].astype(jnp.float32)), holder.shape)
+    key_owner = jnp.sum(jnp.where(holder == sender, owner, 0.0), axis=0, keepdims=True)
     nt = (((1,), (1,)), ((), ()))
+    queries = q_ref[...].reshape(requests * heads, width)
+    s_page = lax.dot_general(queries, keys, nt, preferred_element_type=jnp.float32) * score_scale
+    request = (lax.broadcasted_iota(jnp.int32, s_page.shape, 0) // heads).astype(jnp.float32)
+    s_page = jnp.where(key_owner == request, s_page, -jnp.inf)
+    pos = lax.broadcasted_iota(jnp.int32, (heads, local_len), 1)
+    s_local = []
     for r in range(requests):
-        q = q_ref[r]
-        local = local_ref[r]
-        s_local = lax.dot_general(q, local, nt, preferred_element_type=jnp.float32) * score_scale
-        pos = lax.broadcasted_iota(jnp.int32, (heads, local_len), 1)
-        s_local = jnp.where(pos < len_ref[r], s_local, -jnp.inf)
-        s_page = lax.dot_general(q, paged, nt, preferred_element_type=jnp.float32) * score_scale
-        s_page = jnp.where(key_owner == float(r), s_page, -jnp.inf)
-        peak = jnp.maximum(jnp.max(s_local, axis=1, keepdims=True), jnp.max(s_page, axis=1, keepdims=True))
-        e_local = jnp.exp(s_local - peak)
-        e_page = jnp.exp(s_page - peak)
-        total = jnp.sum(e_local, axis=1, keepdims=True) + jnp.sum(e_page, axis=1, keepdims=True)
-        p_local = (e_local / total).astype(jnp.bfloat16)
-        p_page = (e_page / total).astype(jnp.bfloat16)
-        out = jnp.dot(p_local, local[:, :value], preferred_element_type=jnp.float32)
-        out = out + jnp.dot(p_page, paged[:, :value], preferred_element_type=jnp.float32)
-        out_ref[r] = out.astype(jnp.bfloat16)
+        s = lax.dot_general(q_ref[r], local_ref[r], nt, preferred_element_type=jnp.float32) * score_scale
+        s_local.append(jnp.where(pos < len_ref[r], s, -jnp.inf))
+    s_local = jnp.concatenate(s_local, axis=0)
+    peak = jnp.maximum(jnp.max(s_local, axis=1, keepdims=True), jnp.max(s_page, axis=1, keepdims=True))
+    e_local = jnp.exp(s_local - peak)
+    e_page = jnp.exp(s_page - peak)
+    norm = jnp.sum(e_local, axis=1, keepdims=True) + jnp.sum(e_page, axis=1, keepdims=True)
+    p_local = (e_local / norm).astype(jnp.bfloat16)
+    p_page = (e_page / norm).astype(jnp.bfloat16)
+    paged = jnp.dot(p_page, keys[:, :value], preferred_element_type=jnp.float32)
+    for r in range(requests):
+        at = slice(r * heads, (r + 1) * heads)
+        out = jnp.dot(p_local[at], local_ref[r][:, :value], preferred_element_type=jnp.float32)
+        out_ref[r] = (out + paged[at]).astype(jnp.bfloat16)
 
 
 def tile_of(size, want):
@@ -276,7 +327,7 @@
     total_rows = role_size * half
     tk = tn = tile_of(width, 512)
     weight_bytes = 2 * width * units
-    bits = [dev_size >> (k + 1) for k in range(dev_size.bit_length() - 1)]
+    groups = bit_groups(dev_size)
     weights_in = [pltpu.with_memory_space_constraint(w, pltpu.HBM) for w in (w_gate, w_up, w_down)]
     pool_in = pltpu.with_memory_space_constraint(swap_pool, pltpu.HBM)
     small_in = [
@@ -312,35 +363,39 @@
             cost_estimate=pl.CostEstimate(flops=0, bytes_accessed=2 * size * units, transcendentals=0),
         )(weights_in[0])
 
+    def swap(value, offset):
+        return lax.ppermute(value, "dev", [(i, i ^ offset) for i in range(dev_size)])
+
     loaded = []
     taken = 0
-    for k, bit in enumerate(bits):
-        got = lax.ppermute(held, "dev", [(i, i ^ bit) for i in range(dev_size)])
+    for k, (low, members) in enumerate(groups):
+        got = [swap(held, offset << low) for offset in range(1, members)]
         if k < len(LOADS) - 1:
             loaded.append(load(k, taken))
             taken += LOADS[k] * tk
         held = pl.pallas_call(
-            functools.partial(merge_kernel, bit=bit),
-            out_shape=jax.ShapeDtypeStruct((2 * held.shape[0], packed_width), jnp.bfloat16),
-            in_specs=[SM, VM, VM],
+            functools.partial(merge_kernel, low=low),
+            out_shape=jax.ShapeDtypeStruct((members * held.shape[0], packed_width), jnp.bfloat16),
+            in_specs=[SM] + [VM] * members,
             out_specs=VM,
             compiler_params=pltpu.CompilerParams(vmem_limit_bytes=6 << 20),
-        )(me_arr, held, got)
+        )(me_arr, held, *got)
     other = role_swap(held)
     loaded.append(load(len(LOADS) - 1, taken))
 
-    keep, send, outgoing = pl.pallas_call(
+    keep, send, near, far = pl.pallas_call(
         functools.partial(
             expert_kernel, tk=tk, tn=tn, base=width + LANES, rows=rows, slices=slices,
-            role_size=role_size, loads=len(loaded),
+            groups=groups, loads=len(loaded),
         ),
         out_shape=(
             jax.ShapeDtypeStruct((half, width), jnp.float32),
             jax.ShapeDtypeStruct((half, width), jnp.bfloat16),
-            jax.ShapeDtypeStruct((devices,) + swap_pool.shape[1:], jnp.bfloat16),
+            jax.ShapeDtypeStruct((dev_size,) + swap_pool.shape[1:], jnp.bfloat16),
+            jax.ShapeDtypeStruct((dev_size,) + swap_pool.shape[1:], jnp.bfloat16),
         ),
         in_specs=[SM, VM, VM] + [VM] * len(loaded) + [HBM] * 4,
-        out_specs=(VM, VM, VM),
+        out_specs=(VM, VM, VM, VM),
         scratch_shapes=[
             pltpu.VMEM((GATE_SLOTS, tk, units), jnp.bfloat16),
             pltpu.VMEM((UP_SLOTS, tk, units), jnp.bfloat16),
@@ -355,33 +410,49 @@
             pltpu.SemaphoreType.DMA((UP_SLOTS,)),
             pltpu.SemaphoreType.DMA((DOWN_SLOTS,)),
             pltpu.SemaphoreType.DMA,
-            pltpu.SemaphoreType.DMA((devices,)),
+            pltpu.SemaphoreType.DMA((2,)),
         ],
-        compiler_params=pltpu.CompilerParams(vmem_limit_bytes=32 << 20),
+        compiler_params=pltpu.CompilerParams(vmem_limit_bytes=31 << 20),
         cost_estimate=pl.CostEstimate(
             flops=6 * total_rows * width * units, bytes_accessed=3 * weight_bytes, transcendentals=0
         ),
     )(me_arr, held, other, *loaded, *weights_in, pool_in)
 
-    crossed = role_swap(send)
-    arrived = lax.all_to_all(outgoing, ("role", "dev"), split_axis=0, concat_axis=0, tiled=True)
-
-    attn_out = pl.pallas_call(
-        attention_kernel,
-        out_shape=jax.ShapeDtypeStruct(queries.shape[:2] + (queries.shape[2] - ROPE,), jnp.bfloat16),
-        in_specs=[SM, VM, VM, VM, VM],
+    far = role_swap(far)
+    page_shape = (dev_size, 2 * swap_pool.shape[1], swap_pool.shape[2])
+    outgoing = pl.pallas_call(
+        stack_kernel,
+        out_shape=jax.ShapeDtypeStruct(page_shape, jnp.bfloat16),
+        in_specs=[VM, VM],
         out_specs=VM,
-        compiler_params=pltpu.CompilerParams(vmem_limit_bytes=20 << 20),
-        cost_estimate=pl.CostEstimate(flops=1 << 27, bytes_accessed=1 << 20, transcendentals=1 << 16),
-    )(cache_lengths, page_owner, queries, local_cache, arrived)
-
-    total = (keep + crossed.astype(jnp.float32)).astype(jnp.bfloat16)
-    count = len(bits)
-    total = total.reshape((2,) * count + (rows, width))
-    total = total.transpose(tuple(range(count - 1, -1, -1)) + (count, count + 1)).reshape(dev_size, rows, width)
-    parts = lax.all_to_all(total, "dev", split_axis=0, concat_axis=0, tiled=True)
-    total = jnp.sum(parts.astype(jnp.float32), axis=0)
-    moe_out = (hidden.astype(jnp.float32) + total).astype(jnp.bfloat16)
+        compiler_params=pltpu.CompilerParams(vmem_limit_bytes=8 << 20),
+    )(near, far)
+    arrived = lax.all_to_all(outgoing, "dev", split_axis=0, concat_axis=0, tiled=True)
+
+    got = [role_swap(send)]
+    own = keep
+    for low, members in reversed(groups):
+        count = own.shape[0] // members
+        own, *sends = pl.pallas_call(
+            functools.partial(fold_kernel, low=low, members=members, arrived=len(got)),
+            out_shape=[jax.ShapeDtypeStruct((count, width), jnp.float32)]
+            + [jax.ShapeDtypeStruct((count, width), jnp.bfloat16)] * (members - 1),
+            in_specs=[SM] + [VM] * (1 + len(got)),
+            out_specs=[VM] * members,
+            compiler_params=pltpu.CompilerParams(vmem_limit_bytes=16 << 20),
+        )(me_arr, own, *got)
+        got = [swap(value, (n + 1) << low) for n, value in enumerate(sends)]
+    operands = (me_arr, cache_lengths, page_owner, queries, local_cache, arrived, hidden, own, *got)
+    attn_out, moe_out = pl.pallas_call(
+        finish_kernel,
+        out_shape=(
+            jax.ShapeDtypeStruct(queries.shape[:2] + (queries.shape[2] - ROPE,), jnp.bfloat16),
+            jax.ShapeDtypeStruct(hidden.shape, jnp.bfloat16),
+        ),
+        in_specs=[SM] * 2 + [VM] * (len(operands) - 2),
+        out_specs=(VM, VM),
+        compiler_params=pltpu.CompilerParams(vmem_limit_bytes=24 << 20),
+    )(*operands)
     return (attn_out, moe_out)
 
 

time: 83.4 us -> 75.7 us (0.908)
  waiting for transfers between devices: 24.2 us -> 20.2 us
  Pallas kernels: 38.3 us -> 35.3 us
  starting transfers between devices: 17.7 us -> 19.2 us
  local copies, waits for them, and re-layouts: 0.97 us -> 0.03 us
  other arithmetic: 0.89 us -> 0 us
    all_to_all x2 -> x1, waiting for transfers between devices: 16.3 us -> 0.01 us  [per_device(): lax.all_to_all(outgoing, 'dev', split_axis=0, concat_axis=0, tiled=True)]
    ppermute x3 -> x8, waiting for transfers between devices: 7.93 us -> 17.7 us  [swap(): lax.ppermute(value, 'dev', [(i, i ^ offset) for i in range(dev_size)])]
    ppermute x3 -> x8, starting transfers between devices: 7.55 us -> 14.2 us  [swap(): lax.ppermute(value, 'dev', [(i, i ^ offset) for i in range(dev_size)])]
    all_to_all x2 -> x1, starting transfers between devices: 9.54 us -> 4.21 us  [per_device(): lax.all_to_all(outgoing, 'dev', split_axis=0, concat_axis=0, tiled=True)]
    ppermute x2 -> x3, waiting for transfers between devices: 0.01 us -> 2.43 us  [role_swap(): return lax.ppermute(x, 'role', [(i, size - 1 - i) for i in range(size)])]
    pallas_call x4 -> x3, Pallas kernels: 10.3 us -> 8.02 us  [load(): pl.pallas_call(functools.partial(load_kernel, start=start), out_shape=plt...]
    pallas_call x1, Pallas kernels: 24.6 us -> 23.3 us  [per_device(): pl.pallas_call(functools.partial(expert_kernel, tk=tk, tn=tn, base=width...]
    reshape x2 -> x0, local copies, waits for them, and re-layouts: 0.94 us -> none  [per_device(): total = total.reshape((2,) * count + (rows, width))]
  transfers between devices with their start and end apart: 7 -> 12, of which waited for: 5 -> 8; matrix products, arithmetic and copies ran while one was open for 1% -> 0% of each run, Pallas kernels for 15% -> 11%
where the time goes in v3:
time: 75.7 us; the launch traced here: 75.4 us
  Pallas kernels  35.3 us (47%)
  waiting for transfers between devices  20.2 us (27%)
  starting transfers between devices  19.2 us (25%)
  between operations  0.8 us (1%)
    pallas_call x1, Pallas kernels, per_device(): pl.pallas_call(functools.partial(expert_kernel, tk=tk, tn=tn, base=width...  23.3 us
    ppermute x8, waiting for transfers between devices, swap(): lax.ppermute(value, 'dev', [(i, i ^ offset) for i in range(dev_size)])  17.7 us
    ppermute x8, starting transfers between devices, swap(): lax.ppermute(value, 'dev', [(i, i ^ offset) for i in range(dev_size)])  14.2 us
    pallas_call x3, Pallas kernels, load(): pl.pallas_call(functools.partial(load_kernel, start=start), out_shape=plt...  8.02 us
    all_to_all x1, starting transfers between devices, per_device(): lax.all_to_all(outgoing, 'dev', split_axis=0, concat_axis=0, tiled=True)  4.21 us
    ppermute x3, waiting for transfers between devices, role_swap(): return lax.ppermute(x, 'role', [(i, size - 1 - i) for i in range(size)])  2.43 us
    pallas_call x1, Pallas kernels, per_device(): pl.pallas_call(finish_kernel, out_shape=(jax.ShapeDtypeStruct(queries.sha...  1.9 us
  transfers between devices with their start and end apart: 12, of which 8 were waited for; matrix products, arithmetic and copies ran while one was open for 0% of the time, Pallas kernels for 11%

profile of v3, /device:TPU:0, one launch (start us, length us, event | category | flops | bytes accessed | tf_op | source)
XLA Modules:
  0.0 75.4 jit_solution(2932789059002847397)
XLA Ops:
  0.6 1.0 %shard_map.140.refs_0_ = bf16[2,7424]{1,0:T(2,128)(2,1)S(1)} custom-call(s32[1]{0:T(128)} %bitcast.me_ref.refs_0_, bf16[2,7168]{1,0:T(2,128)(2,1)} %hid_ref.3, bf16[7168]{0:T(1024)(128)(2,1)} %gain_ref.1, s32[2,8]{1,0:T(2,128)} %routes_ref.1, f32[2,8]{1,0:T(2,128)} %weights_ref.1, s32[1,16]{1,0:T(1,128)} %ids_ref.1), custom_call_target="tpu_custom_call" | custom-call | tf_op jit(solution)/shard_map/pallas_call | solution.py:338
  1.6 5.1 %collective-permute-start.2 = (bf16[2,7424]{1,0:T(2,128)(2,1)S(1)}, bf16[2,7424]{1,0:T(2,128)(2,1)S(1)}, u32[]{:S(2)}, u32[]{:S(2)}) collective-permute-start(bf16[2,7424]{1,0:T(2,128)(2,1)S(1)} %shard_map.140.refs_0_), channel_id=1, source_target_pairs={{0,6},{1,7},{2,4},{3,5},{4,2},{5,3},{6,0},{7,1},{8,14},{9,15},{10,... | collective-permute-start | bytes 89096 | tf_op jit(solution)/shard_map/ppermute | solution.py:367
  6.8 0.6 collective-permute-start
  7.4 1.2 %collective-permute-done.2.refs_3_ = bf16[2,7424]{1,0:T(2,128)(2,1)S(1)} collective-permute-done((bf16[2,7424]{1,0:T(2,128)(2,1)S(1)}, bf16[2,7424]{1,0:T(2,128)(2,1)S(1)}, u32[]{:S(2)}, u32[]{:S(2)}) %collective-permute-start.2) | collective-permute-done | bytes 29728 | tf_op jit(solution)/shard_map/ppermute | solution.py:367
  8.6 2.9 %collective-permute-done.1.refs_2_ = bf16[2,7424]{1,0:T(2,128)(2,1)S(1)} collective-permute-done((bf16[2,7424]{1,0:T(2,128)(2,1)S(1)}, bf16[2,7424]{1,0:T(2,128)(2,1)S(1)}, u32[]{:S(2)}, u32[]{:S(2)}) %collective-permute-start.1) | collective-permute-done | bytes 29728 | tf_op jit(solution)/shard_map/ppermute | solution.py:367
  11.6 0.1 shard_map.141.refs_0_
  11.6 1.6 %collective-permute-start.3 = (bf16[8,7424]{1,0:T(8,128)(2,1)S(1)}, bf16[8,7424]{1,0:T(8,128)(2,1)S(1)}, u32[]{:S(2)}, u32[]{:S(2)}) collective-permute-start(bf16[8,7424]{1,0:T(8,128)(2,1)S(1)} %shard_map.141.refs_0_), channel_id=1, source_target_pairs={{0,1},{1,0},{2,3},{3,2},{4,5},{5,4},{6,7},{7,6},{8,9},{9,8},{10,11... | collective-permute-start | bytes 356360 | tf_op jit(solution)/shard_map/ppermute | solution.py:367
  13.2 3.3 %collective-permute-done.3.refs_1_ = bf16[8,7424]{1,0:T(8,128)(2,1)S(1)} collective-permute-done((bf16[8,7424]{1,0:T(8,128)(2,1)S(1)}, bf16[8,7424]{1,0:T(8,128)(2,1)S(1)}, u32[]{:S(2)}, u32[]{:S(2)}) %collective-permute-start.3) | collective-permute-done | bytes 118816 | tf_op jit(solution)/shard_map/ppermute | solution.py:367
  16.6 0.1 collective-permute-start.4
  16.6 2.2 %shard_map.145.refs_5_ = bf16[1024,2048]{1,0:T(8,128)(2,1)S(1)} custom-call(bf16[7168,2048]{1,0:T(8,128)(2,1)} %refs_6_.1), custom_call_target="tpu_custom_call" | custom-call | bytes 4194304 | tf_op jit(solution)/shard_map/pallas_call | solution.py:356
  18.9 2.9 %shard_map.144.refs_4_ = bf16[1536,2048]{1,0:T(8,128)(2,1)S(1)} custom-call(bf16[7168,2048]{1,0:T(8,128)(2,1)} %refs_6_.1), custom_call_target="tpu_custom_call" | custom-call | bytes 6291456 | tf_op jit(solution)/shard_map/pallas_call | solution.py:356
  21.8 2.9 %shard_map.143.refs_3_ = bf16[1536,2048]{1,0:T(8,128)(2,1)S(1)} custom-call(bf16[7168,2048]{1,0:T(8,128)(2,1)} %refs_6_.1), custom_call_target="tpu_custom_call" | custom-call | bytes 6291456 | tf_op jit(solution)/shard_map/pallas_call | solution.py:356
  24.7 0.0 copy-start
  24.7 0.0 copy-start.1
  24.7 0.0 copy-start.3
  24.7 0.0 copy-start.4
  24.8 23.3 %shard_map.146 = (f32[16,7168]{1,0:T(8,128)S(1)}, bf16[16,7168]{1,0:T(8,128)(2,1)S(1)}, bf16[8,16,576]{2,1,0:T(8,128)(2,1)S(1)}, bf16[8,16,576]{2,1,0:T(8,128)(2,1)S(1)}) custom-call(s32[1]{0:T(128)} %bitcast.me_ref.refs_0_, bf16[16,7424]{1,0:T(8,128)(2,1)S(1)} %shard_map.142.refs_1_, bf16[16,7424]{1,0:T(8,128)(2,1)S(1)} %collective-permute-done.4.refs_2_, ...), custom_call_target="tpu_custom_call" | custom-call | flops 2818572288 | bytes 88080384 | tf_op jit(solution)/shard_map/pallas_call | solution.py:386
  48.1 0.6 collective-permute-start.5
  48.6 1.0 %collective-permute-done.5.far_ref = bf16[8,16,576]{2,1,0:T(8,128)(2,1)S(1)} collective-permute-done((bf16[8,16,576]{2,1,0:T(8,128)(2,1)S(1)}, bf16[8,16,576]{2,1,0:T(8,128)(2,1)S(1)}, u32[]{:S(2)}, u32[]{:S(2)}) %collective-permute-start.5) | collective-permute-done | bytes 147488 | tf_op jit(solution)/shard_map/ppermute | solution.py:31
  49.7 0.8 %shard_map.147 = bf16[8,32,576]{2,1,0:T(8,128)(2,1)} custom-call(bf16[8,16,576]{2,1,0:T(8,128)(2,1)S(1)} %get-tuple-element.12.near_ref, bf16[8,16,576]{2,1,0:T(8,128)(2,1)S(1)} %collective-permute-done.5.far_ref), custom_call_target="tpu_custom_call" | custom-call | tf_op jit(solution)/shard_map/pallas_call | solution.py:423
  50.4 4.2 %all-to-all-start = ((bf16[8,32,576]{2,1,0:T(8,128)(2,1)}), bf16[8,32,576]{2,1,0:T(8,128)(2,1)S(1)}, u32[]{:S(2)}, u32[]{:S(2)}) async-start(bf16[8,32,576]{2,1,0:T(8,128)(2,1)} %shard_map.147), calls=%async_computation | async-start | bytes 655360 | tf_op jit(solution)/shard_map/all_to_all | solution.py:430
  54.7 0.1 collective-permute-start.6
  54.7 1.4 %collective-permute-done.6.refs_1_ = bf16[16,7168]{1,0:T(8,128)(2,1)S(1)} collective-permute-done((bf16[16,7168]{1,0:T(8,128)(2,1)S(1)}, bf16[16,7168]{1,0:T(8,128)(2,1)S(1)}, u32[]{:S(2)}, u32[]{:S(2)}) %collective-permute-start.6) | collective-permute-done | bytes 229408 | tf_op jit(solution)/shard_map/ppermute | solution.py:31
  56.2 2.1 %collective-permute-start.7 = (bf16[8,7168]{1,0:T(8,128)(2,1)S(1)}, bf16[8,7168]{1,0:T(8,128)(2,1)S(1)}, u32[]{:S(2)}, u32[]{:S(2)}) collective-permute-start(bf16[8,7168]{1,0:T(8,128)(2,1)S(1)} %get-tuple-element.17), channel_id=1, source_target_pairs={{0,1},{1,0},{2,3},{3,2},{4,5},{5,4},{6,7},{7,6},{8,9},{9,8},{10,11... | collective-permute-start | bytes 344072 | tf_op jit(solution)/shard_map/ppermute | solution.py:367
  58.3 4.9 %collective-permute-done.7.refs_1_ = bf16[8,7168]{1,0:T(8,128)(2,1)S(1)} collective-permute-done((bf16[8,7168]{1,0:T(8,128)(2,1)S(1)}, bf16[8,7168]{1,0:T(8,128)(2,1)S(1)}, u32[]{:S(2)}, u32[]{:S(2)}) %collective-permute-start.7) | collective-permute-done | bytes 114720 | tf_op jit(solution)/shard_map/ppermute | solution.py:367
  63.2 0.1 shard_map.149
  63.3 2.4 %collective-permute-start.8 = (bf16[2,7168]{1,0:T(2,128)(2,1)S(1)}, bf16[2,7168]{1,0:T(2,128)(2,1)S(1)}, u32[]{:S(2)}, u32[]{:S(2)}) collective-permute-start(bf16[2,7168]{1,0:T(2,128)(2,1)S(1)} %get-tuple-element.19), channel_id=1, source_target_pairs={{0,2},{1,3},{2,0},{3,1},{4,6},{5,7},{6,4},{7,5},{8,10},{9,11},{10,... | collective-permute-start | bytes 86024 | tf_op jit(solution)/shard_map/ppermute | solution.py:367
  65.7 2.1 %collective-permute-start.9 = (bf16[2,7168]{1,0:T(2,128)(2,1)S(1)}, bf16[2,7168]{1,0:T(2,128)(2,1)S(1)}, u32[]{:S(2)}, u32[]{:S(2)}) collective-permute-start(bf16[2,7168]{1,0:T(2,128)(2,1)S(1)} %get-tuple-element.20), channel_id=1, source_target_pairs={{0,4},{1,5},{2,6},{3,7},{4,0},{5,1},{6,2},{7,3},{8,12},{9,13},{10,... | collective-permute-start | bytes 86024 | tf_op jit(solution)/shard_map/ppermute | solution.py:367
  67.8 0.3 collective-permute-start.10
  68.2 2.3 %collective-permute-done.9.refs_1_ = bf16[2,7168]{1,0:T(2,128)(2,1)S(1)} collective-permute-done((bf16[2,7168]{1,0:T(2,128)(2,1)S(1)}, bf16[2,7168]{1,0:T(2,128)(2,1)S(1)}, u32[]{:S(2)}, u32[]{:S(2)}) %collective-permute-start.9) | collective-permute-done | bytes 28704 | tf_op jit(solution)/shard_map/ppermute | solution.py:367
  70.5 3.0 %collective-permute-done.10.refs_2_ = bf16[2,7168]{1,0:T(2,128)(2,1)S(1)} collective-permute-done((bf16[2,7168]{1,0:T(2,128)(2,1)S(1)}, bf16[2,7168]{1,0:T(2,128)(2,1)S(1)}, u32[]{:S(2)}, u32[]{:S(2)}) %collective-permute-start.10) | collective-permute-done | bytes 28704 | tf_op jit(solution)/shard_map/ppermute | solution.py:367
  73.5 1.9 %shard_map.150 = (bf16[2,64,512]{2,1,0:T(8,128)(2,1)}, bf16[2,7168]{1,0:T(2,128)(2,1)}) custom-call(s32[1]{0:T(128)} %bitcast.me_ref.refs_0_, s32[2]{0:T(128)S(1)} %copy-done.3, s32[1,16]{1,0:T(1,128)S(1)} %copy-done.4, bf16[2,64,576]{2,1,0:T(8,128)(2,1)S(1)} %copy-done, bf16[2,64,576]{2,1,0:T(8,128)(2,1)S(1)} %copy-done.1, ...), custom_call_target="tpu_custom_call" | custom-call | tf_op jit(solution)/shard_map/pallas_call | solution.py:446
  (13 shorter events, 0.1 us)
Async XLA Ops:
  1.6 7.0 %collective-permute-start.2 = (bf16[2,7424]{1,0:T(2,128)(2,1)S(1)}, bf16[2,7424]{1,0:T(2,128)(2,1)S(1)}, u32[]{:S(2)}, u32[]{:S(2)}) collective-permute-start(bf16[2,7424]{1,0:T(2,128)(2,1)S(1)} %shard_map.140.refs_0_), channel_id=1, source_target_pairs={{0,6},{1,7},{2,4},{3,5},{4,2},{5,3},{6,0},{7,1},{8,14},{9,15},{10,... | collective-permute-start | bytes 89096 | tf_op jit(solution)/shard_map/ppermute | solution.py:367
  6.8 4.8 %collective-permute-start.1 = (bf16[2,7424]{1,0:T(2,128)(2,1)S(1)}, bf16[2,7424]{1,0:T(2,128)(2,1)S(1)}, u32[]{:S(2)}, u32[]{:S(2)}) collective-permute-start(bf16[2,7424]{1,0:T(2,128)(2,1)S(1)} %shard_map.140.refs_0_), channel_id=1, source_target_pairs={{0,4},{1,5},{2,6},{3,7},{4,0},{5,1},{6,2},{7,3},{8,12},{9,13},{10,... | collective-permute-start | bytes 89096 | tf_op jit(solution)/shard_map/ppermute | solution.py:367
  6.8 4.8 %collective-permute-start = (bf16[2,7424]{1,0:T(2,128)(2,1)S(1)}, bf16[2,7424]{1,0:T(2,128)(2,1)S(1)}, u32[]{:S(2)}, u32[]{:S(2)}) collective-permute-start(bf16[2,7424]{1,0:T(2,128)(2,1)S(1)} %shard_map.140.refs_0_), channel_id=1, source_target_pairs={{0,2},{1,3},{2,0},{3,1},{4,6},{5,7},{6,4},{7,5},{8,10},{9,11},{10,... | collective-permute-start | bytes 89096 | tf_op jit(solution)/shard_map/ppermute | solution.py:367
  11.6 4.9 %collective-permute-start.3 = (bf16[8,7424]{1,0:T(8,128)(2,1)S(1)}, bf16[8,7424]{1,0:T(8,128)(2,1)S(1)}, u32[]{:S(2)}, u32[]{:S(2)}) collective-permute-start(bf16[8,7424]{1,0:T(8,128)(2,1)S(1)} %shard_map.141.refs_0_), channel_id=1, source_target_pairs={{0,1},{1,0},{2,3},{3,2},{4,5},{5,4},{6,7},{7,6},{8,9},{9,8},{10,11... | collective-permute-start | bytes 356360 | tf_op jit(solution)/shard_map/ppermute | solution.py:367
  16.6 8.2 %collective-permute-start.4 = (bf16[16,7424]{1,0:T(8,128)(2,1)S(1)}, bf16[16,7424]{1,0:T(8,128)(2,1)S(1)}, u32[]{:S(2)}, u32[]{:S(2)}) collective-permute-start(bf16[16,7424]{1,0:T(8,128)(2,1)S(1)} %shard_map.142.refs_1_), channel_id=1, source_target_pairs={{0,8},{8,0},{1,9},{9,1},{2,10},{10,2},{3,11},{11,3},{4,12},{12,4},... | collective-permute-start | bytes 712712 | tf_op jit(solution)/shard_map/ppermute | solution.py:31
  24.7 48.8 %copy-start = (bf16[2,64,576]{2,1,0:T(8,128)(2,1)S(1)}, bf16[2,64,576]{2,1,0:T(8,128)(2,1)}, u32[]{:S(2)}) copy-start(bf16[2,64,576]{2,1,0:T(8,128)(2,1)} %q_ref.1) | copy-start | bytes 442372
  24.7 48.8 %copy-start.1 = (bf16[2,64,576]{2,1,0:T(8,128)(2,1)S(1)}, bf16[2,64,576]{2,1,0:T(8,128)(2,1)}, u32[]{:S(2)}) copy-start(bf16[2,64,576]{2,1,0:T(8,128)(2,1)} %local_ref.1) | copy-start | bytes 442372
  24.7 48.8 %copy-start.2 = (bf16[2,7168]{1,0:T(2,128)(2,1)S(1)}, bf16[2,7168]{1,0:T(2,128)(2,1)}, u32[]{:S(2)}) copy-start(bf16[2,7168]{1,0:T(2,128)(2,1)} %hid_ref.3) | copy-start | bytes 86020
  24.7 48.8 %copy-start.3 = (s32[2]{0:T(128)S(1)}, s32[2]{0:T(128)}, u32[]{:S(2)}) copy-start(s32[2]{0:T(128)} %len_ref.1) | copy-start | bytes 28
  24.7 48.8 %copy-start.4 = (s32[1,16]{1,0:T(1,128)S(1)}, s32[1,16]{1,0:T(1,128)}, u32[]{:S(2)}) copy-start(s32[1,16]{1,0:T(1,128)} %owner_ref.1) | copy-start | bytes 196
  48.1 1.6 %collective-permute-start.5 = (bf16[8,16,576]{2,1,0:T(8,128)(2,1)S(1)}, bf16[8,16,576]{2,1,0:T(8,128)(2,1)S(1)}, u32[]{:S(2)}, u32[]{:S(2)}) collective-permute-start(bf16[8,16,576]{2,1,0:T(8,128)(2,1)S(1)} %get-tuple-element.13), channel_id=1, source_target_pairs={{0,8},{8,0},{1,9},{9,1},{2,10},{10,2},{3,11},{11,3},{4,12},{12,4},... | collective-permute-start | bytes 442376 | tf_op jit(solution)/shard_map/ppermute | solution.py:31
  50.4 23.0 %all-to-all-start = ((bf16[8,32,576]{2,1,0:T(8,128)(2,1)}), bf16[8,32,576]{2,1,0:T(8,128)(2,1)S(1)}, u32[]{:S(2)}, u32[]{:S(2)}) async-start(bf16[8,32,576]{2,1,0:T(8,128)(2,1)} %shard_map.147), calls=%async_computation | async-start | bytes 655360 | tf_op jit(solution)/shard_map/all_to_all | solution.py:430
  54.7 1.5 %collective-permute-start.6 = (bf16[16,7168]{1,0:T(8,128)(2,1)S(1)}, bf16[16,7168]{1,0:T(8,128)(2,1)S(1)}, u32[]{:S(2)}, u32[]{:S(2)}) collective-permute-start(bf16[16,7168]{1,0:T(8,128)(2,1)S(1)} %get-tuple-element.15), channel_id=1, source_target_pairs={{0,8},{8,0},{1,9},{9,1},{2,10},{10,2},{3,11},{11,3},{4,12},{12,4},... | collective-permute-start | bytes 688136 | tf_op jit(solution)/shard_map/ppermute | solution.py:31
  56.2 7.0 %collective-permute-start.7 = (bf16[8,7168]{1,0:T(8,128)(2,1)S(1)}, bf16[8,7168]{1,0:T(8,128)(2,1)S(1)}, u32[]{:S(2)}, u32[]{:S(2)}) collective-permute-start(bf16[8,7168]{1,0:T(8,128)(2,1)S(1)} %get-tuple-element.17), channel_id=1, source_target_pairs={{0,1},{1,0},{2,3},{3,2},{4,5},{5,4},{6,7},{7,6},{8,9},{9,8},{10,11... | collective-permute-start | bytes 344072 | tf_op jit(solution)/shard_map/ppermute | solution.py:367
  63.3 4.8 %collective-permute-start.8 = (bf16[2,7168]{1,0:T(2,128)(2,1)S(1)}, bf16[2,7168]{1,0:T(2,128)(2,1)S(1)}, u32[]{:S(2)}, u32[]{:S(2)}) collective-permute-start(bf16[2,7168]{1,0:T(2,128)(2,1)S(1)} %get-tuple-element.19), channel_id=1, source_target_pairs={{0,2},{1,3},{2,0},{3,1},{4,6},{5,7},{6,4},{7,5},{8,10},{9,11},{10,... | collective-permute-start | bytes 86024 | tf_op jit(solution)/shard_map/ppermute | solution.py:367
  65.7 4.8 %collective-permute-start.9 = (bf16[2,7168]{1,0:T(2,128)(2,1)S(1)}, bf16[2,7168]{1,0:T(2,128)(2,1)S(1)}, u32[]{:S(2)}, u32[]{:S(2)}) collective-permute-start(bf16[2,7168]{1,0:T(2,128)(2,1)S(1)} %get-tuple-element.20), channel_id=1, source_target_pairs={{0,4},{1,5},{2,6},{3,7},{4,0},{5,1},{6,2},{7,3},{8,12},{9,13},{10,... | collective-permute-start | bytes 86024 | tf_op jit(solution)/shard_map/ppermute | solution.py:367
  67.8 5.7 %collective-permute-start.10 = (bf16[2,7168]{1,0:T(2,128)(2,1)S(1)}, bf16[2,7168]{1,0:T(2,128)(2,1)S(1)}, u32[]{:S(2)}, u32[]{:S(2)}) collective-permute-start(bf16[2,7168]{1,0:T(2,128)(2,1)S(1)} %get-tuple-element.21), channel_id=1, source_target_pairs={{0,6},{1,7},{2,4},{3,5},{4,2},{5,3},{6,0},{7,1},{8,14},{9,15},{10,... | collective-permute-start | bytes 86024 | tf_op jit(solution)/shard_map/ppermute | solution.py:367

commit v4 on v3

--- a/solution.py
+++ b/solution.py
@@ -12,10 +12,11 @@
 EXPERTS = 16
 LANES = 128
 
-LOADS = (3, 3, 2)
-GATE_SLOTS = 4
-UP_SLOTS = 5
-DOWN_SLOTS = 5
+LOADS = (2, 2)
+LEAD = 2
+GATE_SLOTS = 2
+UP_SLOTS = 3
+DOWN_SLOTS = 6
 
 score_scale = 192.0 ** (-0.5)
 norm_eps = 1e-06
@@ -61,6 +62,7 @@
     ids = jnp.broadcast_to(ids_v[...].astype(jnp.float32), (rows, count)).astype(jnp.bfloat16)
     out_ref[:, :width] = normed
     out_ref[:, width : width + LANES] = tail
+    out_ref[:, width + LANES :] = jnp.zeros((rows, out_ref.shape[1] - width - LANES), jnp.bfloat16)
     out_ref[:, width + LANES : width + LANES + count] = ids
 
 
@@ -108,14 +110,21 @@
         c.wait()
 
 
-def expert_kernel(*refs, tk, tn, base, rows, slices, groups, loads):
+def rows_of(xa_ref, xb_ref, i, tk):
+    at = pl.ds(pl.multiple_of(i * tk, tk), tk)
+    return jnp.concatenate([xa_ref[:, at], xb_ref[:, at]], axis=0)
+
+
+def expert_kernel(*refs, tk, tn, base, rows, slices, groups, loads, parts):
     me_ref, xa_ref, xb_ref = refs[:3]
     pre_refs = refs[3 : 3 + loads]
-    g_ref, u_ref, d_ref, pool_ref, keep_ref, send_ref, near_ref, far_ref = refs[3 + loads : 11 + loads]
-    gb, ub, db, ga, ua, h, wsel, vec, ids, semg, semu, semd, semi, semp = refs[11 + loads :]
+    g_ref, u_ref, d_ref, pool_ref, keep_ref = refs[3 + loads : 8 + loads]
+    send_refs = refs[8 + loads : 7 + loads + parts]
+    near_ref, far_ref, gb, ub, db, ga, ua, h, wsel, vec, ids, semg, semu, semd, semi, semp = refs[7 + loads + parts :]
     width = d_ref.shape[1]
     n1, n2 = width // tk, width // tn
     ready = sum(r.shape[0] for r in pre_refs) // tk
+    lead = min(LEAD, ready)
     nb, nd, ng = ub.shape[0], db.shape[0], gb.shape[0]
     half = xa_ref.shape[0]
     me = me_ref[0]
@@ -152,22 +161,6 @@
         tail = ref[:, width : width + LANES].astype(jnp.float32)
         wsel[i * half : (i + 1) * half] = jnp.sum(jnp.where(chosen, tail, 0.0), axis=1, keepdims=True)
 
-    def rows_of(i):
-        at = pl.ds(pl.multiple_of(i * tk, tk), tk)
-        return jnp.concatenate([xa_ref[:, at], xb_ref[:, at]], axis=0)
-
-    def up(i, xs):
-        cu(i).wait()
-        ua[...] += jnp.dot(xs, ub[lax.rem(i, nb)], preferred_element_type=jnp.float32)
-
-        @pl.when(i + nb < n1)
-        def _():
-            cu(i + nb).start()
-
-        @pl.when((i + nd >= n1) & (i + nd - n1 < n2))
-        def _():
-            cd(i + nd - n1).start()
-
     peers = near_ref.shape[0]
 
     def page_start(d):
@@ -176,47 +169,72 @@
             page = pool_ref.at[ids[row + n * half, me]]
             pltpu.make_async_copy(page, ref.at[d], semp.at[n]).start()
 
-    first = 0
-    for n, ref in enumerate(pre_refs):
-        size = ref.shape[0] // tk
-
-        def early(i, c, ref=ref, first=first):
-            at = pl.ds(pl.multiple_of((i - first) * tk, tk), tk)
-            xs = rows_of(i)
-            ga[...] += jnp.dot(xs, ref[at, :], preferred_element_type=jnp.float32)
-            up(i, xs)
-            return c
-
-        lax.fori_loop(first, first + size, early, 0)
-        first += size
-        if n == 0:
-            move.wait()
-            for d in range(peers):
-                page_start(d)
+    def gate(i, weights):
+        ga[...] += jnp.dot(rows_of(xa_ref, xb_ref, i, tk), weights, preferred_element_type=jnp.float32)
+
+    def up(i):
+        cu(i).wait()
+        xs = rows_of(xa_ref, xb_ref, i, tk)
+        ua[...] += jnp.dot(xs, ub[lax.rem(i, nb)], preferred_element_type=jnp.float32)
+
+        @pl.when(i + nb < n1)
+        def _():
+            cu(i + nb).start()
+
+        @pl.when((i + nd >= n1) & (i + nd - n1 < n2))
+        def _():
+            cd(i + nd - n1).start()
+
+    for j in range(min(n2, max(0, nd - n1))):
+        cd(j).start()
+    step = 0
+    for ref in pre_refs:
+        for k in range(ref.shape[0] // tk):
+            gate(step, ref[k * tk : (k + 1) * tk, :])
+            if step == 0:
+                move.wait()
+                for d in range(peers):
+                    page_start(d)
+            if step >= lead:
+                up(step - lead)
+            step += 1
 
     def late(i, c):
         cg(i).wait()
-        xs = rows_of(i)
-        ga[...] += jnp.dot(xs, gb[lax.rem(i - ready, ng)], preferred_element_type=jnp.float32)
+        gate(i, gb[lax.rem(i - ready, ng)])
 
         @pl.when(i + ng < n1)
         def _():
             cg(i + ng).start()
 
-        up(i, xs)
+        up(i - lead)
         return c
 
+    def rest(i, c):
+        up(i)
+        return c
+
     lax.fori_loop(ready, n1, late, 0)
+    lax.fori_loop(n1 - lead, n1, rest, 0)
     g = ga[...]
     h[...] = ((g / (1.0 + jnp.exp(-g))) * ua[...]).astype(jnp.bfloat16)
+
+    low, members = groups[-1]
+    place = (me >> low) & (members - 1)
+    size = half // members
 
     def down(j, c):
         cd(j).wait()
         at = pl.ds(pl.multiple_of(j * tn, tn), tn)
         out = jnp.dot(h[...], db[lax.rem(j, nd)], preferred_element_type=jnp.float32)
         out = out * wsel[...]
-        keep_ref[:, at] = out[:half]
-        send_ref[:, at] = out[half:].astype(jnp.bfloat16)
+        for n, ref in enumerate((keep_ref,) + tuple(send_refs)):
+            start = (n // members) * half
+            want = place ^ (n % members)
+            block = out[start : start + size]
+            for p in range(1, members):
+                block = jnp.where(want == p, out[start + p * size : start + (p + 1) * size], block)
+            ref[:, at] = block.astype(ref.dtype)
 
         @pl.when(j + nd < n2)
         def _():
@@ -224,7 +242,7 @@
 
         return c
 
-    lax.fori_loop(0, n2, down, 0)
+    lax.fori_loop(0, n2, down, 0, unroll=2)
     for n, ref in enumerate((near_ref, far_ref)):
         pltpu.make_async_copy(ref, ref, semp.at[n]).wait()
 
@@ -252,12 +270,36 @@
 
 
 def stack_kernel(near_ref, far_ref, out_ref):
-    page = near_ref.shape[1]
-    out_ref[:, :page] = near_ref[...]
-    out_ref[:, page:] = far_ref[...]
-
-
-def finish_kernel(me_ref, len_ref, owner_ref, q_ref, local_ref, page_ref, hid_ref, own_ref, *refs):
+    width = near_ref.shape[2]
+    value = width - ROPE
+    for n, ref in enumerate((near_ref, far_ref)):
+        out_ref[:, :, n * value : (n + 1) * value] = ref[:, :, :value]
+        out_ref[:, :, 2 * value + n * ROPE : 2 * value + (n + 1) * ROPE] = ref[:, :, value:]
+
+
+def early_kernel(me_ref, len_ref, owner_ref, q_ref, local_ref, bias_ref, score_ref):
+    requests, heads, _ = q_ref.shape
+    local_len = local_ref.shape[1]
+    devices = owner_ref.shape[1]
+    keys = bias_ref.shape[1]
+    page_len = keys // devices
+    half = devices // 2
+    mine = me_ref[0] // half
+    holder = lax.broadcasted_iota(jnp.int32, (devices, keys), 0)
+    slot = lax.broadcasted_iota(jnp.int32, (devices, keys), 1) // page_len
+    sender = jnp.where(mine == 0, slot, jnp.where(slot < half, slot + half, slot - half))
+    owner = jnp.broadcast_to(jnp.transpose(owner_ref[...].astype(jnp.float32)), holder.shape)
+    key_owner = jnp.sum(jnp.where(holder == sender, owner, 0.0), axis=0, keepdims=True)
+    request = (lax.broadcasted_iota(jnp.int32, bias_ref.shape, 0) // heads).astype(jnp.float32)
+    bias_ref[...] = jnp.where(key_owner == request, 0.0, -jnp.inf)
+    pos = lax.broadcasted_iota(jnp.int32, (heads, local_len), 1)
+    nt = (((1,), (1,)), ((), ()))
+    for r in range(requests):
+        s = lax.dot_general(q_ref[r], local_ref[r], nt, preferred_element_type=jnp.float32) * score_scale
+        score_ref[r * heads : (r + 1) * heads] = jnp.where(pos < len_ref[r], s, -jnp.inf)
+
+
+def finish_kernel(bias_ref, score_ref, q_ref, local_ref, page_ref, hid_ref, own_ref, *refs):
     got_refs, out_ref, moe_ref = refs[:-2], refs[-2], refs[-1]
     total = own_ref[...]
     for ref in got_refs:
@@ -266,37 +308,27 @@
 
     requests, heads, width = q_ref.shape
     value = out_ref.shape[2]
-    local_len = local_ref.shape[1]
-    peers, both, _ = page_ref.shape
-    page_len = both // 2
-    devices = owner_ref.shape[1]
-    role = me_ref[0] // peers
-    keys = page_ref[...].reshape(peers * both, width)
-    holder = lax.broadcasted_iota(jnp.int32, (devices, peers * both), 0)
-    col = lax.broadcasted_iota(jnp.int32, (devices, peers * both), 1)
-    source = col // both
-    far = (col - source * both) // page_len
-    sender = jnp.where(far == 0, role, devices // peers - 1 - role) * peers + source
-    owner = jnp.broadcast_to(jnp.transpose(owner_ref[...].astype(jnp.float32)), holder.shape)
-    key_owner = jnp.sum(jnp.where(holder == sender, owner, 0.0), axis=0, keepdims=True)
+    peers, page_len, _ = page_ref.shape
+
+    def keys_of(start, size):
+        part = page_ref[:, :, start : start + size]
+        return part.reshape(peers * page_len, size)
+
+    wide = jnp.concatenate([keys_of(0, value), keys_of(value, value)], axis=0)
+    thin = jnp.concatenate([keys_of(2 * value, ROPE), keys_of(2 * value + ROPE, ROPE)], axis=0)
     nt = (((1,), (1,)), ((), ()))
     queries = q_ref[...].reshape(requests * heads, width)
-    s_page = lax.dot_general(queries, keys, nt, preferred_element_type=jnp.float32) * score_scale
-    request = (lax.broadcasted_iota(jnp.int32, s_page.shape, 0) // heads).astype(jnp.float32)
-    s_page = jnp.where(key_owner == request, s_page, -jnp.inf)
-    pos = lax.broadcasted_iota(jnp.int32, (heads, local_len), 1)
-    s_local = []
-    for r in range(requests):
-        s = lax.dot_general(q_ref[r], local_ref[r], nt, preferred_element_type=jnp.float32) * score_scale
-        s_local.append(jnp.where(pos < len_ref[r], s, -jnp.inf))
-    s_local = jnp.concatenate(s_local, axis=0)
+    s_page = lax.dot_general(queries[:, :value], wide, nt, preferred_element_type=jnp.float32)
+    s_page = s_page + lax.dot_general(queries[:, value:], thin, nt, preferred_element_type=jnp.float32)
+    s_page = s_page * score_scale + bias_ref[...]
+    s_local = score_ref[...]
     peak = jnp.maximum(jnp.max(s_local, axis=1, keepdims=True), jnp.max(s_page, axis=1, keepdims=True))
     e_local = jnp.exp(s_local - peak)
     e_page = jnp.exp(s_page - peak)
     norm = jnp.sum(e_local, axis=1, keepdims=True) + jnp.sum(e_page, axis=1, keepdims=True)
     p_local = (e_local / norm).astype(jnp.bfloat16)
     p_page = (e_page / norm).astype(jnp.bfloat16)
-    paged = jnp.dot(p_page, keys[:, :value], preferred_element_type=jnp.float32)
+    paged = jnp.dot(p_page, wide, preferred_element_type=jnp.float32)
     for r in range(requests):
         at = slice(r * heads, (r + 1) * heads)
         out = jnp.dot(p_local[at], local_ref[r][:, :value], preferred_element_type=jnp.float32)
@@ -325,7 +357,7 @@
     packed_width = width + LANES + id_cols
     half = dev_size * rows
     total_rows = role_size * half
-    tk = tn = tile_of(width, 512)
+    tk, tn = tile_of(width, 1024), tile_of(width, 512)
     weight_bytes = 2 * width * units
     groups = bit_groups(dev_size)
     weights_in = [pltpu.with_memory_space_constraint(w, pltpu.HBM) for w in (w_gate, w_up, w_down)]
@@ -358,7 +390,7 @@
             out_shape=pltpu.VMEM((size, units), jnp.bfloat16),
             in_specs=[HBM],
             out_specs=VM,
-            scratch_shapes=[pltpu.SemaphoreType.DMA((LOADS[index],))],
+            scratch_shapes=[pltpu.SemaphoreType.DMA((2 * LOADS[index],))],
             compiler_params=pltpu.CompilerParams(vmem_limit_bytes=1 << 20),
             cost_estimate=pl.CostEstimate(flops=0, bytes_accessed=2 * size * units, transcendentals=0),
         )(weights_in[0])
@@ -370,7 +402,7 @@
     taken = 0
     for k, (low, members) in enumerate(groups):
         got = [swap(held, offset << low) for offset in range(1, members)]
-        if k < len(LOADS) - 1:
+        if k < len(LOADS):
             loaded.append(load(k, taken))
             taken += LOADS[k] * tk
         held = pl.pallas_call(
@@ -381,21 +413,20 @@
             compiler_params=pltpu.CompilerParams(vmem_limit_bytes=6 << 20),
         )(me_arr, held, *got)
     other = role_swap(held)
-    loaded.append(load(len(LOADS) - 1, taken))
-
-    keep, send, near, far = pl.pallas_call(
+
+    low, members = groups[-1]
+    parts = role_size * members
+    size = half // members
+    own, *rest = pl.pallas_call(
         functools.partial(
             expert_kernel, tk=tk, tn=tn, base=width + LANES, rows=rows, slices=slices,
-            groups=groups, loads=len(loaded),
+            groups=groups, loads=len(loaded), parts=parts,
         ),
-        out_shape=(
-            jax.ShapeDtypeStruct((half, width), jnp.float32),
-            jax.ShapeDtypeStruct((half, width), jnp.bfloat16),
-            jax.ShapeDtypeStruct((dev_size,) + swap_pool.shape[1:], jnp.bfloat16),
-            jax.ShapeDtypeStruct((dev_size,) + swap_pool.shape[1:], jnp.bfloat16),
-        ),
+        out_shape=[jax.ShapeDtypeStruct((size, width), jnp.float32)]
+        + [jax.ShapeDtypeStruct((size, width), jnp.bfloat16)] * (parts - 1)
+        + [jax.ShapeDtypeStruct((dev_size,) + swap_pool.shape[1:], jnp.bfloat16)] * 2,
         in_specs=[SM, VM, VM] + [VM] * len(loaded) + [HBM] * 4,
-        out_specs=(VM, VM, VM, VM),
+        out_specs=[VM] * (parts + 2),
         scratch_shapes=[
             pltpu.VMEM((GATE_SLOTS, tk, units), jnp.bfloat16),
             pltpu.VMEM((UP_SLOTS, tk, units), jnp.bfloat16),
@@ -412,14 +443,19 @@
             pltpu.SemaphoreType.DMA,
             pltpu.SemaphoreType.DMA((2,)),
         ],
-        compiler_params=pltpu.CompilerParams(vmem_limit_bytes=31 << 20),
+        compiler_params=pltpu.CompilerParams(vmem_limit_bytes=36 << 20),
         cost_estimate=pl.CostEstimate(
             flops=6 * total_rows * width * units, bytes_accessed=3 * weight_bytes, transcendentals=0
         ),
     )(me_arr, held, other, *loaded, *weights_in, pool_in)
 
+    sends, near, far = rest[:-2], rest[-2], rest[-1]
     far = role_swap(far)
-    page_shape = (dev_size, 2 * swap_pool.shape[1], swap_pool.shape[2])
+    got = []
+    for n, value in enumerate(sends):
+        flat = ((n + 1) // members) * dev_size + (((n + 1) % members) << low)
+        got.append(lax.ppermute(value, ("role", "dev"), [(i, i ^ flat) for i in range(devices)]))
+    page_shape = (dev_size, swap_pool.shape[1], 2 * swap_pool.shape[2])
     outgoing = pl.pallas_call(
         stack_kernel,
         out_shape=jax.ShapeDtypeStruct(page_shape, jnp.bfloat16),
@@ -428,10 +464,7 @@
         compiler_params=pltpu.CompilerParams(vmem_limit_bytes=8 << 20),
     )(near, far)
     arrived = lax.all_to_all(outgoing, "dev", split_axis=0, concat_axis=0, tiled=True)
-
-    got = [role_swap(send)]
-    own = keep
-    for low, members in reversed(groups):
+    for low, members in reversed(groups[:-1]):
         count = own.shape[0] // members
         own, *sends = pl.pallas_call(
             functools.partial(fold_kernel, low=low, members=members, arrived=len(got)),
@@ -442,14 +475,25 @@
             compiler_params=pltpu.CompilerParams(vmem_limit_bytes=16 << 20),
         )(me_arr, own, *got)
         got = [swap(value, (n + 1) << low) for n, value in enumerate(sends)]
-    operands = (me_arr, cache_lengths, page_owner, queries, local_cache, arrived, hidden, own, *got)
+    query_rows = queries.shape[0] * queries.shape[1]
+    bias, scores = pl.pallas_call(
+        early_kernel,
+        out_shape=(
+            jax.ShapeDtypeStruct((query_rows, devices * swap_pool.shape[1]), jnp.float32),
+            jax.ShapeDtypeStruct((query_rows, local_cache.shape[1]), jnp.float32),
+        ),
+        in_specs=[SM] * 2 + [VM] * 3,
+        out_specs=(VM, VM),
+        compiler_params=pltpu.CompilerParams(vmem_limit_bytes=16 << 20),
+    )(me_arr, cache_lengths, page_owner, queries, local_cache)
+    operands = (bias, scores, queries, local_cache, arrived, hidden, own, *got)
     attn_out, moe_out = pl.pallas_call(
         finish_kernel,
         out_shape=(
             jax.ShapeDtypeStruct(queries.shape[:2] + (queries.shape[2] - ROPE,), jnp.bfloat16),
             jax.ShapeDtypeStruct(hidden.shape, jnp.bfloat16),
         ),
-        in_specs=[SM] * 2 + [VM] * (len(operands) - 2),
+        in_specs=[VM] * len(operands),
         out_specs=(VM, VM),
         compiler_params=pltpu.CompilerParams(vmem_limit_bytes=24 << 20),
     )(*operands)

time: 75.7 us -> 74.8 us (0.988)
  waiting for transfers between devices: 20.2 us -> 22 us
  starting transfers between devices: 19.2 us -> 17.5 us
  Pallas kernels: 35.3 us -> 34.1 us
    ppermute x0 -> x3, waiting for transfers between devices: none -> 8.32 us  [per_device(): lax.ppermute(value, ('role', 'dev'), [(i, i ^ flat) for i in range(device...]
    ppermute x8 -> x7, waiting for transfers between devices: 17.7 us -> 12.7 us  [swap(): lax.ppermute(value, 'dev', [(i, i ^ offset) for i in range(dev_size)])]
    ppermute x8 -> x7, starting transfers between devices: 14.2 us -> 11.3 us  [swap(): lax.ppermute(value, 'dev', [(i, i ^ offset) for i in range(dev_size)])]
    ppermute x0 -> x3, starting transfers between devices: none -> 2.21 us  [per_device(): lax.ppermute(value, ('role', 'dev'), [(i, i ^ flat) for i in range(device...]
    ppermute x3 -> x2, waiting for transfers between devices: 2.43 us -> 1.03 us  [role_swap(): return lax.ppermute(x, 'role', [(i, size - 1 - i) for i in range(size)])]
    pallas_call x3 -> x2, Pallas kernels: 8.02 us -> 7.01 us  [load(): pl.pallas_call(functools.partial(load_kernel, start=start), out_shape=plt...]
    all_to_all x1, starting transfers between devices: 4.21 us -> 3.42 us  [per_device(): lax.all_to_all(outgoing, 'dev', split_axis=0, concat_axis=0, tiled=True)]
  transfers between devices with their start and end apart: 12 -> 13, of which waited for: 8 -> 7; matrix products, arithmetic and copies ran while one was open for 0% -> 0% of each run, Pallas kernels for 11% -> 11%
where the time goes in v4:
time: 74.8 us; the launch traced here: 74.5 us
  Pallas kernels  34.1 us (46%)
  waiting for transfers between devices  22 us (29%)
  starting transfers between devices  17.5 us (23%)
  between operations  0.78 us (1%)
    pallas_call x1, Pallas kernels, per_device(): pl.pallas_call(functools.partial(expert_kernel, tk=tk, tn=tn, base=width...  22.8 us
    ppermute x7, waiting for transfers between devices, swap(): lax.ppermute(value, 'dev', [(i, i ^ offset) for i in range(dev_size)])  12.7 us
    ppermute x7, starting transfers between devices, swap(): lax.ppermute(value, 'dev', [(i, i ^ offset) for i in range(dev_size)])  11.3 us
    ppermute x3, waiting for transfers between devices, per_device(): lax.ppermute(value, ('role', 'dev'), [(i, i ^ flat) for i in range(device...  8.32 us
    pallas_call x2, Pallas kernels, load(): pl.pallas_call(functools.partial(load_kernel, start=start), out_shape=plt...  7.01 us
    all_to_all x1, starting transfers between devices, per_device(): lax.all_to_all(outgoing, 'dev', split_axis=0, concat_axis=0, tiled=True)  3.42 us
    ppermute x3, starting transfers between devices, per_device(): lax.ppermute(value, ('role', 'dev'), [(i, i ^ flat) for i in range(device...  2.21 us
  transfers between devices with their start and end apart: 13, of which 7 were waited for; matrix products, arithmetic and copies ran while one was open for 0% of the time, Pallas kernels for 11%

profile of v4, /device:TPU:0, one launch (start us, length us, event | category | flops | bytes accessed | tf_op | source)
XLA Modules:
  0.0 74.5 jit_solution(14040086457588893581)
XLA Ops:
  0.6 1.0 %shard_map.141.refs_0_ = bf16[2,7424]{1,0:T(2,128)(2,1)S(1)} custom-call(s32[1]{0:T(128)} %bitcast.me_ref.refs_0_, bf16[2,7168]{1,0:T(2,128)(2,1)} %hid_ref.3, bf16[7168]{0:T(1024)(128)(2,1)} %gain_ref.1, s32[2,8]{1,0:T(2,128)} %routes_ref.1, f32[2,8]{1,0:T(2,128)} %weights_ref.1, s32[1,16]{1,0:T(1,128)} %ids_ref.1), custom_call_target="tpu_custom_call" | custom-call | tf_op jit(solution)/shard_map/pallas_call | solution.py:370
  1.6 3.1 %collective-permute-start = (bf16[2,7424]{1,0:T(2,128)(2,1)S(1)}, bf16[2,7424]{1,0:T(2,128)(2,1)S(1)}, u32[]{:S(2)}, u32[]{:S(2)}) collective-permute-start(bf16[2,7424]{1,0:T(2,128)(2,1)S(1)} %shard_map.141.refs_0_), channel_id=1, source_target_pairs={{0,2},{1,3},{2,0},{3,1},{4,6},{5,7},{6,4},{7,5},{8,10},{9,11},{10,... | collective-permute-start | bytes 89096 | tf_op jit(solution)/shard_map/ppermute | solution.py:399
  4.7 2.6 %collective-permute-start.1 = (bf16[2,7424]{1,0:T(2,128)(2,1)S(1)}, bf16[2,7424]{1,0:T(2,128)(2,1)S(1)}, u32[]{:S(2)}, u32[]{:S(2)}) collective-permute-start(bf16[2,7424]{1,0:T(2,128)(2,1)S(1)} %shard_map.141.refs_0_), channel_id=1, source_target_pairs={{0,4},{1,5},{2,6},{3,7},{4,0},{5,1},{6,2},{7,3},{8,12},{9,13},{10,... | collective-permute-start | bytes 89096 | tf_op jit(solution)/shard_map/ppermute | solution.py:399
  7.3 2.7 %collective-permute-done.1.refs_2_ = bf16[2,7424]{1,0:T(2,128)(2,1)S(1)} collective-permute-done((bf16[2,7424]{1,0:T(2,128)(2,1)S(1)}, bf16[2,7424]{1,0:T(2,128)(2,1)S(1)}, u32[]{:S(2)}, u32[]{:S(2)}) %collective-permute-start.1) | collective-permute-done | bytes 29728 | tf_op jit(solution)/shard_map/ppermute | solution.py:399
  10.0 3.0 %collective-permute-done.2.refs_3_ = bf16[2,7424]{1,0:T(2,128)(2,1)S(1)} collective-permute-done((bf16[2,7424]{1,0:T(2,128)(2,1)S(1)}, bf16[2,7424]{1,0:T(2,128)(2,1)S(1)}, u32[]{:S(2)}, u32[]{:S(2)}) %collective-permute-start.2) | collective-permute-done | bytes 29728 | tf_op jit(solution)/shard_map/ppermute | solution.py:399
  13.0 0.1 shard_map.142.refs_0_
  13.1 1.6 %collective-permute-start.3 = (bf16[8,7424]{1,0:T(8,128)(2,1)S(1)}, bf16[8,7424]{1,0:T(8,128)(2,1)S(1)}, u32[]{:S(2)}, u32[]{:S(2)}) collective-permute-start(bf16[8,7424]{1,0:T(8,128)(2,1)S(1)} %shard_map.142.refs_0_), channel_id=1, source_target_pairs={{0,1},{1,0},{2,3},{3,2},{4,5},{5,4},{6,7},{7,6},{8,9},{9,8},{10,11... | collective-permute-start | bytes 356360 | tf_op jit(solution)/shard_map/ppermute | solution.py:399
  14.7 3.3 %collective-permute-done.3.refs_1_ = bf16[8,7424]{1,0:T(8,128)(2,1)S(1)} collective-permute-done((bf16[8,7424]{1,0:T(8,128)(2,1)S(1)}, bf16[8,7424]{1,0:T(8,128)(2,1)S(1)}, u32[]{:S(2)}, u32[]{:S(2)}) %collective-permute-start.3) | collective-permute-done | bytes 118816 | tf_op jit(solution)/shard_map/ppermute | solution.py:399
  18.0 0.1 collective-permute-start.4
  18.1 3.5 %shard_map.144.refs_3_ = bf16[2048,2048]{1,0:T(8,128)(2,1)S(1)} custom-call(bf16[7168,2048]{1,0:T(8,128)(2,1)} %refs_5_.1), custom_call_target="tpu_custom_call" | custom-call | bytes 8388608 | tf_op jit(solution)/shard_map/pallas_call | solution.py:388
  21.6 3.5 %shard_map.145.refs_4_ = bf16[2048,2048]{1,0:T(8,128)(2,1)S(1)} custom-call(bf16[7168,2048]{1,0:T(8,128)(2,1)} %refs_5_.1), custom_call_target="tpu_custom_call" | custom-call | bytes 8388608 | tf_op jit(solution)/shard_map/pallas_call | solution.py:388
  25.1 0.0 copy-start
  25.1 0.0 copy-start.1
  25.2 0.0 copy-start.3
  25.2 0.0 copy-start.4
  25.2 22.8 %shard_map.146 = (f32[8,7168]{1,0:T(8,128)S(1)}, bf16[8,7168]{1,0:T(8,128)(2,1)S(1)}, bf16[8,7168]{1,0:T(8,128)(2,1)S(1)}, bf16[8,7168]{1,0:T(8,128)(2,1)S(1)}, ...) custom-call(s32[1]{0:T(128)} %bitcast.me_ref.refs_0_, bf16[16,7424]{1,0:T(8,128)(2,1)S(1)} %shard_map.143.refs_1_, ...), custom_call_target="tpu_custom_call" | custom-call | flops 2818572288 | bytes 88080384 | tf_op jit(solution)/shard_map/pallas_call | solution.py:420
  48.0 0.6 collective-permute-start.5
  48.5 1.0 %collective-permute-done.5.far_ref = bf16[8,16,576]{2,1,0:T(8,128)(2,1)S(1)} collective-permute-done((bf16[8,16,576]{2,1,0:T(8,128)(2,1)S(1)}, bf16[8,16,576]{2,1,0:T(8,128)(2,1)S(1)}, u32[]{:S(2)}, u32[]{:S(2)}) %collective-permute-start.5) | collective-permute-done | bytes 147488 | tf_op jit(solution)/shard_map/ppermute | solution.py:32
  49.6 0.8 %shard_map.147 = bf16[8,16,1152]{2,1,0:T(8,128)(2,1)} custom-call(bf16[8,16,576]{2,1,0:T(8,128)(2,1)S(1)} %get-tuple-element.16.near_ref, bf16[8,16,576]{2,1,0:T(8,128)(2,1)S(1)} %collective-permute-done.5.far_ref), custom_call_target="tpu_custom_call" | custom-call | tf_op jit(solution)/shard_map/pallas_call | solution.py:459
  50.4 3.4 %all-to-all-start = ((bf16[8,16,1152]{2,1,0:T(8,128)(2,1)}), bf16[8,16,1152]{2,1,0:T(8,128)(2,1)S(1)}, u32[]{:S(2)}, u32[]{:S(2)}) async-start(bf16[8,16,1152]{2,1,0:T(8,128)(2,1)} %shard_map.147), calls=%async_computation | async-start | bytes 589824 | tf_op jit(solution)/shard_map/all_to_all | solution.py:466
  53.8 1.9 %collective-permute-start.6 = (bf16[8,7168]{1,0:T(8,128)(2,1)S(1)}, bf16[8,7168]{1,0:T(8,128)(2,1)S(1)}, u32[]{:S(2)}, u32[]{:S(2)}) collective-permute-start(bf16[8,7168]{1,0:T(8,128)(2,1)S(1)} %get-tuple-element.19), channel_id=1, source_target_pairs={{0,1},{1,0},{2,3},{3,2},{4,5},{5,4},{6,7},{7,6},{8,9},{9,8},{10,11... | collective-permute-start | bytes 344072 | tf_op jit(solution)/shard_map/ppermute | solution.py:457
  55.7 0.3 collective-permute-start.8
  56.0 6.4 %collective-permute-done.6.refs_1_ = bf16[8,7168]{1,0:T(8,128)(2,1)S(1)} collective-permute-done((bf16[8,7168]{1,0:T(8,128)(2,1)S(1)}, bf16[8,7168]{1,0:T(8,128)(2,1)S(1)}, u32[]{:S(2)}, u32[]{:S(2)}) %collective-permute-start.6) | collective-permute-done | bytes 114720 | tf_op jit(solution)/shard_map/ppermute | solution.py:457
  62.4 1.9 %collective-permute-done.8.refs_3_ = bf16[8,7168]{1,0:T(8,128)(2,1)S(1)} collective-permute-done((bf16[8,7168]{1,0:T(8,128)(2,1)S(1)}, bf16[8,7168]{1,0:T(8,128)(2,1)S(1)}, u32[]{:S(2)}, u32[]{:S(2)}) %collective-permute-start.8) | collective-permute-done | bytes 114720 | tf_op jit(solution)/shard_map/ppermute | solution.py:457
  64.3 0.2 shard_map.148
  64.6 2.8 %collective-permute-start.10 = (bf16[2,7168]{1,0:T(2,128)(2,1)S(1)}, bf16[2,7168]{1,0:T(2,128)(2,1)S(1)}, u32[]{:S(2)}, u32[]{:S(2)}) collective-permute-start(bf16[2,7168]{1,0:T(2,128)(2,1)S(1)} %get-tuple-element.24), channel_id=1, source_target_pairs={{0,4},{1,5},{2,6},{3,7},{4,0},{5,1},{6,2},{7,3},{8,12},{9,13},{10,... | collective-permute-start | bytes 86024 | tf_op jit(solution)/shard_map/ppermute | solution.py:399
  67.4 1.1 %collective-permute-start.11 = (bf16[2,7168]{1,0:T(2,128)(2,1)S(1)}, bf16[2,7168]{1,0:T(2,128)(2,1)S(1)}, u32[]{:S(2)}, u32[]{:S(2)}) collective-permute-start(bf16[2,7168]{1,0:T(2,128)(2,1)S(1)} %get-tuple-element.25), channel_id=1, source_target_pairs={{0,6},{1,7},{2,4},{3,5},{4,2},{5,3},{6,0},{7,1},{8,14},{9,15},{10,... | collective-permute-start | bytes 86024 | tf_op jit(solution)/shard_map/ppermute | solution.py:399
  68.5 0.1 collective-permute-start.9
  68.6 0.7 shard_map.140
  69.4 0.0 collective-permute-done.10.refs_1_
  69.4 3.6 %collective-permute-done.11.refs_2_ = bf16[2,7168]{1,0:T(2,128)(2,1)S(1)} collective-permute-done((bf16[2,7168]{1,0:T(2,128)(2,1)S(1)}, bf16[2,7168]{1,0:T(2,128)(2,1)S(1)}, u32[]{:S(2)}, u32[]{:S(2)}) %collective-permute-start.11) | collective-permute-done | bytes 28704 | tf_op jit(solution)/shard_map/ppermute | solution.py:399
  73.1 1.4 %shard_map.149 = (bf16[2,64,512]{2,1,0:T(8,128)(2,1)}, bf16[2,7168]{1,0:T(2,128)(2,1)}) custom-call(f32[128,256]{1,0:T(8,128)S(1)} %get-tuple-element.14.bias_ref, f32[128,64]{1,0:T(8,128)S(1)} %get-tuple-element.15.score_ref, bf16[2,64,576]{2,1,0:T(8,128)(2,1)S(1)} %copy-done, bf16[2,64,576]{2,1,0:T(8,128)(2,1)S(1)} %copy-done.1, ...), custom_call_target="tpu_custom_call" | custom-call | tf_op jit(solution)/shard_map/pallas_call | solution.py:490
  (14 shorter events, 0.1 us)
Async XLA Ops:
  1.6 5.7 %collective-permute-start = (bf16[2,7424]{1,0:T(2,128)(2,1)S(1)}, bf16[2,7424]{1,0:T(2,128)(2,1)S(1)}, u32[]{:S(2)}, u32[]{:S(2)}) collective-permute-start(bf16[2,7424]{1,0:T(2,128)(2,1)S(1)} %shard_map.141.refs_0_), channel_id=1, source_target_pairs={{0,2},{1,3},{2,0},{3,1},{4,6},{5,7},{6,4},{7,5},{8,10},{9,11},{10,... | collective-permute-start | bytes 89096 | tf_op jit(solution)/shard_map/ppermute | solution.py:399
  4.7 5.3 %collective-permute-start.1 = (bf16[2,7424]{1,0:T(2,128)(2,1)S(1)}, bf16[2,7424]{1,0:T(2,128)(2,1)S(1)}, u32[]{:S(2)}, u32[]{:S(2)}) collective-permute-start(bf16[2,7424]{1,0:T(2,128)(2,1)S(1)} %shard_map.141.refs_0_), channel_id=1, source_target_pairs={{0,4},{1,5},{2,6},{3,7},{4,0},{5,1},{6,2},{7,3},{8,12},{9,13},{10,... | collective-permute-start | bytes 89096 | tf_op jit(solution)/shard_map/ppermute | solution.py:399
  7.3 5.7 %collective-permute-start.2 = (bf16[2,7424]{1,0:T(2,128)(2,1)S(1)}, bf16[2,7424]{1,0:T(2,128)(2,1)S(1)}, u32[]{:S(2)}, u32[]{:S(2)}) collective-permute-start(bf16[2,7424]{1,0:T(2,128)(2,1)S(1)} %shard_map.141.refs_0_), channel_id=1, source_target_pairs={{0,6},{1,7},{2,4},{3,5},{4,2},{5,3},{6,0},{7,1},{8,14},{9,15},{10,... | collective-permute-start | bytes 89096 | tf_op jit(solution)/shard_map/ppermute | solution.py:399
  13.1 4.9 %collective-permute-start.3 = (bf16[8,7424]{1,0:T(8,128)(2,1)S(1)}, bf16[8,7424]{1,0:T(8,128)(2,1)S(1)}, u32[]{:S(2)}, u32[]{:S(2)}) collective-permute-start(bf16[8,7424]{1,0:T(8,128)(2,1)S(1)} %shard_map.142.refs_0_), channel_id=1, source_target_pairs={{0,1},{1,0},{2,3},{3,2},{4,5},{5,4},{6,7},{7,6},{8,9},{9,8},{10,11... | collective-permute-start | bytes 356360 | tf_op jit(solution)/shard_map/ppermute | solution.py:399
  18.0 7.2 %collective-permute-start.4 = (bf16[16,7424]{1,0:T(8,128)(2,1)S(1)}, bf16[16,7424]{1,0:T(8,128)(2,1)S(1)}, u32[]{:S(2)}, u32[]{:S(2)}) collective-permute-start(bf16[16,7424]{1,0:T(8,128)(2,1)S(1)} %shard_map.143.refs_1_), channel_id=1, source_target_pairs={{0,8},{8,0},{1,9},{9,1},{2,10},{10,2},{3,11},{11,3},{4,12},{12,4},... | collective-permute-start | bytes 712712 | tf_op jit(solution)/shard_map/ppermute | solution.py:32
  25.1 43.5 %copy-start = (bf16[2,64,576]{2,1,0:T(8,128)(2,1)S(1)}, bf16[2,64,576]{2,1,0:T(8,128)(2,1)}, u32[]{:S(2)}) copy-start(bf16[2,64,576]{2,1,0:T(8,128)(2,1)} %q_ref.3) | copy-start | bytes 442372
  25.1 43.5 %copy-start.1 = (bf16[2,64,576]{2,1,0:T(8,128)(2,1)S(1)}, bf16[2,64,576]{2,1,0:T(8,128)(2,1)}, u32[]{:S(2)}) copy-start(bf16[2,64,576]{2,1,0:T(8,128)(2,1)} %local_ref.3) | copy-start | bytes 442372
  25.2 43.5 %copy-start.3 = (s32[2]{0:T(128)S(1)}, s32[2]{0:T(128)}, u32[]{:S(2)}) copy-start(s32[2]{0:T(128)} %len_ref.1) | copy-start | bytes 28
  25.2 43.5 %copy-start.4 = (s32[1,16]{1,0:T(1,128)S(1)}, s32[1,16]{1,0:T(1,128)}, u32[]{:S(2)}) copy-start(s32[1,16]{1,0:T(1,128)} %owner_ref.1) | copy-start | bytes 196
  25.2 47.9 %copy-start.2 = (bf16[2,7168]{1,0:T(2,128)(2,1)S(1)}, bf16[2,7168]{1,0:T(2,128)(2,1)}, u32[]{:S(2)}) copy-start(bf16[2,7168]{1,0:T(2,128)(2,1)} %hid_ref.3) | copy-start | bytes 86020
  48.0 1.6 %collective-permute-start.5 = (bf16[8,16,576]{2,1,0:T(8,128)(2,1)S(1)}, bf16[8,16,576]{2,1,0:T(8,128)(2,1)S(1)}, u32[]{:S(2)}, u32[]{:S(2)}) collective-permute-start(bf16[8,16,576]{2,1,0:T(8,128)(2,1)S(1)} %get-tuple-element.17), channel_id=1, source_target_pairs={{0,8},{8,0},{1,9},{9,1},{2,10},{10,2},{3,11},{11,3},{4,12},{12,4},... | collective-permute-start | bytes 442376 | tf_op jit(solution)/shard_map/ppermute | solution.py:32
  50.4 22.7 %all-to-all-start = ((bf16[8,16,1152]{2,1,0:T(8,128)(2,1)}), bf16[8,16,1152]{2,1,0:T(8,128)(2,1)S(1)}, u32[]{:S(2)}, u32[]{:S(2)}) async-start(bf16[8,16,1152]{2,1,0:T(8,128)(2,1)} %shard_map.147), calls=%async_computation | async-start | bytes 589824 | tf_op jit(solution)/shard_map/all_to_all | solution.py:466
  53.8 8.6 %collective-permute-start.6 = (bf16[8,7168]{1,0:T(8,128)(2,1)S(1)}, bf16[8,7168]{1,0:T(8,128)(2,1)S(1)}, u32[]{:S(2)}, u32[]{:S(2)}) collective-permute-start(bf16[8,7168]{1,0:T(8,128)(2,1)S(1)} %get-tuple-element.19), channel_id=1, source_target_pairs={{0,1},{1,0},{2,3},{3,2},{4,5},{5,4},{6,7},{7,6},{8,9},{9,8},{10,11... | collective-permute-start | bytes 344072 | tf_op jit(solution)/shard_map/ppermute | solution.py:457
  55.7 6.7 %collective-permute-start.7 = (bf16[8,7168]{1,0:T(8,128)(2,1)S(1)}, bf16[8,7168]{1,0:T(8,128)(2,1)S(1)}, u32[]{:S(2)}, u32[]{:S(2)}) collective-permute-start(bf16[8,7168]{1,0:T(8,128)(2,1)S(1)} %get-tuple-element.20), channel_id=1, source_target_pairs={{0,8},{1,9},{2,10},{3,11},{4,12},{5,13},{6,14},{7,15},{8,0},{9,1},... | collective-permute-start | bytes 344072 | tf_op jit(solution)/shard_map/ppermute | solution.py:457
  55.7 8.6 %collective-permute-start.8 = (bf16[8,7168]{1,0:T(8,128)(2,1)S(1)}, bf16[8,7168]{1,0:T(8,128)(2,1)S(1)}, u32[]{:S(2)}, u32[]{:S(2)}) collective-permute-start(bf16[8,7168]{1,0:T(8,128)(2,1)S(1)} %get-tuple-element.21), channel_id=1, source_target_pairs={{0,9},{1,8},{2,11},{3,10},{4,13},{5,12},{6,15},{7,14},{8,1},{9,0},... | collective-permute-start | bytes 344072 | tf_op jit(solution)/shard_map/ppermute | solution.py:457
  64.6 4.8 %collective-permute-start.10 = (bf16[2,7168]{1,0:T(2,128)(2,1)S(1)}, bf16[2,7168]{1,0:T(2,128)(2,1)S(1)}, u32[]{:S(2)}, u32[]{:S(2)}) collective-permute-start(bf16[2,7168]{1,0:T(2,128)(2,1)S(1)} %get-tuple-element.24), channel_id=1, source_target_pairs={{0,4},{1,5},{2,6},{3,7},{4,0},{5,1},{6,2},{7,3},{8,12},{9,13},{10,... | collective-permute-start | bytes 86024 | tf_op jit(solution)/shard_map/ppermute | solution.py:399
  67.4 5.7 %collective-permute-start.11 = (bf16[2,7168]{1,0:T(2,128)(2,1)S(1)}, bf16[2,7168]{1,0:T(2,128)(2,1)S(1)}, u32[]{:S(2)}, u32[]{:S(2)}) collective-permute-start(bf16[2,7168]{1,0:T(2,128)(2,1)S(1)} %get-tuple-element.25), channel_id=1, source_target_pairs={{0,6},{1,7},{2,4},{3,5},{4,2},{5,3},{6,0},{7,1},{8,14},{9,15},{10,... | collective-permute-start | bytes 86024 | tf_op jit(solution)/shard_map/ppermute | solution.py:399
  68.5 4.6 %collective-permute-start.9 = (bf16[2,7168]{1,0:T(2,128)(2,1)S(1)}, bf16[2,7168]{1,0:T(2,128)(2,1)S(1)}, u32[]{:S(2)}, u32[]{:S(2)}) collective-permute-start(bf16[2,7168]{1,0:T(2,128)(2,1)S(1)} %get-tuple-element.23), channel_id=1, source_target_pairs={{0,2},{1,3},{2,0},{3,1},{4,6},{5,7},{6,4},{7,5},{8,10},{9,11},{10,... | collective-permute-start | bytes 86024 | tf_op jit(solution)/shard_map/ppermute | solution.py:399

commit v5 on v4

--- a/solution.py
+++ b/solution.py
@@ -277,7 +277,7 @@
         out_ref[:, :, 2 * value + n * ROPE : 2 * value + (n + 1) * ROPE] = ref[:, :, value:]
 
 
-def early_kernel(me_ref, len_ref, owner_ref, q_ref, local_ref, bias_ref, score_ref):
+def early_kernel(me_ref, len_ref, owner_ref, q_ref, local_ref, bias_ref, peak_ref, sum_ref, part_ref):
     requests, heads, _ = q_ref.shape
     local_len = local_ref.shape[1]
     devices = owner_ref.shape[1]
@@ -296,10 +296,17 @@
     nt = (((1,), (1,)), ((), ()))
     for r in range(requests):
         s = lax.dot_general(q_ref[r], local_ref[r], nt, preferred_element_type=jnp.float32) * score_scale
-        score_ref[r * heads : (r + 1) * heads] = jnp.where(pos < len_ref[r], s, -jnp.inf)
-
-
-def finish_kernel(bias_ref, score_ref, q_ref, local_ref, page_ref, hid_ref, own_ref, *refs):
+        s = jnp.where(pos < len_ref[r], s, -jnp.inf)
+        at = slice(r * heads, (r + 1) * heads)
+        peak = jnp.max(s, axis=1, keepdims=True)
+        e = jnp.exp(s - peak)
+        peak_ref[at] = peak
+        sum_ref[at] = jnp.sum(e, axis=1, keepdims=True)
+        local = local_ref[r][:, : part_ref.shape[1]]
+        part_ref[at] = jnp.dot(e.astype(jnp.bfloat16), local, preferred_element_type=jnp.float32)
+
+
+def finish_kernel(bias_ref, peak_ref, sum_ref, part_ref, q_ref, page_ref, hid_ref, own_ref, *refs):
     got_refs, out_ref, moe_ref = refs[:-2], refs[-2], refs[-1]
     total = own_ref[...]
     for ref in got_refs:
@@ -321,18 +328,14 @@
     s_page = lax.dot_general(queries[:, :value], wide, nt, preferred_element_type=jnp.float32)
     s_page = s_page + lax.dot_general(queries[:, value:], thin, nt, preferred_element_type=jnp.float32)
     s_page = s_page * score_scale + bias_ref[...]
-    s_local = score_ref[...]
-    peak = jnp.maximum(jnp.max(s_local, axis=1, keepdims=True), jnp.max(s_page, axis=1, keepdims=True))
-    e_local = jnp.exp(s_local - peak)
+    peak = jnp.maximum(peak_ref[...], jnp.max(s_page, axis=1, keepdims=True))
+    scale = jnp.exp(peak_ref[...] - peak)
     e_page = jnp.exp(s_page - peak)
-    norm = jnp.sum(e_local, axis=1, keepdims=True) + jnp.sum(e_page, axis=1, keepdims=True)
-    p_local = (e_local / norm).astype(jnp.bfloat16)
+    norm = sum_ref[...] * scale + jnp.sum(e_page, axis=1, keepdims=True)
     p_page = (e_page / norm).astype(jnp.bfloat16)
-    paged = jnp.dot(p_page, wide, preferred_element_type=jnp.float32)
+    out = jnp.dot(p_page, wide, preferred_element_type=jnp.float32) + part_ref[...] * (scale / norm)
     for r in range(requests):
-        at = slice(r * heads, (r + 1) * heads)
-        out = jnp.dot(p_local[at], local_ref[r][:, :value], preferred_element_type=jnp.float32)
-        out_ref[r] = (out + paged[at]).astype(jnp.bfloat16)
+        out_ref[r] = out[r * heads : (r + 1) * heads].astype(jnp.bfloat16)
 
 
 def tile_of(size, want):
@@ -476,17 +479,19 @@
         )(me_arr, own, *got)
         got = [swap(value, (n + 1) << low) for n, value in enumerate(sends)]
     query_rows = queries.shape[0] * queries.shape[1]
-    bias, scores = pl.pallas_call(
+    bias, peaks, sums, local_out = pl.pallas_call(
         early_kernel,
         out_shape=(
             jax.ShapeDtypeStruct((query_rows, devices * swap_pool.shape[1]), jnp.float32),
-            jax.ShapeDtypeStruct((query_rows, local_cache.shape[1]), jnp.float32),
+            jax.ShapeDtypeStruct((query_rows, 1), jnp.float32),
+            jax.ShapeDtypeStruct((query_rows, 1), jnp.float32),
+            jax.ShapeDtypeStruct((query_rows, queries.shape[2] - ROPE), jnp.float32),
         ),
         in_specs=[SM] * 2 + [VM] * 3,
-        out_specs=(VM, VM),
+        out_specs=(VM,) * 4,
         compiler_params=pltpu.CompilerParams(vmem_limit_bytes=16 << 20),
     )(me_arr, cache_lengths, page_owner, queries, local_cache)
-    operands = (bias, scores, queries, local_cache, arrived, hidden, own, *got)
+    operands = (bias, peaks, sums, local_out, queries, arrived, hidden, own, *got)
     attn_out, moe_out = pl.pallas_call(
         finish_kernel,
         out_shape=(

time: 74.8 us -> 74.8 us (level)
  no operation moved by 1% of the time
where the time goes in v5:
time: 74.8 us; the launch traced here: 74.5 us
  Pallas kernels  34.5 us (46%)
  waiting for transfers between devices  21.6 us (29%)
  starting transfers between devices  17.5 us (23%)
  between operations  0.79 us (1%)
    pallas_call x1, Pallas kernels, per_device(): pl.pallas_call(functools.partial(expert_kernel, tk=tk, tn=tn, base=width...  22.8 us
    ppermute x7, waiting for transfers between devices, swap(): lax.ppermute(value, 'dev', [(i, i ^ offset) for i in range(dev_size)])  12.2 us
    ppermute x7, starting transfers between devices, swap(): lax.ppermute(value, 'dev', [(i, i ^ offset) for i in range(dev_size)])  11.3 us
    ppermute x3, waiting for transfers between devices, per_device(): lax.ppermute(value, ('role', 'dev'), [(i, i ^ flat) for i in range(device...  8.32 us
    pallas_call x2, Pallas kernels, load(): pl.pallas_call(functools.partial(load_kernel, start=start), out_shape=plt...  7.01 us
    all_to_all x1, starting transfers between devices, per_device(): lax.all_to_all(outgoing, 'dev', split_axis=0, concat_axis=0, tiled=True)  3.42 us
    ppermute x3, starting transfers between devices, per_device(): lax.ppermute(value, ('role', 'dev'), [(i, i ^ flat) for i in range(device...  2.21 us
  transfers between devices with their start and end apart: 13, of which 7 were waited for; matrix products, arithmetic and copies ran while one was open for 0% of the time, Pallas kernels for 11%

profile of v5, /device:TPU:0, one launch (start us, length us, event | category | flops | bytes accessed | tf_op | source)
XLA Modules:
  0.0 74.5 jit_solution(9278224434395512294)
XLA Ops:
  0.6 1.0 %shard_map.141.refs_0_ = bf16[2,7424]{1,0:T(2,128)(2,1)S(1)} custom-call(s32[1]{0:T(128)} %bitcast.me_ref.refs_0_, bf16[2,7168]{1,0:T(2,128)(2,1)} %hid_ref.3, bf16[7168]{0:T(1024)(128)(2,1)} %gain_ref.1, s32[2,8]{1,0:T(2,128)} %routes_ref.1, f32[2,8]{1,0:T(2,128)} %weights_ref.1, s32[1,16]{1,0:T(1,128)} %ids_ref.1), custom_call_target="tpu_custom_call" | custom-call | tf_op jit(solution)/shard_map/pallas_call | solution.py:373
  1.6 3.1 %collective-permute-start = (bf16[2,7424]{1,0:T(2,128)(2,1)S(1)}, bf16[2,7424]{1,0:T(2,128)(2,1)S(1)}, u32[]{:S(2)}, u32[]{:S(2)}) collective-permute-start(bf16[2,7424]{1,0:T(2,128)(2,1)S(1)} %shard_map.141.refs_0_), channel_id=1, source_target_pairs={{0,2},{1,3},{2,0},{3,1},{4,6},{5,7},{6,4},{7,5},{8,10},{9,11},{10,... | collective-permute-start | bytes 89096 | tf_op jit(solution)/shard_map/ppermute | solution.py:402
  4.7 2.6 %collective-permute-start.1 = (bf16[2,7424]{1,0:T(2,128)(2,1)S(1)}, bf16[2,7424]{1,0:T(2,128)(2,1)S(1)}, u32[]{:S(2)}, u32[]{:S(2)}) collective-permute-start(bf16[2,7424]{1,0:T(2,128)(2,1)S(1)} %shard_map.141.refs_0_), channel_id=1, source_target_pairs={{0,4},{1,5},{2,6},{3,7},{4,0},{5,1},{6,2},{7,3},{8,12},{9,13},{10,... | collective-permute-start | bytes 89096 | tf_op jit(solution)/shard_map/ppermute | solution.py:402
  7.3 2.7 %collective-permute-done.1.refs_2_ = bf16[2,7424]{1,0:T(2,128)(2,1)S(1)} collective-permute-done((bf16[2,7424]{1,0:T(2,128)(2,1)S(1)}, bf16[2,7424]{1,0:T(2,128)(2,1)S(1)}, u32[]{:S(2)}, u32[]{:S(2)}) %collective-permute-start.1) | collective-permute-done | bytes 29728 | tf_op jit(solution)/shard_map/ppermute | solution.py:402
  10.0 3.0 %collective-permute-done.2.refs_3_ = bf16[2,7424]{1,0:T(2,128)(2,1)S(1)} collective-permute-done((bf16[2,7424]{1,0:T(2,128)(2,1)S(1)}, bf16[2,7424]{1,0:T(2,128)(2,1)S(1)}, u32[]{:S(2)}, u32[]{:S(2)}) %collective-permute-start.2) | collective-permute-done | bytes 29728 | tf_op jit(solution)/shard_map/ppermute | solution.py:402
  13.0 0.1 shard_map.142.refs_0_
  13.1 1.6 %collective-permute-start.3 = (bf16[8,7424]{1,0:T(8,128)(2,1)S(1)}, bf16[8,7424]{1,0:T(8,128)(2,1)S(1)}, u32[]{:S(2)}, u32[]{:S(2)}) collective-permute-start(bf16[8,7424]{1,0:T(8,128)(2,1)S(1)} %shard_map.142.refs_0_), channel_id=1, source_target_pairs={{0,1},{1,0},{2,3},{3,2},{4,5},{5,4},{6,7},{7,6},{8,9},{9,8},{10,11... | collective-permute-start | bytes 356360 | tf_op jit(solution)/shard_map/ppermute | solution.py:402
  14.7 3.3 %collective-permute-done.3.refs_1_ = bf16[8,7424]{1,0:T(8,128)(2,1)S(1)} collective-permute-done((bf16[8,7424]{1,0:T(8,128)(2,1)S(1)}, bf16[8,7424]{1,0:T(8,128)(2,1)S(1)}, u32[]{:S(2)}, u32[]{:S(2)}) %collective-permute-start.3) | collective-permute-done | bytes 118816 | tf_op jit(solution)/shard_map/ppermute | solution.py:402
  18.0 0.1 collective-permute-start.4
  18.1 3.5 %shard_map.144.refs_3_ = bf16[2048,2048]{1,0:T(8,128)(2,1)S(1)} custom-call(bf16[7168,2048]{1,0:T(8,128)(2,1)} %refs_5_.1), custom_call_target="tpu_custom_call" | custom-call | bytes 8388608 | tf_op jit(solution)/shard_map/pallas_call | solution.py:391
  21.6 3.5 %shard_map.145.refs_4_ = bf16[2048,2048]{1,0:T(8,128)(2,1)S(1)} custom-call(bf16[7168,2048]{1,0:T(8,128)(2,1)} %refs_5_.1), custom_call_target="tpu_custom_call" | custom-call | bytes 8388608 | tf_op jit(solution)/shard_map/pallas_call | solution.py:391
  25.1 0.0 copy-start
  25.1 0.0 copy-start.1
  25.2 0.0 copy-start.3
  25.2 0.0 copy-start.4
  25.2 0.0 copy-start.2
  25.2 22.8 %shard_map.146 = (f32[8,7168]{1,0:T(8,128)S(1)}, bf16[8,7168]{1,0:T(8,128)(2,1)S(1)}, bf16[8,7168]{1,0:T(8,128)(2,1)S(1)}, bf16[8,7168]{1,0:T(8,128)(2,1)S(1)}, ...) custom-call(s32[1]{0:T(128)} %bitcast.me_ref.refs_0_, bf16[16,7424]{1,0:T(8,128)(2,1)S(1)} %shard_map.143.refs_1_, ...), custom_call_target="tpu_custom_call" | custom-call | flops 2818572288 | bytes 88080384 | tf_op jit(solution)/shard_map/pallas_call | solution.py:423
  48.0 0.6 collective-permute-start.5
  48.5 1.0 %collective-permute-done.5.far_ref = bf16[8,16,576]{2,1,0:T(8,128)(2,1)S(1)} collective-permute-done((bf16[8,16,576]{2,1,0:T(8,128)(2,1)S(1)}, bf16[8,16,576]{2,1,0:T(8,128)(2,1)S(1)}, u32[]{:S(2)}, u32[]{:S(2)}) %collective-permute-start.5) | collective-permute-done | bytes 147488 | tf_op jit(solution)/shard_map/ppermute | solution.py:32
  49.6 0.8 %shard_map.147 = bf16[8,16,1152]{2,1,0:T(8,128)(2,1)} custom-call(bf16[8,16,576]{2,1,0:T(8,128)(2,1)S(1)} %get-tuple-element.20.near_ref, bf16[8,16,576]{2,1,0:T(8,128)(2,1)S(1)} %collective-permute-done.5.far_ref), custom_call_target="tpu_custom_call" | custom-call | tf_op jit(solution)/shard_map/pallas_call | solution.py:462
  50.4 3.4 %all-to-all-start = ((bf16[8,16,1152]{2,1,0:T(8,128)(2,1)}), bf16[8,16,1152]{2,1,0:T(8,128)(2,1)S(1)}, u32[]{:S(2)}, u32[]{:S(2)}) async-start(bf16[8,16,1152]{2,1,0:T(8,128)(2,1)} %shard_map.147), calls=%async_computation | async-start | bytes 589824 | tf_op jit(solution)/shard_map/all_to_all | solution.py:469
  53.8 1.9 %collective-permute-start.6 = (bf16[8,7168]{1,0:T(8,128)(2,1)S(1)}, bf16[8,7168]{1,0:T(8,128)(2,1)S(1)}, u32[]{:S(2)}, u32[]{:S(2)}) collective-permute-start(bf16[8,7168]{1,0:T(8,128)(2,1)S(1)} %get-tuple-element.23), channel_id=1, source_target_pairs={{0,1},{1,0},{2,3},{3,2},{4,5},{5,4},{6,7},{7,6},{8,9},{9,8},{10,11... | collective-permute-start | bytes 344072 | tf_op jit(solution)/shard_map/ppermute | solution.py:460
  55.7 0.3 collective-permute-start.8
  56.0 6.4 %collective-permute-done.6.refs_1_ = bf16[8,7168]{1,0:T(8,128)(2,1)S(1)} collective-permute-done((bf16[8,7168]{1,0:T(8,128)(2,1)S(1)}, bf16[8,7168]{1,0:T(8,128)(2,1)S(1)}, u32[]{:S(2)}, u32[]{:S(2)}) %collective-permute-start.6) | collective-permute-done | bytes 114720 | tf_op jit(solution)/shard_map/ppermute | solution.py:460
  62.4 1.9 %collective-permute-done.8.refs_3_ = bf16[8,7168]{1,0:T(8,128)(2,1)S(1)} collective-permute-done((bf16[8,7168]{1,0:T(8,128)(2,1)S(1)}, bf16[8,7168]{1,0:T(8,128)(2,1)S(1)}, u32[]{:S(2)}, u32[]{:S(2)}) %collective-permute-start.8) | collective-permute-done | bytes 114720 | tf_op jit(solution)/shard_map/ppermute | solution.py:460
  64.3 0.2 shard_map.148
  64.6 2.8 %collective-permute-start.10 = (bf16[2,7168]{1,0:T(2,128)(2,1)S(1)}, bf16[2,7168]{1,0:T(2,128)(2,1)S(1)}, u32[]{:S(2)}, u32[]{:S(2)}) collective-permute-start(bf16[2,7168]{1,0:T(2,128)(2,1)S(1)} %get-tuple-element.28), channel_id=1, source_target_pairs={{0,4},{1,5},{2,6},{3,7},{4,0},{5,1},{6,2},{7,3},{8,12},{9,13},{10,... | collective-permute-start | bytes 86024 | tf_op jit(solution)/shard_map/ppermute | solution.py:402
  67.4 1.1 %collective-permute-start.11 = (bf16[2,7168]{1,0:T(2,128)(2,1)S(1)}, bf16[2,7168]{1,0:T(2,128)(2,1)S(1)}, u32[]{:S(2)}, u32[]{:S(2)}) collective-permute-start(bf16[2,7168]{1,0:T(2,128)(2,1)S(1)} %get-tuple-element.29), channel_id=1, source_target_pairs={{0,6},{1,7},{2,4},{3,5},{4,2},{5,3},{6,0},{7,1},{8,14},{9,15},{10,... | collective-permute-start | bytes 86024 | tf_op jit(solution)/shard_map/ppermute | solution.py:402
  68.5 0.1 collective-permute-start.9
  68.6 1.2 %shard_map.140 = (f32[128,256]{1,0:T(8,128)S(1)}, f32[128,1]{1,0:T(8,128)S(1)}, f32[128,1]{1,0:T(8,128)S(1)}, f32[128,512]{1,0:T(8,128)S(1)}) custom-call(s32[1]{0:T(128)} %bitcast.me_ref.refs_0_, s32[2]{0:T(128)S(1)} %copy-done.3, s32[1,16]{1,0:T(1,128)S(1)} %copy-done.4, bf16[2,64,576]{2,1,0:T(8,128)(2,1)S(1)} %copy-done, bf16[2,64,576]{2,1,0:T(8,128)(2,1)S(1)} %copy-done.1), custom_call_target="tpu_custom_call" | custom-call | tf_op jit(solution)/shard_map/pallas_call | solution.py:482
  69.8 3.2 %collective-permute-done.11.refs_2_ = bf16[2,7168]{1,0:T(2,128)(2,1)S(1)} collective-permute-done((bf16[2,7168]{1,0:T(2,128)(2,1)S(1)}, bf16[2,7168]{1,0:T(2,128)(2,1)S(1)}, u32[]{:S(2)}, u32[]{:S(2)}) %collective-permute-start.11) | collective-permute-done | bytes 28704 | tf_op jit(solution)/shard_map/ppermute | solution.py:402
  73.1 1.4 %shard_map.149 = (bf16[2,64,512]{2,1,0:T(8,128)(2,1)}, bf16[2,7168]{1,0:T(2,128)(2,1)}) custom-call(f32[128,256]{1,0:T(8,128)S(1)} %get-tuple-element.16.bias_ref, f32[128,1]{1,0:T(8,128)S(1)} %get-tuple-element.17.peak_ref, f32[128,1]{1,0:T(8,128)S(1)} %get-tuple-element.18.sum_ref, f32[128,512]{1,0:T(8,128)S(1)} %get-tuple-element.19.part_ref, ...), custom_call_target="tpu_custom_call" | custom-call | tf_op jit(solution)/shard_map/pallas_call | solution.py:495
  (14 shorter events, 0.0 us)
Async XLA Ops:
  1.6 5.7 %collective-permute-start = (bf16[2,7424]{1,0:T(2,128)(2,1)S(1)}, bf16[2,7424]{1,0:T(2,128)(2,1)S(1)}, u32[]{:S(2)}, u32[]{:S(2)}) collective-permute-start(bf16[2,7424]{1,0:T(2,128)(2,1)S(1)} %shard_map.141.refs_0_), channel_id=1, source_target_pairs={{0,2},{1,3},{2,0},{3,1},{4,6},{5,7},{6,4},{7,5},{8,10},{9,11},{10,... | collective-permute-start | bytes 89096 | tf_op jit(solution)/shard_map/ppermute | solution.py:402
  4.7 5.3 %collective-permute-start.1 = (bf16[2,7424]{1,0:T(2,128)(2,1)S(1)}, bf16[2,7424]{1,0:T(2,128)(2,1)S(1)}, u32[]{:S(2)}, u32[]{:S(2)}) collective-permute-start(bf16[2,7424]{1,0:T(2,128)(2,1)S(1)} %shard_map.141.refs_0_), channel_id=1, source_target_pairs={{0,4},{1,5},{2,6},{3,7},{4,0},{5,1},{6,2},{7,3},{8,12},{9,13},{10,... | collective-permute-start | bytes 89096 | tf_op jit(solution)/shard_map/ppermute | solution.py:402
  7.3 5.7 %collective-permute-start.2 = (bf16[2,7424]{1,0:T(2,128)(2,1)S(1)}, bf16[2,7424]{1,0:T(2,128)(2,1)S(1)}, u32[]{:S(2)}, u32[]{:S(2)}) collective-permute-start(bf16[2,7424]{1,0:T(2,128)(2,1)S(1)} %shard_map.141.refs_0_), channel_id=1, source_target_pairs={{0,6},{1,7},{2,4},{3,5},{4,2},{5,3},{6,0},{7,1},{8,14},{9,15},{10,... | collective-permute-start | bytes 89096 | tf_op jit(solution)/shard_map/ppermute | solution.py:402
  13.1 4.9 %collective-permute-start.3 = (bf16[8,7424]{1,0:T(8,128)(2,1)S(1)}, bf16[8,7424]{1,0:T(8,128)(2,1)S(1)}, u32[]{:S(2)}, u32[]{:S(2)}) collective-permute-start(bf16[8,7424]{1,0:T(8,128)(2,1)S(1)} %shard_map.142.refs_0_), channel_id=1, source_target_pairs={{0,1},{1,0},{2,3},{3,2},{4,5},{5,4},{6,7},{7,6},{8,9},{9,8},{10,11... | collective-permute-start | bytes 356360 | tf_op jit(solution)/shard_map/ppermute | solution.py:402
  18.0 7.2 %collective-permute-start.4 = (bf16[16,7424]{1,0:T(8,128)(2,1)S(1)}, bf16[16,7424]{1,0:T(8,128)(2,1)S(1)}, u32[]{:S(2)}, u32[]{:S(2)}) collective-permute-start(bf16[16,7424]{1,0:T(8,128)(2,1)S(1)} %shard_map.143.refs_1_), channel_id=1, source_target_pairs={{0,8},{8,0},{1,9},{9,1},{2,10},{10,2},{3,11},{11,3},{4,12},{12,4},... | collective-permute-start | bytes 712712 | tf_op jit(solution)/shard_map/ppermute | solution.py:32
  25.1 43.5 %copy-start = (bf16[2,64,576]{2,1,0:T(8,128)(2,1)S(1)}, bf16[2,64,576]{2,1,0:T(8,128)(2,1)}, u32[]{:S(2)}) copy-start(bf16[2,64,576]{2,1,0:T(8,128)(2,1)} %q_ref.3) | copy-start | bytes 442372
  25.1 43.5 %copy-start.1 = (bf16[2,64,576]{2,1,0:T(8,128)(2,1)S(1)}, bf16[2,64,576]{2,1,0:T(8,128)(2,1)}, u32[]{:S(2)}) copy-start(bf16[2,64,576]{2,1,0:T(8,128)(2,1)} %local_ref.1) | copy-start | bytes 442372
  25.2 43.5 %copy-start.3 = (s32[2]{0:T(128)S(1)}, s32[2]{0:T(128)}, u32[]{:S(2)}) copy-start(s32[2]{0:T(128)} %len_ref.1) | copy-start | bytes 28
  25.2 43.5 %copy-start.4 = (s32[1,16]{1,0:T(1,128)S(1)}, s32[1,16]{1,0:T(1,128)}, u32[]{:S(2)}) copy-start(s32[1,16]{1,0:T(1,128)} %owner_ref.1) | copy-start | bytes 196
  25.2 47.9 %copy-start.2 = (bf16[2,7168]{1,0:T(2,128)(2,1)S(1)}, bf16[2,7168]{1,0:T(2,128)(2,1)}, u32[]{:S(2)}) copy-start(bf16[2,7168]{1,0:T(2,128)(2,1)} %hid_ref.3) | copy-start | bytes 86020
  48.0 1.6 %collective-permute-start.5 = (bf16[8,16,576]{2,1,0:T(8,128)(2,1)S(1)}, bf16[8,16,576]{2,1,0:T(8,128)(2,1)S(1)}, u32[]{:S(2)}, u32[]{:S(2)}) collective-permute-start(bf16[8,16,576]{2,1,0:T(8,128)(2,1)S(1)} %get-tuple-element.21), channel_id=1, source_target_pairs={{0,8},{8,0},{1,9},{9,1},{2,10},{10,2},{3,11},{11,3},{4,12},{12,4},... | collective-permute-start | bytes 442376 | tf_op jit(solution)/shard_map/ppermute | solution.py:32
  50.4 22.7 %all-to-all-start = ((bf16[8,16,1152]{2,1,0:T(8,128)(2,1)}), bf16[8,16,1152]{2,1,0:T(8,128)(2,1)S(1)}, u32[]{:S(2)}, u32[]{:S(2)}) async-start(bf16[8,16,1152]{2,1,0:T(8,128)(2,1)} %shard_map.147), calls=%async_computation | async-start | bytes 589824 | tf_op jit(solution)/shard_map/all_to_all | solution.py:469
  53.8 8.6 %collective-permute-start.6 = (bf16[8,7168]{1,0:T(8,128)(2,1)S(1)}, bf16[8,7168]{1,0:T(8,128)(2,1)S(1)}, u32[]{:S(2)}, u32[]{:S(2)}) collective-permute-start(bf16[8,7168]{1,0:T(8,128)(2,1)S(1)} %get-tuple-element.23), channel_id=1, source_target_pairs={{0,1},{1,0},{2,3},{3,2},{4,5},{5,4},{6,7},{7,6},{8,9},{9,8},{10,11... | collective-permute-start | bytes 344072 | tf_op jit(solution)/shard_map/ppermute | solution.py:460
  55.7 6.7 %collective-permute-start.7 = (bf16[8,7168]{1,0:T(8,128)(2,1)S(1)}, bf16[8,7168]{1,0:T(8,128)(2,1)S(1)}, u32[]{:S(2)}, u32[]{:S(2)}) collective-permute-start(bf16[8,7168]{1,0:T(8,128)(2,1)S(1)} %get-tuple-element.24), channel_id=1, source_target_pairs={{0,8},{1,9},{2,10},{3,11},{4,12},{5,13},{6,14},{7,15},{8,0},{9,1},... | collective-permute-start | bytes 344072 | tf_op jit(solution)/shard_map/ppermute | solution.py:460
  55.7 8.6 %collective-permute-start.8 = (bf16[8,7168]{1,0:T(8,128)(2,1)S(1)}, bf16[8,7168]{1,0:T(8,128)(2,1)S(1)}, u32[]{:S(2)}, u32[]{:S(2)}) collective-permute-start(bf16[8,7168]{1,0:T(8,128)(2,1)S(1)} %get-tuple-element.25), channel_id=1, source_target_pairs={{0,9},{1,8},{2,11},{3,10},{4,13},{5,12},{6,15},{7,14},{8,1},{9,0},... | collective-permute-start | bytes 344072 | tf_op jit(solution)/shard_map/ppermute | solution.py:460
  64.6 5.2 %collective-permute-start.10 = (bf16[2,7168]{1,0:T(2,128)(2,1)S(1)}, bf16[2,7168]{1,0:T(2,128)(2,1)S(1)}, u32[]{:S(2)}, u32[]{:S(2)}) collective-permute-start(bf16[2,7168]{1,0:T(2,128)(2,1)S(1)} %get-tuple-element.28), channel_id=1, source_target_pairs={{0,4},{1,5},{2,6},{3,7},{4,0},{5,1},{6,2},{7,3},{8,12},{9,13},{10,... | collective-permute-start | bytes 86024 | tf_op jit(solution)/shard_map/ppermute | solution.py:402
  67.4 5.7 %collective-permute-start.11 = (bf16[2,7168]{1,0:T(2,128)(2,1)S(1)}, bf16[2,7168]{1,0:T(2,128)(2,1)S(1)}, u32[]{:S(2)}, u32[]{:S(2)}) collective-permute-start(bf16[2,7168]{1,0:T(2,128)(2,1)S(1)} %get-tuple-element.29), channel_id=1, source_target_pairs={{0,6},{1,7},{2,4},{3,5},{4,2},{5,3},{6,0},{7,1},{8,14},{9,15},{10,... | collective-permute-start | bytes 86024 | tf_op jit(solution)/shard_map/ppermute | solution.py:402
  68.5 4.6 %collective-permute-start.9 = (bf16[2,7168]{1,0:T(2,128)(2,1)S(1)}, bf16[2,7168]{1,0:T(2,128)(2,1)S(1)}, u32[]{:S(2)}, u32[]{:S(2)}) collective-permute-start(bf16[2,7168]{1,0:T(2,128)(2,1)S(1)} %get-tuple-element.27), channel_id=1, source_target_pairs={{0,2},{1,3},{2,0},{3,1},{4,6},{5,7},{6,4},{7,5},{8,10},{9,11},{10,... | collective-permute-start | bytes 86024 | tf_op jit(solution)/shard_map/ppermute | solution.py:402

commit v6 on v5

--- a/solution.py
+++ b/solution.py
@@ -269,12 +269,19 @@
             keep_ref[...] = block(place)
 
 
-def stack_kernel(near_ref, far_ref, out_ref):
-    width = near_ref.shape[2]
-    value = width - ROPE
+def stack_kernel(near_ref, far_ref, out_ref, thin, sems):
+    value = near_ref.shape[2] - ROPE
+    copies = []
     for n, ref in enumerate((near_ref, far_ref)):
-        out_ref[:, :, n * value : (n + 1) * value] = ref[:, :, :value]
-        out_ref[:, :, 2 * value + n * ROPE : 2 * value + (n + 1) * ROPE] = ref[:, :, value:]
+        target = out_ref.at[:, :, n * value : (n + 1) * value]
+        copies.append(pltpu.make_async_copy(ref.at[:, :, :value], target, sems.at[n]))
+        copies[-1].start()
+    for n, ref in enumerate((near_ref, far_ref)):
+        thin[:, :, n * ROPE : (n + 1) * ROPE] = ref[:, :, value:]
+    copies.append(pltpu.make_async_copy(thin, out_ref.at[:, :, 2 * value :], sems.at[2]))
+    copies[-1].start()
+    for c in copies:
+        c.wait()
 
 
 def early_kernel(me_ref, len_ref, owner_ref, q_ref, local_ref, bias_ref, peak_ref, sum_ref, part_ref):
@@ -463,7 +470,11 @@
         stack_kernel,
         out_shape=jax.ShapeDtypeStruct(page_shape, jnp.bfloat16),
         in_specs=[VM, VM],
-        out_specs=VM,
+        out_specs=HBM,
+        scratch_shapes=[
+            pltpu.VMEM((dev_size, swap_pool.shape[1], 2 * ROPE), jnp.bfloat16),
+            pltpu.SemaphoreType.DMA((3,)),
+        ],
         compiler_params=pltpu.CompilerParams(vmem_limit_bytes=8 << 20),
     )(near, far)
     arrived = lax.all_to_all(outgoing, "dev", split_axis=0, concat_axis=0, tiled=True)

time: 74.8 us -> 74.8 us (level)
  no operation moved by 1% of the time
where the time goes in v6:
time: 74.8 us; the launch traced here: 74.5 us
  Pallas kernels  34.5 us (46%)
  waiting for transfers between devices  21.6 us (29%)
  starting transfers between devices  17.6 us (24%)
  between operations  0.8 us (1%)
    pallas_call x1, Pallas kernels, per_device(): pl.pallas_call(functools.partial(expert_kernel, tk=tk, tn=tn, base=width...  22.8 us
    ppermute x7, waiting for transfers between devices, swap(): lax.ppermute(value, 'dev', [(i, i ^ offset) for i in range(dev_size)])  12.2 us
    ppermute x7, starting transfers between devices, swap(): lax.ppermute(value, 'dev', [(i, i ^ offset) for i in range(dev_size)])  11.3 us
    ppermute x3, waiting for transfers between devices, per_device(): lax.ppermute(value, ('role', 'dev'), [(i, i ^ flat) for i in range(device...  8.32 us
    pallas_call x2, Pallas kernels, load(): pl.pallas_call(functools.partial(load_kernel, start=start), out_shape=plt...  7.01 us
    all_to_all x1, starting transfers between devices, per_device(): lax.all_to_all(outgoing, 'dev', split_axis=0, concat_axis=0, tiled=True)  3.43 us
    ppermute x3, starting transfers between devices, per_device(): lax.ppermute(value, ('role', 'dev'), [(i, i ^ flat) for i in range(device...  2.21 us
  transfers between devices with their start and end apart: 13, of which 7 were waited for; matrix products, arithmetic and copies ran while one was open for 0% of the time, Pallas kernels for 11%

profile of v6, /device:TPU:0, one launch (start us, length us, event | category | flops | bytes accessed | tf_op | source)
XLA Modules:
  0.0 74.5 jit_solution(85139115621820858)
XLA Ops:
  0.6 1.0 %shard_map.141.refs_0_ = bf16[2,7424]{1,0:T(2,128)(2,1)S(1)} custom-call(s32[1]{0:T(128)} %bitcast.me_ref.refs_0_, bf16[2,7168]{1,0:T(2,128)(2,1)} %hid_ref.3, bf16[7168]{0:T(1024)(128)(2,1)} %gain_ref.1, s32[2,8]{1,0:T(2,128)} %routes_ref.1, f32[2,8]{1,0:T(2,128)} %weights_ref.1, s32[1,16]{1,0:T(1,128)} %ids_ref.1), custom_call_target="tpu_custom_call" | custom-call | tf_op jit(solution)/shard_map/pallas_call | solution.py:380
  1.6 3.1 %collective-permute-start = (bf16[2,7424]{1,0:T(2,128)(2,1)S(1)}, bf16[2,7424]{1,0:T(2,128)(2,1)S(1)}, u32[]{:S(2)}, u32[]{:S(2)}) collective-permute-start(bf16[2,7424]{1,0:T(2,128)(2,1)S(1)} %shard_map.141.refs_0_), channel_id=1, source_target_pairs={{0,2},{1,3},{2,0},{3,1},{4,6},{5,7},{6,4},{7,5},{8,10},{9,11},{10,... | collective-permute-start | bytes 89096 | tf_op jit(solution)/shard_map/ppermute | solution.py:409
  4.7 2.6 %collective-permute-start.1 = (bf16[2,7424]{1,0:T(2,128)(2,1)S(1)}, bf16[2,7424]{1,0:T(2,128)(2,1)S(1)}, u32[]{:S(2)}, u32[]{:S(2)}) collective-permute-start(bf16[2,7424]{1,0:T(2,128)(2,1)S(1)} %shard_map.141.refs_0_), channel_id=1, source_target_pairs={{0,4},{1,5},{2,6},{3,7},{4,0},{5,1},{6,2},{7,3},{8,12},{9,13},{10,... | collective-permute-start | bytes 89096 | tf_op jit(solution)/shard_map/ppermute | solution.py:409
  7.3 2.7 %collective-permute-done.1.refs_2_ = bf16[2,7424]{1,0:T(2,128)(2,1)S(1)} collective-permute-done((bf16[2,7424]{1,0:T(2,128)(2,1)S(1)}, bf16[2,7424]{1,0:T(2,128)(2,1)S(1)}, u32[]{:S(2)}, u32[]{:S(2)}) %collective-permute-start.1) | collective-permute-done | bytes 29728 | tf_op jit(solution)/shard_map/ppermute | solution.py:409
  10.0 3.0 %collective-permute-done.2.refs_3_ = bf16[2,7424]{1,0:T(2,128)(2,1)S(1)} collective-permute-done((bf16[2,7424]{1,0:T(2,128)(2,1)S(1)}, bf16[2,7424]{1,0:T(2,128)(2,1)S(1)}, u32[]{:S(2)}, u32[]{:S(2)}) %collective-permute-start.2) | collective-permute-done | bytes 29728 | tf_op jit(solution)/shard_map/ppermute | solution.py:409
  13.0 0.1 shard_map.142.refs_0_
  13.1 1.6 %collective-permute-start.3 = (bf16[8,7424]{1,0:T(8,128)(2,1)S(1)}, bf16[8,7424]{1,0:T(8,128)(2,1)S(1)}, u32[]{:S(2)}, u32[]{:S(2)}) collective-permute-start(bf16[8,7424]{1,0:T(8,128)(2,1)S(1)} %shard_map.142.refs_0_), channel_id=1, source_target_pairs={{0,1},{1,0},{2,3},{3,2},{4,5},{5,4},{6,7},{7,6},{8,9},{9,8},{10,11... | collective-permute-start | bytes 356360 | tf_op jit(solution)/shard_map/ppermute | solution.py:409
  14.7 3.3 %collective-permute-done.3.refs_1_ = bf16[8,7424]{1,0:T(8,128)(2,1)S(1)} collective-permute-done((bf16[8,7424]{1,0:T(8,128)(2,1)S(1)}, bf16[8,7424]{1,0:T(8,128)(2,1)S(1)}, u32[]{:S(2)}, u32[]{:S(2)}) %collective-permute-start.3) | collective-permute-done | bytes 118816 | tf_op jit(solution)/shard_map/ppermute | solution.py:409
  18.0 0.1 collective-permute-start.4
  18.1 3.5 %shard_map.144.refs_3_ = bf16[2048,2048]{1,0:T(8,128)(2,1)S(1)} custom-call(bf16[7168,2048]{1,0:T(8,128)(2,1)} %refs_5_.1), custom_call_target="tpu_custom_call" | custom-call | bytes 8388608 | tf_op jit(solution)/shard_map/pallas_call | solution.py:398
  21.6 3.5 %shard_map.145.refs_4_ = bf16[2048,2048]{1,0:T(8,128)(2,1)S(1)} custom-call(bf16[7168,2048]{1,0:T(8,128)(2,1)} %refs_5_.1), custom_call_target="tpu_custom_call" | custom-call | bytes 8388608 | tf_op jit(solution)/shard_map/pallas_call | solution.py:398
  25.1 0.0 copy-start
  25.1 0.0 copy-start.1
  25.2 0.0 copy-start.3
  25.2 0.0 copy-start.4
  25.2 0.0 copy-start.2
  25.2 22.8 %shard_map.146 = (f32[8,7168]{1,0:T(8,128)S(1)}, bf16[8,7168]{1,0:T(8,128)(2,1)S(1)}, bf16[8,7168]{1,0:T(8,128)(2,1)S(1)}, bf16[8,7168]{1,0:T(8,128)(2,1)S(1)}, ...) custom-call(s32[1]{0:T(128)} %bitcast.me_ref.refs_0_, bf16[16,7424]{1,0:T(8,128)(2,1)S(1)} %shard_map.143.refs_1_, ...), custom_call_target="tpu_custom_call" | custom-call | flops 2818572288 | bytes 88080384 | tf_op jit(solution)/shard_map/pallas_call | solution.py:430
  48.0 0.6 collective-permute-start.5
  48.5 1.0 %collective-permute-done.5.far_ref = bf16[8,16,576]{2,1,0:T(8,128)(2,1)S(1)} collective-permute-done((bf16[8,16,576]{2,1,0:T(8,128)(2,1)S(1)}, bf16[8,16,576]{2,1,0:T(8,128)(2,1)S(1)}, u32[]{:S(2)}, u32[]{:S(2)}) %collective-permute-start.5) | collective-permute-done | bytes 147488 | tf_op jit(solution)/shard_map/ppermute | solution.py:32
  49.6 0.8 %shard_map.147 = bf16[8,16,1152]{2,1,0:T(8,128)(2,1)} custom-call(bf16[8,16,576]{2,1,0:T(8,128)(2,1)S(1)} %get-tuple-element.20.near_ref, bf16[8,16,576]{2,1,0:T(8,128)(2,1)S(1)} %collective-permute-done.5.far_ref), custom_call_target="tpu_custom_call" | custom-call | tf_op jit(solution)/shard_map/pallas_call | solution.py:469
  50.4 3.4 %all-to-all-start = ((bf16[8,16,1152]{2,1,0:T(8,128)(2,1)}), bf16[8,16,1152]{2,1,0:T(8,128)(2,1)S(1)}, u32[]{:S(2)}, u32[]{:S(2)}) async-start(bf16[8,16,1152]{2,1,0:T(8,128)(2,1)} %shard_map.147), calls=%async_computation | async-start | bytes 589824 | tf_op jit(solution)/shard_map/all_to_all | solution.py:480
  53.8 1.9 %collective-permute-start.6 = (bf16[8,7168]{1,0:T(8,128)(2,1)S(1)}, bf16[8,7168]{1,0:T(8,128)(2,1)S(1)}, u32[]{:S(2)}, u32[]{:S(2)}) collective-permute-start(bf16[8,7168]{1,0:T(8,128)(2,1)S(1)} %get-tuple-element.23), channel_id=1, source_target_pairs={{0,1},{1,0},{2,3},{3,2},{4,5},{5,4},{6,7},{7,6},{8,9},{9,8},{10,11... | collective-permute-start | bytes 344072 | tf_op jit(solution)/shard_map/ppermute | solution.py:467
  55.7 0.3 collective-permute-start.8
  56.0 6.4 %collective-permute-done.6.refs_1_ = bf16[8,7168]{1,0:T(8,128)(2,1)S(1)} collective-permute-done((bf16[8,7168]{1,0:T(8,128)(2,1)S(1)}, bf16[8,7168]{1,0:T(8,128)(2,1)S(1)}, u32[]{:S(2)}, u32[]{:S(2)}) %collective-permute-start.6) | collective-permute-done | bytes 114720 | tf_op jit(solution)/shard_map/ppermute | solution.py:467
  62.4 1.9 %collective-permute-done.8.refs_3_ = bf16[8,7168]{1,0:T(8,128)(2,1)S(1)} collective-permute-done((bf16[8,7168]{1,0:T(8,128)(2,1)S(1)}, bf16[8,7168]{1,0:T(8,128)(2,1)S(1)}, u32[]{:S(2)}, u32[]{:S(2)}) %collective-permute-start.8) | collective-permute-done | bytes 114720 | tf_op jit(solution)/shard_map/ppermute | solution.py:467
  64.3 0.2 shard_map.148
  64.6 2.8 %collective-permute-start.10 = (bf16[2,7168]{1,0:T(2,128)(2,1)S(1)}, bf16[2,7168]{1,0:T(2,128)(2,1)S(1)}, u32[]{:S(2)}, u32[]{:S(2)}) collective-permute-start(bf16[2,7168]{1,0:T(2,128)(2,1)S(1)} %get-tuple-element.28), channel_id=1, source_target_pairs={{0,4},{1,5},{2,6},{3,7},{4,0},{5,1},{6,2},{7,3},{8,12},{9,13},{10,... | collective-permute-start | bytes 86024 | tf_op jit(solution)/shard_map/ppermute | solution.py:409
  67.4 1.1 %collective-permute-start.11 = (bf16[2,7168]{1,0:T(2,128)(2,1)S(1)}, bf16[2,7168]{1,0:T(2,128)(2,1)S(1)}, u32[]{:S(2)}, u32[]{:S(2)}) collective-permute-start(bf16[2,7168]{1,0:T(2,128)(2,1)S(1)} %get-tuple-element.29), channel_id=1, source_target_pairs={{0,6},{1,7},{2,4},{3,5},{4,2},{5,3},{6,0},{7,1},{8,14},{9,15},{10,... | collective-permute-start | bytes 86024 | tf_op jit(solution)/shard_map/ppermute | solution.py:409
  68.5 0.1 collective-permute-start.9
  68.6 1.2 %shard_map.140 = (f32[128,256]{1,0:T(8,128)S(1)}, f32[128,1]{1,0:T(8,128)S(1)}, f32[128,1]{1,0:T(8,128)S(1)}, f32[128,512]{1,0:T(8,128)S(1)}) custom-call(s32[1]{0:T(128)} %bitcast.me_ref.refs_0_, s32[2]{0:T(128)S(1)} %copy-done.3, s32[1,16]{1,0:T(1,128)S(1)} %copy-done.4, bf16[2,64,576]{2,1,0:T(8,128)(2,1)S(1)} %copy-done, bf16[2,64,576]{2,1,0:T(8,128)(2,1)S(1)} %copy-done.1), custom_call_target="tpu_custom_call" | custom-call | tf_op jit(solution)/shard_map/pallas_call | solution.py:493
  69.8 3.2 %collective-permute-done.11.refs_2_ = bf16[2,7168]{1,0:T(2,128)(2,1)S(1)} collective-permute-done((bf16[2,7168]{1,0:T(2,128)(2,1)S(1)}, bf16[2,7168]{1,0:T(2,128)(2,1)S(1)}, u32[]{:S(2)}, u32[]{:S(2)}) %collective-permute-start.11) | collective-permute-done | bytes 28704 | tf_op jit(solution)/shard_map/ppermute | solution.py:409
  73.0 1.4 %shard_map.149 = (bf16[2,64,512]{2,1,0:T(8,128)(2,1)}, bf16[2,7168]{1,0:T(2,128)(2,1)}) custom-call(f32[128,256]{1,0:T(8,128)S(1)} %get-tuple-element.16.bias_ref, f32[128,1]{1,0:T(8,128)S(1)} %get-tuple-element.17.peak_ref, f32[128,1]{1,0:T(8,128)S(1)} %get-tuple-element.18.sum_ref, f32[128,512]{1,0:T(8,128)S(1)} %get-tuple-element.19.part_ref, ...), custom_call_target="tpu_custom_call" | custom-call | tf_op jit(solution)/shard_map/pallas_call | solution.py:506
  (14 shorter events, 0.0 us)
Async XLA Ops:
  1.6 5.7 %collective-permute-start = (bf16[2,7424]{1,0:T(2,128)(2,1)S(1)}, bf16[2,7424]{1,0:T(2,128)(2,1)S(1)}, u32[]{:S(2)}, u32[]{:S(2)}) collective-permute-start(bf16[2,7424]{1,0:T(2,128)(2,1)S(1)} %shard_map.141.refs_0_), channel_id=1, source_target_pairs={{0,2},{1,3},{2,0},{3,1},{4,6},{5,7},{6,4},{7,5},{8,10},{9,11},{10,... | collective-permute-start | bytes 89096 | tf_op jit(solution)/shard_map/ppermute | solution.py:409
  4.7 5.3 %collective-permute-start.1 = (bf16[2,7424]{1,0:T(2,128)(2,1)S(1)}, bf16[2,7424]{1,0:T(2,128)(2,1)S(1)}, u32[]{:S(2)}, u32[]{:S(2)}) collective-permute-start(bf16[2,7424]{1,0:T(2,128)(2,1)S(1)} %shard_map.141.refs_0_), channel_id=1, source_target_pairs={{0,4},{1,5},{2,6},{3,7},{4,0},{5,1},{6,2},{7,3},{8,12},{9,13},{10,... | collective-permute-start | bytes 89096 | tf_op jit(solution)/shard_map/ppermute | solution.py:409
  7.3 5.7 %collective-permute-start.2 = (bf16[2,7424]{1,0:T(2,128)(2,1)S(1)}, bf16[2,7424]{1,0:T(2,128)(2,1)S(1)}, u32[]{:S(2)}, u32[]{:S(2)}) collective-permute-start(bf16[2,7424]{1,0:T(2,128)(2,1)S(1)} %shard_map.141.refs_0_), channel_id=1, source_target_pairs={{0,6},{1,7},{2,4},{3,5},{4,2},{5,3},{6,0},{7,1},{8,14},{9,15},{10,... | collective-permute-start | bytes 89096 | tf_op jit(solution)/shard_map/ppermute | solution.py:409
  13.1 4.9 %collective-permute-start.3 = (bf16[8,7424]{1,0:T(8,128)(2,1)S(1)}, bf16[8,7424]{1,0:T(8,128)(2,1)S(1)}, u32[]{:S(2)}, u32[]{:S(2)}) collective-permute-start(bf16[8,7424]{1,0:T(8,128)(2,1)S(1)} %shard_map.142.refs_0_), channel_id=1, source_target_pairs={{0,1},{1,0},{2,3},{3,2},{4,5},{5,4},{6,7},{7,6},{8,9},{9,8},{10,11... | collective-permute-start | bytes 356360 | tf_op jit(solution)/shard_map/ppermute | solution.py:409
  18.0 7.2 %collective-permute-start.4 = (bf16[16,7424]{1,0:T(8,128)(2,1)S(1)}, bf16[16,7424]{1,0:T(8,128)(2,1)S(1)}, u32[]{:S(2)}, u32[]{:S(2)}) collective-permute-start(bf16[16,7424]{1,0:T(8,128)(2,1)S(1)} %shard_map.143.refs_1_), channel_id=1, source_target_pairs={{0,8},{8,0},{1,9},{9,1},{2,10},{10,2},{3,11},{11,3},{4,12},{12,4},... | collective-permute-start | bytes 712712 | tf_op jit(solution)/shard_map/ppermute | solution.py:32
  25.1 43.5 %copy-start = (bf16[2,64,576]{2,1,0:T(8,128)(2,1)S(1)}, bf16[2,64,576]{2,1,0:T(8,128)(2,1)}, u32[]{:S(2)}) copy-start(bf16[2,64,576]{2,1,0:T(8,128)(2,1)} %q_ref.3) | copy-start | bytes 442372
  25.1 43.5 %copy-start.1 = (bf16[2,64,576]{2,1,0:T(8,128)(2,1)S(1)}, bf16[2,64,576]{2,1,0:T(8,128)(2,1)}, u32[]{:S(2)}) copy-start(bf16[2,64,576]{2,1,0:T(8,128)(2,1)} %local_ref.1) | copy-start | bytes 442372
  25.2 43.5 %copy-start.3 = (s32[2]{0:T(128)S(1)}, s32[2]{0:T(128)}, u32[]{:S(2)}) copy-start(s32[2]{0:T(128)} %len_ref.1) | copy-start | bytes 28
  25.2 43.5 %copy-start.4 = (s32[1,16]{1,0:T(1,128)S(1)}, s32[1,16]{1,0:T(1,128)}, u32[]{:S(2)}) copy-start(s32[1,16]{1,0:T(1,128)} %owner_ref.1) | copy-start | bytes 196
  25.2 47.9 %copy-start.2 = (bf16[2,7168]{1,0:T(2,128)(2,1)S(1)}, bf16[2,7168]{1,0:T(2,128)(2,1)}, u32[]{:S(2)}) copy-start(bf16[2,7168]{1,0:T(2,128)(2,1)} %hid_ref.3) | copy-start | bytes 86020
  48.0 1.6 %collective-permute-start.5 = (bf16[8,16,576]{2,1,0:T(8,128)(2,1)S(1)}, bf16[8,16,576]{2,1,0:T(8,128)(2,1)S(1)}, u32[]{:S(2)}, u32[]{:S(2)}) collective-permute-start(bf16[8,16,576]{2,1,0:T(8,128)(2,1)S(1)} %get-tuple-element.21), channel_id=1, source_target_pairs={{0,8},{8,0},{1,9},{9,1},{2,10},{10,2},{3,11},{11,3},{4,12},{12,4},... | collective-permute-start | bytes 442376 | tf_op jit(solution)/shard_map/ppermute | solution.py:32
  50.4 22.7 %all-to-all-start = ((bf16[8,16,1152]{2,1,0:T(8,128)(2,1)}), bf16[8,16,1152]{2,1,0:T(8,128)(2,1)S(1)}, u32[]{:S(2)}, u32[]{:S(2)}) async-start(bf16[8,16,1152]{2,1,0:T(8,128)(2,1)} %shard_map.147), calls=%async_computation | async-start | bytes 589824 | tf_op jit(solution)/shard_map/all_to_all | solution.py:480
  53.8 8.6 %collective-permute-start.6 = (bf16[8,7168]{1,0:T(8,128)(2,1)S(1)}, bf16[8,7168]{1,0:T(8,128)(2,1)S(1)}, u32[]{:S(2)}, u32[]{:S(2)}) collective-permute-start(bf16[8,7168]{1,0:T(8,128)(2,1)S(1)} %get-tuple-element.23), channel_id=1, source_target_pairs={{0,1},{1,0},{2,3},{3,2},{4,5},{5,4},{6,7},{7,6},{8,9},{9,8},{10,11... | collective-permute-start | bytes 344072 | tf_op jit(solution)/shard_map/ppermute | solution.py:467
  55.7 6.7 %collective-permute-start.7 = (bf16[8,7168]{1,0:T(8,128)(2,1)S(1)}, bf16[8,7168]{1,0:T(8,128)(2,1)S(1)}, u32[]{:S(2)}, u32[]{:S(2)}) collective-permute-start(bf16[8,7168]{1,0:T(8,128)(2,1)S(1)} %get-tuple-element.24), channel_id=1, source_target_pairs={{0,8},{1,9},{2,10},{3,11},{4,12},{5,13},{6,14},{7,15},{8,0},{9,1},... | collective-permute-start | bytes 344072 | tf_op jit(solution)/shard_map/ppermute | solution.py:467
  55.7 8.6 %collective-permute-start.8 = (bf16[8,7168]{1,0:T(8,128)(2,1)S(1)}, bf16[8,7168]{1,0:T(8,128)(2,1)S(1)}, u32[]{:S(2)}, u32[]{:S(2)}) collective-permute-start(bf16[8,7168]{1,0:T(8,128)(2,1)S(1)} %get-tuple-element.25), channel_id=1, source_target_pairs={{0,9},{1,8},{2,11},{3,10},{4,13},{5,12},{6,15},{7,14},{8,1},{9,0},... | collective-permute-start | bytes 344072 | tf_op jit(solution)/shard_map/ppermute | solution.py:467
  64.6 5.2 %collective-permute-start.10 = (bf16[2,7168]{1,0:T(2,128)(2,1)S(1)}, bf16[2,7168]{1,0:T(2,128)(2,1)S(1)}, u32[]{:S(2)}, u32[]{:S(2)}) collective-permute-start(bf16[2,7168]{1,0:T(2,128)(2,1)S(1)} %get-tuple-element.28), channel_id=1, source_target_pairs={{0,4},{1,5},{2,6},{3,7},{4,0},{5,1},{6,2},{7,3},{8,12},{9,13},{10,... | collective-permute-start | bytes 86024 | tf_op jit(solution)/shard_map/ppermute | solution.py:409
  67.4 5.7 %collective-permute-start.11 = (bf16[2,7168]{1,0:T(2,128)(2,1)S(1)}, bf16[2,7168]{1,0:T(2,128)(2,1)S(1)}, u32[]{:S(2)}, u32[]{:S(2)}) collective-permute-start(bf16[2,7168]{1,0:T(2,128)(2,1)S(1)} %get-tuple-element.29), channel_id=1, source_target_pairs={{0,6},{1,7},{2,4},{3,5},{4,2},{5,3},{6,0},{7,1},{8,14},{9,15},{10,... | collective-permute-start | bytes 86024 | tf_op jit(solution)/shard_map/ppermute | solution.py:409
  68.5 4.6 %collective-permute-start.9 = (bf16[2,7168]{1,0:T(2,128)(2,1)S(1)}, bf16[2,7168]{1,0:T(2,128)(2,1)S(1)}, u32[]{:S(2)}, u32[]{:S(2)}) collective-permute-start(bf16[2,7168]{1,0:T(2,128)(2,1)S(1)} %get-tuple-element.27), channel_id=1, source_target_pairs={{0,2},{1,3},{2,0},{3,1},{4,6},{5,7},{6,4},{7,5},{8,10},{9,11},{10,... | collective-permute-start | bytes 86024 | tf_op jit(solution)/shard_map/ppermute | solution.py:409
